TPU v7x, 32 devices: a whole 2x2x4 slice. The times are simulated.
32 devices in a mesh: shot: 4 (over x, core), band: 4 (over z), net: 2 (over y).
Axes of the slice: x: 2, y: 2, z: 4, core: 2. Of those that a mesh axis runs over, the one named last changes fastest.
Arguments:
- velocity: float32 [128, 1024], P('band'), may hold values from 1.5 to 4
- wave_now: float32 [16, 128, 1024], P(('shot', 'net'), 'band'), may hold values from -6 to 6
- wave_before: float32 [16, 128, 1024], P(('shot', 'net'), 'band'), may hold values from -6 to 6
- adjoint_last: float32 [16, 128, 1024], P(('shot', 'net'), 'band'), may hold values from -6 to 6
- adjoint_after: float32 [16, 128, 1024], P(('shot', 'net'), 'band'), may hold values from -6 to 6
- wavelet: float32 [16, 16], P(('shot', 'net')), may hold values from -72 to 72
- source_col: int32 [16], P(('shot', 'net')), may hold values from 0 to 1023
- rec_first: int32 [16], P(('shot', 'net')), may hold values from 0 to 1022
- rec_last: int32 [16], P(('shot', 'net')), may hold values from 1 to 1023
- rec_count: int32 [16], P(('shot', 'net')), may hold values from 2 to 128, as said below
- observed: float32 [16, 16, 128], P(('shot', 'net')), may hold values from -72 to 72
- conv_in: float32 [32, 18], replicated, may hold values from -1.5 to 1.5
- conv_mid: float32 [32, 288], replicated, may hold values from -0.375 to 0.375
- conv_out: float32 [1, 288], replicated, may hold values from -0.375 to 0.375
- cotangent: float32 [128, 1024], P('band', ('shot', 'net')), may hold values from -0.06629126 to 0.06629126
Outputs:
- new_velocity: float32 [128, 1024], P('band', ('shot', 'net'))
- grad_in: float32 [32, 18], replicated
- grad_mid: float32 [32, 288], replicated
- grad_out: float32 [1, 288], replicated
Inputs may be any that keep to these rules, and one draw needn't show every extreme that they name: rec_last - rec_first >= rec_count - 1 for every shot; some shot has 128 receivers.
All inputs are finite; a program needn't handle non-finite values.
Results may differ from a plain program's by a relative error of at most 0.0003.
Values sent between devices are 32-bit elements; how exact they have to be, the bound alone decides.
A program may use at most 128 MiB of HBM per device.

v0:
```python
import functools

import jax
import jax.numpy as jnp
import numpy as np
from jax import lax
from jax.experimental import pallas as pl
from jax.experimental.pallas import tpu as pltpu
from jax.sharding import PartitionSpec as P

coefficients = (-205.0 / 72.0, 8.0 / 5.0, -1.0 / 5.0, 8.0 / 315.0, -1.0 / 560.0)
speed_factor = 0.11
source_depth = 2
receiver_depth = 3
highest = lax.Precision.HIGHEST


def extended_2(block, sides, width):
    for axis, dim in sides:
        count = lax.axis_size(axis)
        forward = [(i, i + 1) for i in range(count - 1)]
        backward = [(target, source) for source, target in forward]
        low = lax.ppermute(
            lax.slice_in_dim(block, block.shape[dim] - width, None, axis=dim), axis, forward
        )
        high = lax.ppermute(lax.slice_in_dim(block, 0, width, axis=dim), axis, backward)
        block = jnp.concatenate([low, block, high], axis=dim)
    return block


def laplace(extended):
    middle = extended[..., 4:-4, :]
    height = middle.shape[-2]
    breadth = middle.shape[-1]
    padding = [(0, 0)] * (middle.ndim - 1) + [(4, 4)]
    padded = jnp.pad(middle, padding)
    running = 2.0 * coefficients[0] * middle
    for reach in range(1, 5):
        vertical = (
            extended[..., 4 - reach : 4 - reach + height, :]
            + extended[..., 4 + reach : 4 + reach + height, :]
        )
        lateral = (
            padded[..., 4 - reach : 4 - reach + breadth]
            + padded[..., 4 + reach : 4 + reach + breadth]
        )
        running = running + coefficients[reach] * (vertical + lateral)
    return running


def receiver_table(rec_first, rec_last, rec_count, breadth, slots):
    columns = jnp.arange(breadth, dtype=jnp.int32)
    slot_ids = jnp.arange(slots, dtype=jnp.int32)
    placed = (
        rec_first[:, None]
        + slot_ids[None, :] * (rec_last - rec_first)[:, None] // (rec_count - 1)[:, None]
    )
    active = slot_ids[None, :] < rec_count[:, None]
    return ((columns[None, :, None] == placed[:, None, :]) & active[:, None, :]).astype(jnp.float32)


def flipped(weights):
    outputs = weights.shape[0]
    channels = weights.shape[1] // 9
    return (
        weights.reshape(outputs, 9, channels)[:, ::-1, :]
        .transpose(2, 1, 0)
        .reshape(channels, 9 * outputs)
    )


MESH = pl.DeviceIdType.MESH
group_axes = ("shot", "net")
chunk = 512


def vmem(count):
    return [pl.BlockSpec(memory_space=pltpu.VMEM)] * count


def remote(source, target, send, receive, device):
    return pltpu.make_async_remote_copy(
        src_ref=source,
        dst_ref=target,
        send_sem=send,
        recv_sem=receive,
        device_id=device,
        device_id_type=MESH,
    )


def gather_kernel(
    groups, nets, bands, image, velocity, cotangent,
    out_image, out_cot, out_low, out_high,
    padded, slots, total, halo, speed_halo,
    send, receive, side_send, side_receive, row_send, row_receive,
):
    rows, breadth = image.shape
    piece = cotangent.shape[1]
    shot = lax.axis_index("shot")
    net = lax.axis_index("net")
    band = lax.axis_index("band")
    me = shot * nets + net

    def member(index):
        return {"shot": index // nets, "net": lax.rem(index, nets)}

    total[1] = jnp.zeros((rows, 3 * piece), jnp.float32)
    halo[...] = jnp.zeros(halo.shape, jnp.float32)
    speed_halo[...] = jnp.zeros(speed_halo.shape, jnp.float32)
    barrier = pltpu.get_barrier_semaphore()
    for step in range(1, groups):
        pl.semaphore_signal(
            barrier, inc=1, device_id=member(lax.rem(me + step, groups)), device_id_type=MESH
        )

    @pl.when(band > 0)
    def _():
        pl.semaphore_signal(barrier, inc=1, device_id={"band": band - 1}, device_id_type=MESH)

    @pl.when(band < bands - 1)
    def _():
        pl.semaphore_signal(barrier, inc=1, device_id={"band": band + 1}, device_id_type=MESH)

    padded[:, :piece] = jnp.zeros((rows, piece), jnp.float32)
    padded[:, piece + breadth :] = jnp.zeros((rows, piece), jnp.float32)
    padded[:, piece : piece + breadth] = image[...]
    pl.semaphore_wait(
        barrier, groups - 1 + lax.min(band, 1) + lax.min(bands - 1 - band, 1)
    )

    def scatter(step):
        target = lax.rem(me + step, groups)
        start = pl.multiple_of(target * piece, 128)
        return remote(
            padded.at[:, pl.ds(start, 3 * piece)],
            slots.at[step],
            send.at[step],
            receive.at[step],
            member(target),
        )

    for step in range(1, groups):
        scatter(step).start()

    def to_right():
        return remote(
            cotangent, total.at[1, :, pl.ds(0, piece)], side_send.at[0], side_receive.at[0],
            member(me + 1),
        )

    def to_left():
        return remote(
            cotangent, total.at[1, :, pl.ds(2 * piece, piece)], side_send.at[1],
            side_receive.at[1], member(me - 1),
        )

    def speed_up():
        return remote(
            velocity.at[pl.ds(0, 8)], speed_halo.at[1], row_send.at[0], row_receive.at[0],
            {"band": band - 1},
        )

    def speed_down():
        return remote(
            velocity.at[pl.ds(rows - 8, 8)], speed_halo.at[0], row_send.at[1], row_receive.at[1],
            {"band": band + 1},
        )

    def field_up():
        return remote(
            total.at[:, pl.ds(0, 8)], halo.at[1], row_send.at[2], row_receive.at[2],
            {"band": band - 1},
        )

    def field_down():
        return remote(
            total.at[:, pl.ds(rows - 8, 8)], halo.at[0], row_send.at[3], row_receive.at[3],
            {"band": band + 1},
        )

    pl.when(me < groups - 1)(lambda: to_right().start())
    pl.when(me > 0)(lambda: to_left().start())
    pl.when(band > 0)(lambda: speed_up().start())
    pl.when(band < bands - 1)(lambda: speed_down().start())

    own = pl.multiple_of(me * piece, 128)
    slots[0] = padded[:, pl.ds(own, 3 * piece)]
    for step in range(1, groups):
        scatter(step).wait_recv()
    summed = slots[0]
    for step in range(1, groups):
        summed = summed + slots[step]
    total[0] = summed
    pl.when(me > 0)(lambda: to_right().wait_recv())
    pl.when(me < groups - 1)(lambda: to_left().wait_recv())
    total[1, :, piece : 2 * piece] = cotangent[...]
    pl.when(band > 0)(lambda: field_up().start())
    pl.when(band < bands - 1)(lambda: field_down().start())
    for step in range(1, groups):
        scatter(step).wait_send()
    pl.when(me < groups - 1)(lambda: to_right().wait_send())
    pl.when(me > 0)(lambda: to_left().wait_send())
    pl.when(band > 0)(lambda: speed_up().wait_send())
    pl.when(band < bands - 1)(lambda: speed_down().wait_send())
    pl.when(band > 0)(lambda: speed_down().wait_recv())
    pl.when(band < bands - 1)(lambda: speed_up().wait_recv())
    pl.when(band > 0)(lambda: field_up().wait_send())
    pl.when(band < bands - 1)(lambda: field_down().wait_send())
    pl.when(band > 0)(lambda: field_down().wait_recv())
    pl.when(band < bands - 1)(lambda: field_up().wait_recv())
    for which, target in ((0, out_image), (1, out_cot)):
        target[0:8] = halo[0, which]
        target[8 : 8 + rows] = total[which]
        target[8 + rows :] = halo[1, which]
    out_low[...] = speed_halo[0]
    out_high[...] = speed_halo[1]


def gather_pieces(image, velocity, cotangent):
    rows, breadth = image.shape
    piece = cotangent.shape[1]
    groups = lax.axis_size(group_axes)
    nets = lax.axis_size("net")
    bands = lax.axis_size("band")
    f32 = jnp.float32
    dma = pltpu.SemaphoreType.DMA
    return pl.pallas_call(
        functools.partial(gather_kernel, groups, nets, bands),
        name="gather_pieces",
        out_shape=[jax.ShapeDtypeStruct((rows + 16, 3 * piece), f32)] * 2
        + [jax.ShapeDtypeStruct((8, breadth), f32)] * 2,
        in_specs=vmem(3),
        out_specs=vmem(4),
        scratch_shapes=[
            pltpu.VMEM((rows, breadth + 2 * piece), f32),
            pltpu.VMEM((groups, rows, 3 * piece), f32),
            pltpu.VMEM((2, rows, 3 * piece), f32),
            pltpu.VMEM((2, 2, 8, 3 * piece), f32),
            pltpu.VMEM((2, 8, breadth), f32),
            dma((groups,)),
            dma((groups,)),
            dma((2,)),
            dma((2,)),
            dma((4,)),
            dma((4,)),
        ],
        compiler_params=pltpu.CompilerParams(collective_id=1, has_side_effects=True),
    )(image, velocity, cotangent)


def total_kernel(sizes, grads, out, shot_slots, net_slots, band_slots, ready, send, receive):
    part = grads.shape[0] // sizes["shot"]
    barrier = pltpu.get_barrier_semaphore()
    count = 0
    for axis, size in sizes.items():
        me = lax.axis_index(axis)
        for step in range(1, size):
            pl.semaphore_signal(
                barrier, inc=1, device_id={axis: lax.rem(me + step, size)}, device_id_type=MESH
            )
            count += 1
    pl.semaphore_wait(barrier, count)
    base = 0

    def stage(axis, source, target_of, base):
        size = sizes[axis]
        me = lax.axis_index(axis)

        def copy(step, sender):
            peer = lax.rem(me + step, size)
            return remote(
                source(peer), target_of(sender), send.at[base + step], receive.at[base + sender],
                {axis: peer},
            )

        for step in range(1, size):
            copy(step, me).start()
        return copy, size, me

    def finish(handle):
        copy, size, me = handle
        for step in range(1, size):
            copy(step, lax.rem(me + step, size)).wait_recv()
        for step in range(1, size):
            copy(step, me).wait_send()

    shot = lax.axis_index("shot")
    handle = stage(
        "shot",
        lambda peer: grads.at[pl.ds(pl.multiple_of(peer * part, 8), part)],
        lambda sender: shot_slots.at[sender],
        0,
    )
    shot_slots[shot] = grads[pl.ds(pl.multiple_of(shot * part, 8), part)]
    finish(handle)

    def add(slots):
        running = slots[0]
        for index in range(1, slots.shape[0]):
            running = running + slots[index]
        return running

    base = sizes["shot"]
    ready[0] = add(shot_slots)
    handle = stage("net", lambda peer: ready.at[0], lambda sender: net_slots.at[sender], base)
    net_slots[lax.axis_index("net")] = ready[0]
    finish(handle)
    base += sizes["net"]
    ready[1] = add(net_slots)
    handle = stage("band", lambda peer: ready.at[1], lambda sender: band_slots.at[sender], base)
    band_slots[lax.axis_index("band")] = ready[1]
    finish(handle)
    base += sizes["band"]
    ready[2] = add(band_slots)
    handle = stage(
        "shot",
        lambda peer: ready.at[2],
        lambda sender: out.at[pl.ds(pl.multiple_of(sender * part, 8), part)],
        base,
    )
    out[pl.ds(pl.multiple_of(shot * part, 8), part)] = ready[2]
    finish(handle)


def total_grads(grads):
    sizes = {axis: lax.axis_size(axis) for axis in ("shot", "net", "band")}
    part = (grads.shape[0] // sizes["shot"], grads.shape[1])
    f32 = jnp.float32
    count = 2 * sizes["shot"] + sizes["net"] + sizes["band"]
    return pl.pallas_call(
        functools.partial(total_kernel, sizes),
        name="total_grads",
        out_shape=jax.ShapeDtypeStruct(grads.shape, f32),
        in_specs=vmem(1),
        out_specs=vmem(1)[0],
        scratch_shapes=[
            pltpu.VMEM((sizes["shot"],) + part, f32),
            pltpu.VMEM((sizes["net"],) + part, f32),
            pltpu.VMEM((sizes["band"],) + part, f32),
            pltpu.VMEM((3,) + part, f32),
            pltpu.SemaphoreType.DMA((count,)),
            pltpu.SemaphoreType.DMA((count,)),
        ],
        compiler_params=pltpu.CompilerParams(collective_id=2, has_side_effects=True),
    )(grads)


def halves(values):
    high = values.astype(jnp.bfloat16)
    return high, (values - high.astype(jnp.float32)).astype(jnp.bfloat16)


def dot3(left, right_high, right_low, dims):
    high, low = halves(left)
    height = left.shape[0]
    both = lax.dot_general(
        jnp.concatenate([high, low], 0), right_high, (dims, ((), ())),
        preferred_element_type=jnp.float32,
    )
    rest = lax.dot_general(
        high, right_low, (dims, ((), ())), preferred_element_type=jnp.float32
    )
    return both[:height] + both[height:] + rest


def network_kernel(
    width, first, middle, middle_back, last, layers,
    new_velocity, grads,
    patch_zero, patch_high, patch_low, before_one, hidden, slope_two, last_taps,
):
    length = layers.shape[1]
    channels = middle.shape[0]
    shifts = [down * width + across for down in (-1, 0, 1) for across in (-1, 0, 1)]
    pieces = length // chunk
    flat = ((1,), (0,))
    over = ((1,), (1,))

    for tap, shift in enumerate(shifts):
        patch_zero[tap * 8 : tap * 8 + 8] = pltpu.roll(layers[...], (-shift) % length, 1)

    def spread(source):
        for group in range(channels // 16):
            rows = source[group * 16 : group * 16 + 16]
            for tap, shift in enumerate(shifts):
                high, low = halves(pltpu.roll(rows, (-shift) % length, 1))
                start = tap * channels + group * 16
                patch_high[start : start + 16] = high
                patch_low[start : start + 16] = low

    def each(body, init=0):
        def step(index, carry):
            return body(pl.ds(pl.multiple_of(index * chunk, chunk), chunk), carry)

        return lax.fori_loop(0, pieces, step, init)

    def slope(values):
        squashed = 1.0 / (1.0 + jnp.exp(-values))
        return squashed * (1.0 + values * (1.0 - squashed))

    def silu(values):
        return values / (1.0 + jnp.exp(-values))

    def open_layer(at, carry):
        high, low = halves(patch_zero[:, at])
        both = dot3(first[...], high, low, flat)
        inside = layers[4:5, at] > 0.5
        before = both[:channels]
        before_one[:, at] = before
        hidden[:, at] = jnp.where(inside, silu(before), 0.0)
        slope_two[:, at] = both[channels:]
        return carry

    each(open_layer)
    spread(hidden)

    def middle_layer(at, carry):
        high = patch_high[:, at]
        low = patch_low[:, at]
        before = dot3(middle[...], high, low, flat)
        inside = layers[4:5, at] > 0.5
        owned = layers[5:6, at] > 0.5
        after = jnp.where(inside, silu(before), 0.0)
        hidden[:, at] = after
        fall = jnp.where(inside, slope_two[:, at] * slope(before), 0.0)
        slope_two[:, at] = fall
        after_high, after_low = halves(after)
        last_taps[:, at] = dot3(last[...], after_high, after_low, flat)
        return carry + dot3(jnp.where(owned, fall, 0.0), high, low, over)

    grad_middle = each(middle_layer, jnp.zeros((channels, 9 * channels), jnp.float32))
    spread(slope_two)
    update = layers[0:1]
    for tap, shift in enumerate(shifts):
        update = update + pltpu.roll(last_taps[...], (-shift) % length, 1)[tap : tap + 1]
    new_velocity[...] = update

    def first_grads(at, carry):
        back = dot3(middle_back[...], patch_high[:, at], patch_low[:, at], flat)
        owned = layers[5:6, at] > 0.5
        fall = jnp.where(owned, back * slope(before_one[:, at]), 0.0)
        high, low = halves(patch_zero[:, at])
        return carry + dot3(jnp.concatenate([fall, hidden[:, at]], 0), high, low, over)

    outer = each(first_grads, jnp.zeros((2 * channels, 72), jnp.float32))
    grads[...] = jnp.zeros(grads.shape, jnp.float32)
    grads[:, 0 : 9 * channels] = grad_middle
    start = -(-9 * channels // 128) * 128
    grads[:, start : start + 72] = outer[:channels]
    grads[:, start + 128 : start + 200] = outer[channels:]


def network(layers, width, conv_in, conv_mid, conv_out):
    length = layers.shape[1]
    channels = conv_mid.shape[0]
    f32 = jnp.float32
    taken = conv_in.reshape(channels, 9, 2)
    first = jnp.concatenate(
        [
            jnp.pad(taken, ((0, 0), (0, 0), (0, 6))).reshape(channels, 72),
            jnp.pad(flipped(conv_out)[:, :, None], ((0, 0), (0, 0), (2, 5))).reshape(channels, 72),
        ],
        0,
    )
    last = jnp.pad(conv_out.reshape(9, channels), ((0, 7), (0, 0)))
    start = -(-9 * channels // 128) * 128
    return pl.pallas_call(
        functools.partial(network_kernel, width),
        name="network",
        out_shape=[
            jax.ShapeDtypeStruct((1, length), f32),
            jax.ShapeDtypeStruct((channels, start + 256), f32),
        ],
        in_specs=vmem(5),
        out_specs=vmem(2),
        scratch_shapes=[
            pltpu.VMEM((72, length), f32),
            pltpu.VMEM((9 * channels, length), jnp.bfloat16),
            pltpu.VMEM((9 * channels, length), jnp.bfloat16),
            pltpu.VMEM((channels, length), f32),
            pltpu.VMEM((channels, length), f32),
            pltpu.VMEM((channels, length), f32),
            pltpu.VMEM((16, length), f32),
        ],
        compiler_params=pltpu.CompilerParams(vmem_limit_bytes=48 * 1024 * 1024),
    )(first, conv_mid, flipped(conv_mid), last, layers)


def update_model(imaging, velocity, cotangent, num_steps, shot_count, conv_in, conv_mid, conv_out):
    rows, breadth = velocity.shape
    piece = cotangent.shape[1]
    channels = conv_mid.shape[0]
    bands = lax.axis_size("band")
    groups = lax.axis_size(group_axes)
    image, cot, low, high = gather_pieces(imaging, velocity, cotangent)
    scaled = image[5:-5, piece - 3 : 2 * piece + 3] / float(num_steps * shot_count) ** 0.5
    cot = cot[5:-5, piece - 3 : 2 * piece + 3]
    tall = jnp.concatenate([low[5:], velocity, high[:3]], 0)
    start_col = lax.axis_index(group_axes) * piece
    around = lax.dynamic_slice_in_dim(
        jnp.pad(tall, ((0, 0), (piece, piece))), start_col, 3 * piece, 1
    )[:, piece - 3 : 2 * piece + 3]
    height, width = around.shape
    row_ids = lax.axis_index("band") * rows - 3 + jnp.arange(height)
    col_ids = start_col - 3 + jnp.arange(width)
    inside = ((row_ids >= 0) & (row_ids < rows * bands))[:, None] & (
        (col_ids >= 0) & (col_ids < piece * groups)
    )[None, :]
    owned = np.zeros((height, width), np.float32)
    owned[3:-3, 3:-3] = 1.0
    blank = jnp.zeros((height, width), jnp.float32)
    layers = jnp.stack(
        [around, scaled, cot, cot * owned, inside.astype(jnp.float32), jnp.asarray(owned), blank, blank]
    ).reshape(8, height * width)
    length = -(-height * width // chunk) * chunk
    layers = jnp.pad(layers, ((0, 0), (0, length - height * width)))
    fresh, grads = network(layers, width, conv_in, conv_mid, conv_out)
    new_velocity = fresh[0, : height * width].reshape(height, width)[3:-3, 3:-3]
    grads = total_grads(grads)
    start = -(-9 * channels // 128) * 128
    grad_in = grads[:, start : start + 72].reshape(channels, 9, 8)[:, :, :2].reshape(channels, 18)
    spare = grads[:, start + 128 : start + 200].reshape(channels, 9, 8)[:, ::-1, 3]
    return new_velocity, grad_in, grads[:, : 9 * channels], spare.T.reshape(1, 9 * channels)


def on_device(
    velocity,
    wave_now,
    wave_before,
    adjoint_last,
    adjoint_after,
    wavelet,
    source_col,
    rec_first,
    rec_last,
    rec_count,
    observed,
    conv_in,
    conv_mid,
    conv_out,
    cotangent,
):
    rows_here = velocity.shape[0]
    breadth = velocity.shape[1]
    shot_here = wave_now.shape[0]
    num_steps = wavelet.shape[1]
    slots = observed.shape[2]
    piece_cols = cotangent.shape[1]
    first_row = lax.axis_index("band") * rows_here
    speed_sq = (velocity * speed_factor) ** 2
    columns = jnp.arange(breadth, dtype=jnp.int32)
    source_cols = (columns[None, :] == source_col[:, None]).astype(jnp.float32)[:, None, :]
    table = receiver_table(rec_first, rec_last, rec_count, breadth, slots)
    active = (jnp.arange(slots, dtype=jnp.int32)[None, :] < rec_count[:, None]).astype(jnp.float32)

    def source_term(row_start, height, amount):
        row_ids = row_start + jnp.arange(height, dtype=jnp.int32)
        marked = (row_ids == source_depth).astype(jnp.float32)[None, :, None]
        return marked * source_cols * amount[:, None, None]

    def receiver_term(row_start, height, residual):
        row_ids = row_start + jnp.arange(height, dtype=jnp.int32)
        marked = (row_ids == receiver_depth).astype(jnp.float32)[None, :, None]
        injected = jnp.einsum("swk,sk->sw", table, residual, precision=highest)
        return marked * injected[:, None, :]

    speed_wide = extended_2(speed_sq, (("band", 0),), 16)

    def propagate(start, prior, drive, inject):
        grouped = drive.reshape((num_steps // 4, 4) + drive.shape[1:])

        def block(carry, amounts):
            stacked = extended_2(jnp.stack([carry[0], carry[1]]), (("band", 2),), 16)
            current = stacked[0]
            earlier = stacked[1]
            margin = 16
            saved = []
            for offset in range(4):
                inner = margin - 4
                speed_part = speed_wide[16 - inner : 16 + rows_here + inner]
                fresh = (
                    2.0 * current[:, 4:-4]
                    - earlier[:, 4:-4]
                    + speed_part * laplace(current)
                    + inject(first_row - inner, rows_here + 2 * inner, amounts[offset])
                )
                earlier = current[:, 4:-4]
                current = fresh
                margin = inner
                saved.append(fresh[:, inner : inner + rows_here])
            return ((current, earlier), jnp.stack(saved))

        ignored, states = lax.scan(block, (start, prior), grouped)
        return states.reshape((num_steps,) + start.shape)

    stored = propagate(wave_now, wave_before, wavelet.T, source_term)
    samples = jnp.einsum("tsw,swk->tsk", stored[:, :, receiver_depth, :], table, precision=highest)
    misfit = (samples - jnp.transpose(observed, (1, 0, 2))) * active[None]
    adjoint = propagate(adjoint_last, adjoint_after, misfit[::-1], receiver_term)
    imaging = jnp.sum(stored * adjoint[::-1], axis=(0, 1))
    group_count = shot_here * lax.axis_size(("shot", "net"))
    return update_model(
        imaging, velocity, cotangent, num_steps, group_count, conv_in, conv_mid, conv_out
    )


def solution(mesh):
    in_specs = (
        P("band", None),
        P(("shot", "net"), "band", None),
        P(("shot", "net"), "band", None),
        P(("shot", "net"), "band", None),
        P(("shot", "net"), "band", None),
        P(("shot", "net"), None),
        P(("shot", "net")),
        P(("shot", "net")),
        P(("shot", "net")),
        P(("shot", "net")),
        P(("shot", "net"), None, None),
        P(),
        P(),
        P(),
        P("band", ("shot", "net")),
    )
    out_specs = (P("band", ("shot", "net")), P(), P(), P())
    return jax.shard_map(
        on_device, mesh=mesh, in_specs=in_specs, out_specs=out_specs, check_vma=False
    )
```

profile of v0, /device:TPU:0, one launch (start us, length us, event | category | flops | bytes accessed | tf_op | source)
XLA Modules:
  0.0 225.1 jit_solution(3251882293626447012)
XLA Ops:
  1.7 5.0 %collective-permute-start.4 = (f32[16,1024]{1,0:T(8,128)S(1)}, f32[16,1024]{1,0:T(8,128)S(1)}, u32[]{:S(2)}, u32[]{:S(2)}) collective-permute-start(f32[16,1024]{1,0:T(8,128)S(1)} %get-tuple-element.455), channel_id=1, source_target_pairs={{0,2},{2,4},{4,6},{1,3},{3,5},{5,7},{8,10},{10,12},{12,14},{9,11},... | collective-permute-start | bytes 196616 | tf_op jit(solution)/shard_map/ppermute | solution.py:23
  6.6 1.3 collective-permute-start.5
  15.1 2.5 %broadcast.587.clone = f32[4,4,2,32,1024]{4,3,2,1,0:T(8,128)} broadcast(f32[]{:T(128)} %constant.216.clone.1), dimensions={} | broadcast | bytes 4194308 | tf_op jit(solution)/shard_map/broadcast.114
  17.6 62.0 %while.34 = (s32[]{:T(128)}, f32[2,32,1024]{2,1,0:T(8,128)S(1)}, f32[2,32,1024]{2,1,0:T(8,128)S(1)}, f32[4,4,2,32,1024]{4,3,2,1,0:T(8,128)}, f32[64,1024]{1,0:T(...) while((s32[]{:T(128)}, f32[2,32,1024]{2,1,0:T(8,128)S(1)}, ...), condition=%wide.region_1.2_spmd.clone, body=%wide.region_0.1_spmd.clone.sunk | while | flops 11801106 | bytes 31434516 | solution.py:593
  17.7 1.3 collective-permute-start
  19.0 5.2 %collective-permute-start.1 = (f32[2,2,16,1024]{3,2,1,0:T(8,128)S(1)}, f32[2,2,16,1024]{3,2,1,0:T(8,128)S(1)}, u32[]{:S(2)}, u32[]{:S(2)}) collective-permute-start(f32[2,2,16,1024]{3,2,1,0:T(8,128)S(1)} %get-tuple-element.622), channel_id=1, source_target_pairs={{0,2},{2,4},{4,6},{1,3},{3,5},{5,7},{8,10},{10,12},{12,14},{9,11},... | collective-permute-start | bytes 786440 | tf_op jit(solution)/shard_map/while/body/eval_jaxpr/ppermute | solution.py:23
  24.4 3.6 %collective-permute-done = f32[2,2,16,1024]{3,2,1,0:T(8,128)S(1)} collective-permute-done((f32[2,2,16,1024]{3,2,1,0:T(8,128)S(1)}, f32[2,2,16,1024]{3,2,1,0:T(8,128)S(1)}, u32[]{:S(2)}, u32[]{:S(2)}) %collective-permute-start) | collective-permute-done | bytes 262176 | tf_op jit(solution)/shard_map/while/body/eval_jaxpr/ppermute | solution.py:26
  28.0 1.2 collective-permute-done.1
  32.9 1.2 fusion.237
  34.1 1.3 collective-permute-start
  35.4 5.0 %collective-permute-start.1 = (f32[2,2,16,1024]{3,2,1,0:T(8,128)S(1)}, f32[2,2,16,1024]{3,2,1,0:T(8,128)S(1)}, u32[]{:S(2)}, u32[]{:S(2)}) collective-permute-start(f32[2,2,16,1024]{3,2,1,0:T(8,128)S(1)} %get-tuple-element.622), channel_id=1, source_target_pairs={{0,2},{2,4},{4,6},{1,3},{3,5},{5,7},{8,10},{10,12},{12,14},{9,11},... | collective-permute-start | bytes 786440 | tf_op jit(solution)/shard_map/while/body/eval_jaxpr/ppermute | solution.py:23
  40.7 2.7 %collective-permute-done = f32[2,2,16,1024]{3,2,1,0:T(8,128)S(1)} collective-permute-done((f32[2,2,16,1024]{3,2,1,0:T(8,128)S(1)}, f32[2,2,16,1024]{3,2,1,0:T(8,128)S(1)}, u32[]{:S(2)}, u32[]{:S(2)}) %collective-permute-start) | collective-permute-done | bytes 262176 | tf_op jit(solution)/shard_map/while/body/eval_jaxpr/ppermute | solution.py:26
  43.4 1.2 collective-permute-done.1
  48.3 1.1 fusion.237
  49.5 1.3 collective-permute-start
  50.8 5.0 %collective-permute-start.1 = (f32[2,2,16,1024]{3,2,1,0:T(8,128)S(1)}, f32[2,2,16,1024]{3,2,1,0:T(8,128)S(1)}, u32[]{:S(2)}, u32[]{:S(2)}) collective-permute-start(f32[2,2,16,1024]{3,2,1,0:T(8,128)S(1)} %get-tuple-element.622), channel_id=1, source_target_pairs={{0,2},{2,4},{4,6},{1,3},{3,5},{5,7},{8,10},{10,12},{12,14},{9,11},... | collective-permute-start | bytes 786440 | tf_op jit(solution)/shard_map/while/body/eval_jaxpr/ppermute | solution.py:23
  56.0 2.2 collective-permute-done
  58.2 1.5 collective-permute-done.1
  63.4 1.1 fusion.237
  64.5 1.3 collective-permute-start
  65.8 5.0 %collective-permute-start.1 = (f32[2,2,16,1024]{3,2,1,0:T(8,128)S(1)}, f32[2,2,16,1024]{3,2,1,0:T(8,128)S(1)}, u32[]{:S(2)}, u32[]{:S(2)}) collective-permute-start(f32[2,2,16,1024]{3,2,1,0:T(8,128)S(1)} %get-tuple-element.622), channel_id=1, source_target_pairs={{0,2},{2,4},{4,6},{1,3},{3,5},{5,7},{8,10},{10,12},{12,14},{9,11},... | collective-permute-start | bytes 786440 | tf_op jit(solution)/shard_map/while/body/eval_jaxpr/ppermute | solution.py:23
  71.1 2.2 collective-permute-done
  73.3 1.5 collective-permute-done.1
  78.5 1.1 fusion.237
  79.6 4.6 %copy.50 = f32[16,2,32,1024]{3,0,1,2:T(8,128)S(1)} copy(f32[16,2,32,1024]{3,2,1,0:T(8,128)} %bitcast.192) | data formatting | bytes 8388608 | tf_op jit(solution)/shard_map/reshape | solution.py:594
  84.8 2.5 %broadcast.587 = f32[4,4,2,32,1024]{4,3,2,1,0:T(8,128)} broadcast(f32[]{:T(128)} %constant.216.clone.1), dimensions={} | broadcast | bytes 4194308 | tf_op jit(solution)/shard_map/broadcast.114
  87.3 61.2 %while.35 = (s32[]{:T(128)}, f32[2,32,1024]{2,1,0:T(8,128)S(1)}, f32[2,32,1024]{2,1,0:T(8,128)S(1)}, f32[4,4,2,32,1024]{4,3,2,1,0:T(8,128)}, f32[64,1024]{1,0:T(...) while((s32[]{:T(128)}, f32[2,32,1024]{2,1,0:T(8,128)S(1)}, ...), condition=%wide.region_3.4_spmd.clone, body=%wide.region_2.3_spmd.clone.sunk | while | flops 27165204 | bytes 31534800 | solution.py:593
  87.3 1.3 collective-permute-start.2
  88.6 5.0 %collective-permute-start.3 = (f32[2,2,16,1024]{3,2,1,0:T(8,128)S(1)}, f32[2,2,16,1024]{3,2,1,0:T(8,128)S(1)}, u32[]{:S(2)}, u32[]{:S(2)}) collective-permute-start(f32[2,2,16,1024]{3,2,1,0:T(8,128)S(1)} %get-tuple-element.645), channel_id=1, source_target_pairs={{0,2},{2,4},{4,6},{1,3},{3,5},{5,7},{8,10},{10,12},{12,14},{9,11},... | collective-permute-start | bytes 786440 | tf_op jit(solution)/shard_map/while/body/eval_jaxpr/ppermute | solution.py:23
  94.7 1.1 fusion.249
  101.8 1.1 fusion.254
  103.0 1.3 collective-permute-start.2
  104.3 4.6 %collective-permute-start.3 = (f32[2,2,16,1024]{3,2,1,0:T(8,128)S(1)}, f32[2,2,16,1024]{3,2,1,0:T(8,128)S(1)}, u32[]{:S(2)}, u32[]{:S(2)}) collective-permute-start(f32[2,2,16,1024]{3,2,1,0:T(8,128)S(1)} %get-tuple-element.645), channel_id=1, source_target_pairs={{0,2},{2,4},{4,6},{1,3},{3,5},{5,7},{8,10},{10,12},{12,14},{9,11},... | collective-permute-start | bytes 786440 | tf_op jit(solution)/shard_map/while/body/eval_jaxpr/ppermute | solution.py:23
  117.0 1.1 fusion.254
  118.1 1.3 collective-permute-start.2
  119.4 4.6 %collective-permute-start.3 = (f32[2,2,16,1024]{3,2,1,0:T(8,128)S(1)}, f32[2,2,16,1024]{3,2,1,0:T(8,128)S(1)}, u32[]{:S(2)}, u32[]{:S(2)}) collective-permute-start(f32[2,2,16,1024]{3,2,1,0:T(8,128)S(1)} %get-tuple-element.645), channel_id=1, source_target_pairs={{0,2},{2,4},{4,6},{1,3},{3,5},{5,7},{8,10},{10,12},{12,14},{9,11},... | collective-permute-start | bytes 786440 | tf_op jit(solution)/shard_map/while/body/eval_jaxpr/ppermute | solution.py:23
  125.1 1.1 fusion.249
  132.2 1.1 fusion.254
  133.3 1.3 collective-permute-start.2
  134.6 4.6 %collective-permute-start.3 = (f32[2,2,16,1024]{3,2,1,0:T(8,128)S(1)}, f32[2,2,16,1024]{3,2,1,0:T(8,128)S(1)}, u32[]{:S(2)}, u32[]{:S(2)}) collective-permute-start(f32[2,2,16,1024]{3,2,1,0:T(8,128)S(1)} %get-tuple-element.645), channel_id=1, source_target_pairs={{0,2},{2,4},{4,6},{1,3},{3,5},{5,7},{8,10},{10,12},{12,14},{9,11},... | collective-permute-start | bytes 786440 | tf_op jit(solution)/shard_map/while/body/eval_jaxpr/ppermute | solution.py:23
  147.4 1.1 fusion.254
  148.5 6.6 %copy.51 = f32[16,2,32,1024]{3,0,1,2:T(8,128)} copy(f32[16,2,32,1024]{3,2,1,0:T(8,128)} %bitcast.194) | data formatting | bytes 8388608 | tf_op jit(solution)/shard_map/reshape | solution.py:594
  155.1 6.7 %rev.18 = f32[16,2,32,1024]{3,0,1,2:T(8,128)} reverse(f32[16,2,32,1024]{3,0,1,2:T(8,128)} %copy.51), dimensions={0} | reverse | bytes 8388608 | tf_op jit(solution)/shard_map/rev | solution.py:600
  161.8 7.1 %multiply_reduce_fusion.image = f32[32,1024]{1,0:T(8,128)} fusion(f32[16,2,32,1024]{3,0,1,2:T(8,128)} %rev.18, f32[16,2,32,1024]{3,2,1,0:T(8,128)} %bitcast.193), kind=kLoop, calls=%fused_computation.323 | loop fusion | flops 2064384 | bytes 8519680 | tf_op jit(solution)/shard_map/reduce_sum | solution.py:600
  168.9 14.5 %gather_pieces.1 = (f32[48,384]{1,0:T(8,128)}, f32[48,384]{1,0:T(8,128)}, f32[8,1024]{1,0:T(8,128)}, f32[8,1024]{1,0:T(8,128)}) custom-call(f32[32,1024]{1,0:T(8,128)} %multiply_reduce_fusion.image, f32[32,1024]{1,0:T(8,128)} %velocity.1, f32[32,128]{1,0:T(8,128)} %cotangent.1), custom_call_target="tpu_custom_call" | custom-call | tf_op jit(solution)/shard_map/gather_pieces/pallas_call | solution.py:228
  187.0 15.5 %network.1 = (f32[1,5120]{1,0:T(1,128)S(1)}, f32[32,640]{1,0:T(8,128)S(1)}) custom-call(f32[64,72]{1,0:T(8,128)S(1)} %pad_maximum_fusion.5.first, f32[32,288]{1,0:T(8,128)S(1)} %copy-done, f32[32,288]{1,0:T(8,128)S(1)} %copy.38.middle_back, f32[16,32]{1,0:T(8,128)S(1)} %pad.74.last, f32[8,5120]{1,0:T(8,128)S(1)} %pad.76.layers), custom_call_target="tpu_custom_call" | custom-call | tf_op jit(solution)/shard_map/network/pallas_call | solution.py:467
  203.2 17.4 %total_grads.1 = f32[32,640]{1,0:T(8,128)} custom-call(f32[32,640]{1,0:T(8,128)} %copy-done.1), custom_call_target="tpu_custom_call" | custom-call | tf_op jit(solution)/shard_map/total_grads/pallas_call | solution.py:331
  221.3 1.4 slice.1101
  (290 shorter events, 61.4 us)
Async XLA Ops:
  0.6 17.0 %copy-start.3 = (f32[2,32,1024]{2,1,0:T(8,128)S(1)}, f32[2,32,1024]{2,1,0:T(8,128)}, u32[]{:S(2)}) copy-start(f32[2,32,1024]{2,1,0:T(8,128)} %param.21) | copy-start | bytes 786436
  0.6 17.0 %copy-start.4 = (f32[2,32,1024]{2,1,0:T(8,128)S(1)}, f32[2,32,1024]{2,1,0:T(8,128)}, u32[]{:S(2)}) copy-start(f32[2,32,1024]{2,1,0:T(8,128)} %param.22) | copy-start | bytes 786436
  0.7 17.0 %copy-start.9 = (s32[2]{0:T(128)S(1)}, s32[2]{0:T(128)}, u32[]{:S(2)}) copy-start(s32[2]{0:T(128)} %param.26) | copy-start | bytes 28
  1.7 13.4 %collective-permute-start.4 = (f32[16,1024]{1,0:T(8,128)S(1)}, f32[16,1024]{1,0:T(8,128)S(1)}, u32[]{:S(2)}, u32[]{:S(2)}) collective-permute-start(f32[16,1024]{1,0:T(8,128)S(1)} %get-tuple-element.455), channel_id=1, source_target_pairs={{0,2},{2,4},{4,6},{1,3},{3,5},{5,7},{8,10},{10,12},{12,14},{9,11},... | collective-permute-start | bytes 196616 | tf_op jit(solution)/shard_map/ppermute | solution.py:23
  6.6 8.4 %collective-permute-start.5 = (f32[16,1024]{1,0:T(8,128)S(1)}, f32[16,1024]{1,0:T(8,128)S(1)}, u32[]{:S(2)}, u32[]{:S(2)}) collective-permute-start(f32[16,1024]{1,0:T(8,128)S(1)} %get-tuple-element.456), channel_id=1, source_target_pairs={{2,0},{4,2},{6,4},{3,1},{5,3},{7,5},{10,8},{12,10},{14,12},{11,9},... | collective-permute-start | bytes 196616 | tf_op jit(solution)/shard_map/ppermute | solution.py:26
  17.7 10.3 %collective-permute-start = (f32[2,2,16,1024]{3,2,1,0:T(8,128)S(1)}, f32[2,2,16,1024]{3,2,1,0:T(8,128)S(1)}, u32[]{:S(2)}, u32[]{:S(2)}) collective-permute-start(f32[2,2,16,1024]{3,2,1,0:T(8,128)S(1)} %get-tuple-element.621), channel_id=1, source_target_pairs={{2,0},{4,2},{6,4},{3,1},{5,3},{7,5},{10,8},{12,10},{14,12},{11,9},... | collective-permute-start | bytes 786440 | tf_op jit(solution)/shard_map/while/body/eval_jaxpr/ppermute | solution.py:26
  19.0 10.2 %collective-permute-start.1 = (f32[2,2,16,1024]{3,2,1,0:T(8,128)S(1)}, f32[2,2,16,1024]{3,2,1,0:T(8,128)S(1)}, u32[]{:S(2)}, u32[]{:S(2)}) collective-permute-start(f32[2,2,16,1024]{3,2,1,0:T(8,128)S(1)} %get-tuple-element.622), channel_id=1, source_target_pairs={{0,2},{2,4},{4,6},{1,3},{3,5},{5,7},{8,10},{10,12},{12,14},{9,11},... | collective-permute-start | bytes 786440 | tf_op jit(solution)/shard_map/while/body/eval_jaxpr/ppermute | solution.py:23
  34.1 9.3 %collective-permute-start = (f32[2,2,16,1024]{3,2,1,0:T(8,128)S(1)}, f32[2,2,16,1024]{3,2,1,0:T(8,128)S(1)}, u32[]{:S(2)}, u32[]{:S(2)}) collective-permute-start(f32[2,2,16,1024]{3,2,1,0:T(8,128)S(1)} %get-tuple-element.621), channel_id=1, source_target_pairs={{2,0},{4,2},{6,4},{3,1},{5,3},{7,5},{10,8},{12,10},{14,12},{11,9},... | collective-permute-start | bytes 786440 | tf_op jit(solution)/shard_map/while/body/eval_jaxpr/ppermute | solution.py:26
  35.4 9.1 %collective-permute-start.1 = (f32[2,2,16,1024]{3,2,1,0:T(8,128)S(1)}, f32[2,2,16,1024]{3,2,1,0:T(8,128)S(1)}, u32[]{:S(2)}, u32[]{:S(2)}) collective-permute-start(f32[2,2,16,1024]{3,2,1,0:T(8,128)S(1)} %get-tuple-element.622), channel_id=1, source_target_pairs={{0,2},{2,4},{4,6},{1,3},{3,5},{5,7},{8,10},{10,12},{12,14},{9,11},... | collective-permute-start | bytes 786440 | tf_op jit(solution)/shard_map/while/body/eval_jaxpr/ppermute | solution.py:23
  49.5 8.7 %collective-permute-start = (f32[2,2,16,1024]{3,2,1,0:T(8,128)S(1)}, f32[2,2,16,1024]{3,2,1,0:T(8,128)S(1)}, u32[]{:S(2)}, u32[]{:S(2)}) collective-permute-start(f32[2,2,16,1024]{3,2,1,0:T(8,128)S(1)} %get-tuple-element.621), channel_id=1, source_target_pairs={{2,0},{4,2},{6,4},{3,1},{5,3},{7,5},{10,8},{12,10},{14,12},{11,9},... | collective-permute-start | bytes 786440 | tf_op jit(solution)/shard_map/while/body/eval_jaxpr/ppermute | solution.py:26
  50.8 8.9 %collective-permute-start.1 = (f32[2,2,16,1024]{3,2,1,0:T(8,128)S(1)}, f32[2,2,16,1024]{3,2,1,0:T(8,128)S(1)}, u32[]{:S(2)}, u32[]{:S(2)}) collective-permute-start(f32[2,2,16,1024]{3,2,1,0:T(8,128)S(1)} %get-tuple-element.622), channel_id=1, source_target_pairs={{0,2},{2,4},{4,6},{1,3},{3,5},{5,7},{8,10},{10,12},{12,14},{9,11},... | collective-permute-start | bytes 786440 | tf_op jit(solution)/shard_map/while/body/eval_jaxpr/ppermute | solution.py:23
  64.5 8.7 %collective-permute-start = (f32[2,2,16,1024]{3,2,1,0:T(8,128)S(1)}, f32[2,2,16,1024]{3,2,1,0:T(8,128)S(1)}, u32[]{:S(2)}, u32[]{:S(2)}) collective-permute-start(f32[2,2,16,1024]{3,2,1,0:T(8,128)S(1)} %get-tuple-element.621), channel_id=1, source_target_pairs={{2,0},{4,2},{6,4},{3,1},{5,3},{7,5},{10,8},{12,10},{14,12},{11,9},... | collective-permute-start | bytes 786440 | tf_op jit(solution)/shard_map/while/body/eval_jaxpr/ppermute | solution.py:26
  65.8 8.9 %collective-permute-start.1 = (f32[2,2,16,1024]{3,2,1,0:T(8,128)S(1)}, f32[2,2,16,1024]{3,2,1,0:T(8,128)S(1)}, u32[]{:S(2)}, u32[]{:S(2)}) collective-permute-start(f32[2,2,16,1024]{3,2,1,0:T(8,128)S(1)} %get-tuple-element.622), channel_id=1, source_target_pairs={{0,2},{2,4},{4,6},{1,3},{3,5},{5,7},{8,10},{10,12},{12,14},{9,11},... | collective-permute-start | bytes 786440 | tf_op jit(solution)/shard_map/while/body/eval_jaxpr/ppermute | solution.py:23
  79.6 4.7 %copy-start.10 = (f32[2,16,128]{2,1,0:T(8,128)S(1)}, f32[2,16,128]{2,1,0:T(8,128)}, u32[]{:S(2)}) copy-start(f32[2,16,128]{2,1,0:T(8,128)} %param.30) | copy-start | bytes 49156
  84.2 3.0 %copy-start.2 = (f32[2,32,1024]{2,1,0:T(8,128)S(1)}, f32[2,32,1024]{2,1,0:T(8,128)}, u32[]{:S(2)}) copy-start(f32[2,32,1024]{2,1,0:T(8,128)} %param.23) | copy-start | bytes 786436
  84.3 3.0 %copy-start.5 = (f32[2,32,1024]{2,1,0:T(8,128)S(1)}, f32[2,32,1024]{2,1,0:T(8,128)}, u32[]{:S(2)}) copy-start(f32[2,32,1024]{2,1,0:T(8,128)} %param.24) | copy-start | bytes 786436
  87.3 10.7 %collective-permute-start.2 = (f32[2,2,16,1024]{3,2,1,0:T(8,128)S(1)}, f32[2,2,16,1024]{3,2,1,0:T(8,128)S(1)}, u32[]{:S(2)}, u32[]{:S(2)}) collective-permute-start(f32[2,2,16,1024]{3,2,1,0:T(8,128)S(1)} %get-tuple-element.644), channel_id=1, source_target_pairs={{2,0},{4,2},{6,4},{3,1},{5,3},{7,5},{10,8},{12,10},{14,12},{11,9},... | collective-permute-start | bytes 786440 | tf_op jit(solution)/shard_map/while/body/eval_jaxpr/ppermute | solution.py:26
  88.6 9.5 %collective-permute-start.3 = (f32[2,2,16,1024]{3,2,1,0:T(8,128)S(1)}, f32[2,2,16,1024]{3,2,1,0:T(8,128)S(1)}, u32[]{:S(2)}, u32[]{:S(2)}) collective-permute-start(f32[2,2,16,1024]{3,2,1,0:T(8,128)S(1)} %get-tuple-element.645), channel_id=1, source_target_pairs={{0,2},{2,4},{4,6},{1,3},{3,5},{5,7},{8,10},{10,12},{12,14},{9,11},... | collective-permute-start | bytes 786440 | tf_op jit(solution)/shard_map/while/body/eval_jaxpr/ppermute | solution.py:23
  103.0 10.3 %collective-permute-start.2 = (f32[2,2,16,1024]{3,2,1,0:T(8,128)S(1)}, f32[2,2,16,1024]{3,2,1,0:T(8,128)S(1)}, u32[]{:S(2)}, u32[]{:S(2)}) collective-permute-start(f32[2,2,16,1024]{3,2,1,0:T(8,128)S(1)} %get-tuple-element.644), channel_id=1, source_target_pairs={{2,0},{4,2},{6,4},{3,1},{5,3},{7,5},{10,8},{12,10},{14,12},{11,9},... | collective-permute-start | bytes 786440 | tf_op jit(solution)/shard_map/while/body/eval_jaxpr/ppermute | solution.py:26
  104.3 9.0 %collective-permute-start.3 = (f32[2,2,16,1024]{3,2,1,0:T(8,128)S(1)}, f32[2,2,16,1024]{3,2,1,0:T(8,128)S(1)}, u32[]{:S(2)}, u32[]{:S(2)}) collective-permute-start(f32[2,2,16,1024]{3,2,1,0:T(8,128)S(1)} %get-tuple-element.645), channel_id=1, source_target_pairs={{0,2},{2,4},{4,6},{1,3},{3,5},{5,7},{8,10},{10,12},{12,14},{9,11},... | collective-permute-start | bytes 786440 | tf_op jit(solution)/shard_map/while/body/eval_jaxpr/ppermute | solution.py:23
  118.1 10.3 %collective-permute-start.2 = (f32[2,2,16,1024]{3,2,1,0:T(8,128)S(1)}, f32[2,2,16,1024]{3,2,1,0:T(8,128)S(1)}, u32[]{:S(2)}, u32[]{:S(2)}) collective-permute-start(f32[2,2,16,1024]{3,2,1,0:T(8,128)S(1)} %get-tuple-element.644), channel_id=1, source_target_pairs={{2,0},{4,2},{6,4},{3,1},{5,3},{7,5},{10,8},{12,10},{14,12},{11,9},... | collective-permute-start | bytes 786440 | tf_op jit(solution)/shard_map/while/body/eval_jaxpr/ppermute | solution.py:26
  119.4 9.0 %collective-permute-start.3 = (f32[2,2,16,1024]{3,2,1,0:T(8,128)S(1)}, f32[2,2,16,1024]{3,2,1,0:T(8,128)S(1)}, u32[]{:S(2)}, u32[]{:S(2)}) collective-permute-start(f32[2,2,16,1024]{3,2,1,0:T(8,128)S(1)} %get-tuple-element.645), channel_id=1, source_target_pairs={{0,2},{2,4},{4,6},{1,3},{3,5},{5,7},{8,10},{10,12},{12,14},{9,11},... | collective-permute-start | bytes 786440 | tf_op jit(solution)/shard_map/while/body/eval_jaxpr/ppermute | solution.py:23
  133.3 10.3 %collective-permute-start.2 = (f32[2,2,16,1024]{3,2,1,0:T(8,128)S(1)}, f32[2,2,16,1024]{3,2,1,0:T(8,128)S(1)}, u32[]{:S(2)}, u32[]{:S(2)}) collective-permute-start(f32[2,2,16,1024]{3,2,1,0:T(8,128)S(1)} %get-tuple-element.644), channel_id=1, source_target_pairs={{2,0},{4,2},{6,4},{3,1},{5,3},{7,5},{10,8},{12,10},{14,12},{11,9},... | collective-permute-start | bytes 786440 | tf_op jit(solution)/shard_map/while/body/eval_jaxpr/ppermute | solution.py:26
  134.6 9.0 %collective-permute-start.3 = (f32[2,2,16,1024]{3,2,1,0:T(8,128)S(1)}, f32[2,2,16,1024]{3,2,1,0:T(8,128)S(1)}, u32[]{:S(2)}, u32[]{:S(2)}) collective-permute-start(f32[2,2,16,1024]{3,2,1,0:T(8,128)S(1)} %get-tuple-element.645), channel_id=1, source_target_pairs={{0,2},{2,4},{4,6},{1,3},{3,5},{5,7},{8,10},{10,12},{12,14},{9,11},... | collective-permute-start | bytes 786440 | tf_op jit(solution)/shard_map/while/body/eval_jaxpr/ppermute | solution.py:23
  161.8 21.6 %copy-start.7 = (f32[38,134]{1,0:T(8,128)S(1)}, f32[38,134]{1,0:T(8,128)}, u32[]{:S(2)}) copy-start(f32[38,134]{1,0:T(8,128)} %constant.232.clone) | copy-start | bytes 61108
  161.8 24.7 %copy-start.6 = (f32[32,1024]{1,0:T(8,128)S(1)}, f32[32,1024]{1,0:T(8,128)}, u32[]{:S(2)}) copy-start(f32[32,1024]{1,0:T(8,128)} %velocity.1) | copy-start | bytes 393220
  161.8 25.0 %copy-start.8 = (f32[1,5092]{1,0:T(1,128)S(1)}, f32[1,5092]{1,0:T(1,128)}, u32[]{:S(2)}) copy-start(f32[1,5092]{1,0:T(1,128)} %constant.269) | copy-start | bytes 61108
  161.8 25.2 %copy-start = (f32[32,288]{1,0:T(8,128)S(1)}, f32[32,288]{1,0:T(8,128)}, u32[]{:S(2)}) copy-start(f32[32,288]{1,0:T(8,128)} %middle.1) | copy-start | bytes 110596
  202.6 0.6 copy-start.1
where the time goes:
time: 226 us; the launch traced here: 225 us
  starting transfers between devices  55.6 us (25%)
  other arithmetic  49.7 us (22%)
  Pallas kernels  47.4 us (21%)
  local copies, waits for them, and re-layouts  36.7 us (16%)
  matrix products  17.3 us (8%)
  waiting for transfers between devices  15.9 us (7%)
    ppermute x9, starting transfers between devices, extended_2(): lax.ppermute(lax.slice_in_dim(block, block.shape[dim] - width, None, axis...  44 us
    add x24, other arithmetic, block(): 2.0 * current[:, 4:-4] - earlier[:, 4:-4] + speed_part * laplace(current)  21.6 us
    pallas_call x1, Pallas kernels, total_grads(): pl.pallas_call(functools.partial(total_kernel, sizes), name='total_grads'...  17.4 us
    dot_general x16, matrix products, receiver_term(): injected = jnp.einsum('swk,sk->sw', table, residual, precision=highest)  16.8 us
    pallas_call x1, Pallas kernels, network(): pl.pallas_call(functools.partial(network_kernel, width), name='network',...  15.5 us
    pallas_call x1, Pallas kernels, gather_pieces(): pl.pallas_call(functools.partial(gather_kernel, groups, nets, bands), nam...  14.5 us
    ppermute x9, starting transfers between devices, extended_2(): lax.ppermute(lax.slice_in_dim(block, 0, width, axis=dim), axis, backward)  11.6 us
    reshape x2, local copies, waits for them, and re-layouts, propagate(): return states.reshape((num_steps,) + start.shape)  11.2 us
  transfers between devices with their start and end apart: 18, of which 8 were waited for; matrix products, arithmetic and copies ran while one was open for 11% of the time, Pallas kernels for 0%

commit v1 on v0

--- a/solution.py
+++ b/solution.py
@@ -486,20 +486,592 @@
     )(first, conv_mid, flipped(conv_mid), last, layers)
 
 
-def update_model(imaging, velocity, cotangent, num_steps, shot_count, conv_in, conv_mid, conv_out):
+def wave_kernel(
+    sizes,
+    velocity, wave_now, wave_before, adjoint_last, adjoint_after, wavelet, source_col, rec_first,
+    rec_last, rec_count, observed, cotangent,
+    out_image, out_cot, out_speed,
+    arrived, speed_all, speed_sq, small, observed_cols, source_mask, receiver_mask,
+    forward, adjoint, image, flat, parts, part_slots, cross, cross_slots, held, lines, line_slots,
+    strips, cot_all,
+    own_sem, speed_send, speed_recv, plane_send, plane_recv, field_send, field_recv, small_send,
+    small_recv, cot_send, cot_recv, part_send, part_recv, cross_send, cross_recv, line_send, line_recv,
+):
+    shots, nets, bands = sizes
+    mine_shots, rows, breadth = wave_now.shape
+    total_rows = rows * bands
+    steps = observed.shape[1]
+    slots = observed.shape[2]
+    piece = cotangent.shape[1]
+    sides = bands // mine_shots
+    per_side = shots // sides
+    pieces = per_side * nets
+    groups = shots * nets
+    half = breadth // sides
+    margin = 8 * steps
+    width = half + margin
+    depth = total_rows // 8
+    f32 = jnp.float32
+    shot = lax.axis_index("shot")
+    net = lax.axis_index("net")
+    band = lax.axis_index("band")
+    side = shot // per_side
+    lane_in_side = lax.rem(shot, per_side)
+    group = shot * nets + net
+    place = lane_in_side * nets + net
+    owner_side = lax.rem(band, sides)
+    owner_slot = band // sides
+    is_mine = owner_side == side
+    own_start = side * margin
+
+    cot_all[...] = jnp.zeros(cot_all.shape, f32)
+    barrier = pltpu.get_barrier_semaphore()
+    for step in range(1, groups):
+        peer = lax.rem(group + step, groups)
+        pl.semaphore_signal(
+            barrier, inc=1, device_id={"shot": peer // nets, "net": lax.rem(peer, nets)},
+            device_id_type=MESH,
+        )
+    for step in range(1, bands):
+        pl.semaphore_signal(
+            barrier, inc=1, device_id={"band": lax.rem(band + step, bands)}, device_id_type=MESH
+        )
+    for turn in range(1, sides):
+        other = lax.rem(side + turn, sides) * per_side + lane_in_side
+        for step in range(1, bands):
+            pl.semaphore_signal(
+                barrier, inc=1, device_id={"shot": other, "band": lax.rem(band + step, bands)},
+                device_id_type=MESH,
+            )
+
+    column = pl.multiple_of(group * piece, 128)
+
+    def window(which):
+        return pl.ds(pl.multiple_of(which * (half - margin), 128), width)
+
+    fields = (wave_now, wave_before, adjoint_last, adjoint_after)
+
+    def own_field(index):
+        return pltpu.make_async_copy(
+            fields[index].at[owner_slot, :, window(side)],
+            arrived.at[index, pl.ds(pl.multiple_of(band * rows, 8), rows)],
+            own_sem.at[index],
+        )
+
+    own_speed = pltpu.make_async_copy(
+        velocity.at[:, pl.ds(column, piece)],
+        speed_all.at[pl.ds(pl.multiple_of(8 + band * rows, 8), rows), pl.ds(piece + column, piece)],
+        own_sem.at[4],
+    )
+    own_speed.start()
+    for index in range(4):
+        pl.when(is_mine)(lambda index=index: own_field(index).start())
+
+    speed_all[:, 0:piece] = jnp.zeros((total_rows + 16, piece), f32)
+    speed_all[:, piece + breadth :] = jnp.zeros((total_rows + 16, piece), f32)
+    speed_all[0:8] = jnp.zeros((8, breadth + 2 * piece), f32)
+    speed_all[total_rows + 8 :] = jnp.zeros((8, breadth + 2 * piece), f32)
+    cot_all[8 : 8 + rows, piece : 2 * piece] = cotangent[...]
+
+    row_ids = lax.broadcasted_iota(jnp.int32, (8, 128), 0)
+    lane_ids = lax.broadcasted_iota(jnp.int32, (8, 128), 1)
+    table = jnp.zeros((8, 128), f32)
+    for step in range(steps):
+        table = jnp.where((row_ids == 0) & (lane_ids == step), wavelet[owner_slot, step], table)
+    for index, ref in enumerate((source_col, rec_first, rec_last, rec_count)):
+        table = jnp.where(row_ids == index + 1, ref[owner_slot].astype(f32), table)
+
+    @pl.when(is_mine)
+    def _():
+        small[0:8] = table
+        small[8 : 8 + steps] = observed[owner_slot]
+
+    peers = groups - 1 + bands - 1 + (sides - 1) * (bands - 1)
+    pl.semaphore_wait(barrier, peers)
+
+    def speed_line(step):
+        return remote(
+            velocity.at[:, pl.ds(column, piece)],
+            speed_all.at[pl.ds(pl.multiple_of(8 + band * rows, 8), rows), pl.ds(piece + column, piece)],
+            speed_send.at[step], speed_recv.at[bands - step],
+            {"band": lax.rem(band + step, bands)},
+        )
+
+    def speed_line_in(step):
+        source = lax.rem(band + step, bands)
+        return remote(
+            velocity.at[:, pl.ds(column, piece)],
+            speed_all.at[pl.ds(pl.multiple_of(8 + source * rows, 8), rows), pl.ds(piece + column, piece)],
+            speed_send.at[step], speed_recv.at[step], {"band": source},
+        )
+
+    def speed_plane(step):
+        peer = lax.rem(group + step, groups)
+        block = speed_all.at[pl.ds(8, total_rows), pl.ds(piece + column, piece)]
+        return remote(
+            block, block, plane_send.at[step], plane_recv.at[groups - step],
+            {"shot": peer // nets, "net": lax.rem(peer, nets)},
+        )
+
+    def speed_plane_in(step):
+        peer = lax.rem(group + step, groups)
+        block = speed_all.at[
+            pl.ds(8, total_rows), pl.ds(pl.multiple_of(piece + peer * piece, 128), piece)
+        ]
+        return remote(
+            block, block, plane_send.at[step], plane_recv.at[step],
+            {"shot": peer // nets, "net": lax.rem(peer, nets)},
+        )
+
+    def small_out(turn):
+        return remote(
+            small, small, small_send.at[turn], small_recv.at[0],
+            {"shot": lax.rem(side + turn, sides) * per_side + lane_in_side},
+        )
+
+    def cot_down():
+        return remote(
+            cotangent.at[pl.ds(rows - 8, 8)], cot_all.at[pl.ds(0, 8), pl.ds(piece, piece)],
+            cot_send.at[0], cot_recv.at[0], {"band": band + 1},
+        )
+
+    def cot_up():
+        return remote(
+            cotangent.at[pl.ds(0, 8)], cot_all.at[pl.ds(rows + 8, 8), pl.ds(piece, piece)],
+            cot_send.at[1], cot_recv.at[1], {"band": band - 1},
+        )
+
+    def member(index):
+        return {"shot": index // nets, "net": lax.rem(index, nets)}
+
+    def cot_right():
+        return remote(
+            cot_all.at[:, pl.ds(piece, piece)], cot_all.at[:, pl.ds(0, piece)],
+            cot_send.at[2], cot_recv.at[2], member(group + 1),
+        )
+
+    def cot_left():
+        return remote(
+            cot_all.at[:, pl.ds(piece, piece)], cot_all.at[:, pl.ds(2 * piece, piece)],
+            cot_send.at[3], cot_recv.at[3], member(group - 1),
+        )
+
+    def field_out(index, turn, which):
+        slot = lax.rem(band // sides + turn, mine_shots)
+        target = slot * sides + side
+        return target, remote(
+            fields[index].at[slot, :, window(which)],
+            arrived.at[index, pl.ds(pl.multiple_of(band * rows, 8), rows)],
+            field_send.at[index, turn * sides + which], field_recv.at[index, band],
+            {"shot": which * per_side + lane_in_side, "band": target},
+        )
+
+    def field_in(index, source):
+        return remote(
+            fields[index].at[0, :, pl.ds(0, width)],
+            arrived.at[index, pl.ds(source * rows, rows)],
+            field_send.at[index, 0], field_recv.at[index, source],
+            {"shot": owner_side * per_side + lane_in_side, "band": source},
+        )
+
+    def each_field_out(index, act):
+        for turn in range(1, mine_shots + 1):
+            for which in range(sides):
+                target, copy = field_out(index, turn % mine_shots, which)
+                pl.when(jnp.logical_not((target == band) & (side == which)))(
+                    lambda copy=copy: act(copy)
+                )
+
+    def each_field_in(index):
+        for source in range(bands):
+            pl.when(jnp.logical_not((band == source) & is_mine))(
+                lambda source=source: field_in(index, source).wait_recv()
+            )
+        pl.when(is_mine)(lambda: own_field(index).wait())
+
+    for step in range(1, bands):
+        speed_line(step).start()
+    pl.when(band < bands - 1)(lambda: cot_down().start())
+    pl.when(band > 0)(lambda: cot_up().start())
+    for turn in range(1, sides):
+        pl.when(is_mine)(lambda turn=turn: small_out(turn).start())
+    for index in (0, 1):
+        each_field_out(index, lambda copy: copy.start())
+
+    pl.when(jnp.logical_not(is_mine))(lambda: small_out(1).wait_recv())
+    own_speed.wait()
+    for step in range(1, bands):
+        speed_line_in(step).wait_recv()
+    for step in range(1, groups):
+        speed_plane(step).start()
+    pl.when(band > 0)(lambda: cot_down().wait_recv())
+    pl.when(band < bands - 1)(lambda: cot_up().wait_recv())
+    pl.when(group < groups - 1)(lambda: cot_right().start())
+    pl.when(group > 0)(lambda: cot_left().start())
+
+    cols = lax.broadcasted_iota(jnp.int32, (8, width), 1)
+    level = lax.broadcasted_iota(jnp.int32, (8, width), 0)
+    first_cell = jnp.where(side == 0, 0, 4)
+    last_cell = jnp.where(side == 0, width - 4, width)
+    inside = (cols >= first_cell) & (cols < last_cell)
+    keep = inside.astype(f32)
+    top = inside & (level == 0)
+    actual = (cols + side * (half - margin)).astype(f32)
+
+    def setting(index):
+        return jnp.broadcast_to(small[index : index + 1, 0:1], (8, width))
+
+    source_mask[...] = jnp.where(top & (actual == setting(1)), 1.0, 0.0)
+    first = small[2:3, 0:1]
+    span = small[3:4, 0:1] - first
+    count = small[4:5, 0:1]
+    slot_ids = lax.broadcasted_iota(jnp.int32, (slots, width), 0).astype(f32)
+    wide = (lax.broadcasted_iota(jnp.int32, (slots, width), 1) + side * (half - margin)).astype(f32)
+    low = (wide - first) * (count - 1.0)
+    reach = slot_ids * span
+    chosen = jnp.where(
+        (low <= reach) & (reach < low + (count - 1.0)) & (slot_ids < count), 1.0, 0.0
+    ).astype(jnp.bfloat16)
+    recorded = small[8 : 8 + steps]
+    high = recorded.astype(jnp.bfloat16)
+    rest = recorded - high.astype(f32)
+    middle = rest.astype(jnp.bfloat16)
+    lower = (rest - middle.astype(f32)).astype(jnp.bfloat16)
+    stacked = jnp.concatenate([high, middle, lower, jnp.ones((16, slots), jnp.bfloat16)], 0)
+    spread = lax.dot_general(
+        stacked, chosen, (((1,), (0,)), ((), ())), preferred_element_type=f32
+    )
+    observed_cols[...] = (spread[:steps] + spread[steps : 2 * steps]) + spread[2 * steps : 3 * steps]
+    receiver_mask[...] = jnp.where(top, spread[3 * steps : 3 * steps + 8], 0.0)
+
+    for step in range(1, groups):
+        speed_plane_in(step).wait_recv()
+    tiles = width // 128
+    for tile in range(tiles):
+        start = pl.multiple_of(piece + side * (half - margin) + tile * 128, 128)
+        flat[tile] = speed_all[pl.ds(8, total_rows), pl.ds(start, 128)]
+
+    def picked(line):
+        return jnp.concatenate(
+            [flat[tile, pl.ds(line, 8, stride=depth), :] for tile in range(tiles)], 1
+        )
+
+    for line in range(depth):
+        value = picked(line) * speed_factor
+        speed_sq[line] = value * value * keep
+
+    def refill(ref, at):
+        above = pltpu.roll(ref[at, depth : depth + 4], 1, 1)
+        below = pltpu.roll(ref[at, 4:8], 7, 1)
+        edge = lax.broadcasted_iota(jnp.int32, (4, 8, width), 1)
+        ref[at, 0:4] = jnp.where(edge == 0, 0.0, above)
+        ref[at, depth + 4 :] = jnp.where(edge == 7, 0.0, below)
+
+    def unpack(index, ref, at):
+        for tile in range(tiles):
+            flat[tile] = arrived[index, :, tile * 128 : tile * 128 + 128]
+        for line in range(depth):
+            ref[at, 4 + line] = picked(line) * keep
+
+    tall = 2
+
+    def advance(ref, now, before, line):
+        center = ref[now, pl.ds(4 + line, tall)]
+        running = (2.0 * coefficients[0]) * center
+        for reach in range(1, 5):
+            vertical = ref[now, pl.ds(4 + line - reach, tall)] + ref[now, pl.ds(4 + line + reach, tall)]
+            lateral = pltpu.roll(center, reach, 2) + pltpu.roll(center, width - reach, 2)
+            running = running + coefficients[reach] * (vertical + lateral)
+        return 2.0 * center - ref[before, pl.ds(4 + line, tall)] + speed_sq[pl.ds(line, tall)] * running
+
+    each_field_in(0)
+    unpack(0, forward, 1)
+    refill(forward, 1)
+    each_field_in(1)
+    unpack(1, forward, 0)
+    for index in (2, 3):
+        each_field_out(index, lambda copy: copy.start())
+
+    pulses = small[0:1]
+    pulse_ids = lax.broadcasted_iota(jnp.int32, (1, 128), 1)
+
+    def forward_step(index, carry):
+        for line in range(0, depth, tall):
+            forward[index + 2, pl.ds(4 + line, tall)] = advance(forward, index + 1, index, line)
+        amount = jnp.sum(jnp.where(pulse_ids == index, pulses, 0.0), axis=1, keepdims=True)
+        forward[index + 2, 4 + source_depth] = (
+            forward[index + 2, 4 + source_depth] + source_mask[...] * amount
+        )
+        refill(forward, index + 2)
+        return carry
+
+    lax.fori_loop(0, steps, forward_step, 0)
+
+    for index in (2, 3):
+        each_field_in(index)
+    unpack(2, adjoint, 0)
+    refill(adjoint, 0)
+    unpack(3, adjoint, 1)
+    image[...] = jnp.zeros(image.shape, f32)
+
+    def adjoint_step(index, carry):
+        moment = steps - 1 - index
+        now = lax.rem(index, 2)
+        later = 1 - now
+        held_now = forward.at[moment + 2]
+        injected = receiver_mask[...] * (
+            held_now[4 + receiver_depth] - observed_cols[pl.ds(moment, 1), :]
+        )
+        for line in range(0, depth, tall):
+            fresh = advance(adjoint, now, later, line)
+            if line <= receiver_depth < line + tall:
+                blank = jnp.zeros((1, 8, width), f32)
+                fresh = fresh + jnp.concatenate(
+                    [injected[None] if line + k == receiver_depth else blank for k in range(tall)], 0
+                )
+            adjoint[later, pl.ds(4 + line, tall)] = fresh
+            image[pl.ds(line, tall)] = (
+                image[pl.ds(line, tall)] + held_now[pl.ds(4 + line, tall)] * fresh
+            )
+        refill(adjoint, later)
+        return carry
+
+    lax.fori_loop(0, steps, adjoint_step, 0)
+
+    for line in range(depth):
+        value = image[line]
+        for tile in range(tiles):
+            flat[tile, pl.ds(line, 8, stride=depth), :] = value[:, tile * 128 : tile * 128 + 128]
+
+    parts[...] = jnp.zeros(parts.shape, f32)
+    for index in range(pieces):
+        block = flat[own_start // 128 + index]
+        parts[index, 0:total_rows] = block
+        turned = block.T
+        if index + 1 < pieces:
+            parts[index + 1, total_rows : total_rows + 8] = turned[piece - 8 :]
+        else:
+            cross[1] = turned[piece - 8 :]
+        if index > 0:
+            parts[index - 1, total_rows + 8 : total_rows + 16] = turned[0:8]
+        else:
+            cross[0] = turned[0:8]
+
+    def part_out(step):
+        peer = lax.rem(place + step, pieces)
+        return remote(
+            parts.at[peer], part_slots.at[pieces - step], part_send.at[step],
+            part_recv.at[pieces - step], member(side * pieces + peer),
+        )
+
+    def part_in(step):
+        peer = lax.rem(place + step, pieces)
+        return remote(
+            parts.at[peer], part_slots.at[step], part_send.at[step],
+            part_recv.at[step], member(side * pieces + peer),
+        )
+
+    def cross_out(toward):
+        target = (side + 1) * pieces if toward else side * pieces - 1
+        return remote(
+            cross.at[toward], cross_slots.at[1 - toward, place], cross_send.at[toward],
+            cross_recv.at[1 - toward, place], member(target),
+        )
+
+    def cross_in(came, source):
+        return remote(
+            cross.at[came], cross_slots.at[came, source], cross_send.at[came],
+            cross_recv.at[came, source], member(lax.rem(group + 1, groups)),
+        )
+
+    has_right = side < sides - 1
+    has_left = side > 0
+    pl.when(has_right)(lambda: cross_out(1).start())
+    pl.when(has_left)(lambda: cross_out(0).start())
+    for step in range(1, pieces):
+        part_out(step).start()
+    summed = parts[place]
+    for step in range(1, pieces):
+        part_in(step).wait_recv()
+        summed = summed + part_slots[step]
+    held[0:8] = jnp.zeros((8, piece), f32)
+    held[8 : 8 + total_rows] = summed[0:total_rows]
+    held[8 + total_rows : 16 + total_rows] = jnp.zeros((8, piece), f32)
+    held[16 + total_rows :] = summed[total_rows:]
+    for came, present, at in (
+        (0, has_left & (place == 0), 0), (1, has_right & (place == pieces - 1), 8)
+    ):
+        @pl.when(present)
+        def _(came=came, at=at):
+            running = held[16 + total_rows + at : 24 + total_rows + at]
+            for source in range(pieces):
+                cross_in(came, source).wait_recv()
+                running = running + cross_slots[came, source]
+            held[16 + total_rows + at : 24 + total_rows + at] = running
+
+    for target in range(bands):
+        lines[target, 0 : rows + 16] = held[target * rows : target * rows + rows + 16]
+        lines[target, rows + 16 :] = held[16 + total_rows :]
+
+    def line_out(step):
+        peer = lax.rem(band + step, bands)
+        return remote(
+            lines.at[peer], line_slots.at[bands - step], line_send.at[step],
+            line_recv.at[bands - step], {"band": peer},
+        )
+
+    def line_in(step):
+        peer = lax.rem(band + step, bands)
+        return remote(
+            lines.at[peer], line_slots.at[step], line_send.at[step], line_recv.at[step],
+            {"band": peer},
+        )
+
+    for step in range(1, bands):
+        line_out(step).start()
+    out_speed[...] = speed_all[
+        pl.ds(pl.multiple_of(band * rows, 8), rows + 16), pl.ds(column, 3 * piece)
+    ]
+    pl.when(group > 0)(lambda: cot_right().wait_recv())
+    pl.when(group < groups - 1)(lambda: cot_left().wait_recv())
+    out_cot[...] = cot_all[...]
+    out_image[...] = jnp.zeros(out_image.shape, f32)
+    strips[...] = jnp.zeros(strips.shape, f32)
+    final = lines[band]
+    for step in range(1, bands):
+        line_in(step).wait_recv()
+        final = final + line_slots[step]
+    out_image[:, piece : 2 * piece] = final[0 : rows + 16]
+    strips[8 : 8 + total_rows, 0:16] = final[rows + 16 :].T
+    around = pl.ds(pl.multiple_of(band * rows, 8), rows + 16)
+    near = strips[around, :]
+    out_image[:, piece - 8 : piece] = near[:, 0:8]
+    out_image[:, 2 * piece : 2 * piece + 8] = near[:, 8:16]
+
+    for step in range(1, bands):
+        speed_line(step).wait_send()
+    pl.when(band < bands - 1)(lambda: cot_down().wait_send())
+    pl.when(band > 0)(lambda: cot_up().wait_send())
+    for turn in range(1, sides):
+        pl.when(is_mine)(lambda turn=turn: small_out(turn).wait_send())
+    for index in range(4):
+        each_field_out(index, lambda copy: copy.wait_send())
+    for step in range(1, groups):
+        speed_plane(step).wait_send()
+    pl.when(group < groups - 1)(lambda: cot_right().wait_send())
+    pl.when(group > 0)(lambda: cot_left().wait_send())
+    pl.when(has_right)(lambda: cross_out(1).wait_send())
+    pl.when(has_left)(lambda: cross_out(0).wait_send())
+    for step in range(1, pieces):
+        part_out(step).wait_send()
+    for step in range(1, bands):
+        line_out(step).wait_send()
+
+
+def waves_and_pieces(
+    velocity, wave_now, wave_before, adjoint_last, adjoint_after, wavelet, source_col, rec_first,
+    rec_last, rec_count, observed, cotangent,
+):
+    shots = lax.axis_size("shot")
+    nets = lax.axis_size("net")
+    bands = lax.axis_size("band")
+    mine_shots, rows, breadth = wave_now.shape
+    total_rows = rows * bands
+    steps = observed.shape[1]
+    piece = cotangent.shape[1]
+    sides = bands // mine_shots
+    pieces = shots * nets // sides
+    groups = shots * nets
+    half = breadth // sides
+    width = half + 8 * steps
+    depth = total_rows // 8
+    f32 = jnp.float32
+    dma = pltpu.SemaphoreType.DMA
+    anywhere = [pl.BlockSpec(memory_space=pl.ANY)]
+    scalars = [pl.BlockSpec(memory_space=pltpu.SMEM)]
+    return pl.pallas_call(
+        functools.partial(wave_kernel, (shots, nets, bands)),
+        name="waves",
+        out_shape=[jax.ShapeDtypeStruct((rows + 16, 3 * piece), f32)] * 3,
+        in_specs=anywhere * 5 + scalars * 5 + vmem(2),
+        out_specs=vmem(3),
+        scratch_shapes=[
+            pltpu.VMEM((4, total_rows, width), f32),
+            pltpu.VMEM((total_rows + 16, breadth + 2 * piece), f32),
+            pltpu.VMEM((depth, 8, width), f32),
+            pltpu.VMEM((8 + steps, 128), f32),
+            pltpu.VMEM((steps, width), f32),
+            pltpu.VMEM((8, width), f32),
+            pltpu.VMEM((8, width), f32),
+            pltpu.VMEM((steps + 2, depth + 8, 8, width), f32),
+            pltpu.VMEM((2, depth + 8, 8, width), f32),
+            pltpu.VMEM((depth, 8, width), f32),
+            pltpu.VMEM((width // 128, total_rows, 128), f32),
+            pltpu.VMEM((pieces, total_rows + 16, piece), f32),
+            pltpu.VMEM((pieces, total_rows + 16, piece), f32),
+            pltpu.VMEM((2, 8, total_rows), f32),
+            pltpu.VMEM((2, pieces, 8, total_rows), f32),
+            pltpu.VMEM((total_rows + 32, piece), f32),
+            pltpu.VMEM((bands, rows + 32, piece), f32),
+            pltpu.VMEM((bands, rows + 32, piece), f32),
+            pltpu.VMEM((total_rows + 16, 128), f32),
+            pltpu.VMEM((rows + 16, 3 * piece), f32),
+            dma((5,)),
+            dma((bands,)),
+            dma((bands,)),
+            dma((groups,)),
+            dma((groups,)),
+            dma((4, mine_shots * sides)),
+            dma((4, bands)),
+            dma((sides,)),
+            dma((1,)),
+            dma((4,)),
+            dma((4,)),
+            dma((pieces,)),
+            dma((pieces,)),
+            dma((2,)),
+            dma((2, pieces)),
+            dma((bands,)),
+            dma((bands,)),
+        ],
+        compiler_params=pltpu.CompilerParams(
+            collective_id=3, has_side_effects=True, vmem_limit_bytes=56 * 1024 * 1024
+        ),
+    )(
+        velocity, wave_now, wave_before, adjoint_last, adjoint_after, wavelet, source_col,
+        rec_first, rec_last, rec_count, observed, cotangent,
+    )
+
+
+def fits_whole_columns(wave_now, observed, cotangent):
+    mine_shots, rows, breadth = wave_now.shape
+    shots = lax.axis_size("shot")
+    nets = lax.axis_size("net")
+    bands = lax.axis_size("band")
+    steps, slots = observed.shape[1:]
+    return (
+        bands == 2 * mine_shots
+        and shots % 2 == 0
+        and rows * bands == 128
+        and rows % 8 == 0
+        and breadth % 256 == 0
+        and cotangent.shape[1] == 128
+        and 8 * steps == 128
+        and slots == 128
+        and breadth * slots < 2**24
+    )
+
+
+def update_model(around, image, cot, velocity, cotangent, num_steps, shot_count, conv_in, conv_mid, conv_out):
     rows, breadth = velocity.shape
     piece = cotangent.shape[1]
     channels = conv_mid.shape[0]
     bands = lax.axis_size("band")
     groups = lax.axis_size(group_axes)
-    image, cot, low, high = gather_pieces(imaging, velocity, cotangent)
     scaled = image[5:-5, piece - 3 : 2 * piece + 3] / float(num_steps * shot_count) ** 0.5
     cot = cot[5:-5, piece - 3 : 2 * piece + 3]
-    tall = jnp.concatenate([low[5:], velocity, high[:3]], 0)
     start_col = lax.axis_index(group_axes) * piece
-    around = lax.dynamic_slice_in_dim(
-        jnp.pad(tall, ((0, 0), (piece, piece))), start_col, 3 * piece, 1
-    )[:, piece - 3 : 2 * piece + 3]
+    around = around[5:-5, piece - 3 : 2 * piece + 3]
     height, width = around.shape
     row_ids = lax.axis_index("band") * rows - 3 + jnp.arange(height)
     col_ids = start_col - 3 + jnp.arange(width)
@@ -546,6 +1118,15 @@
     num_steps = wavelet.shape[1]
     slots = observed.shape[2]
     piece_cols = cotangent.shape[1]
+    group_count = shot_here * lax.axis_size(("shot", "net"))
+    if fits_whole_columns(wave_now, observed, cotangent):
+        image, cot, around = waves_and_pieces(
+            velocity, wave_now, wave_before, adjoint_last, adjoint_after, wavelet, source_col,
+            rec_first, rec_last, rec_count, observed, cotangent,
+        )
+        return update_model(
+            around, image, cot, velocity, cotangent, num_steps, group_count, conv_in, conv_mid, conv_out
+        )
     first_row = lax.axis_index("band") * rows_here
     speed_sq = (velocity * speed_factor) ** 2
     columns = jnp.arange(breadth, dtype=jnp.int32)
@@ -598,9 +1179,14 @@
     misfit = (samples - jnp.transpose(observed, (1, 0, 2))) * active[None]
     adjoint = propagate(adjoint_last, adjoint_after, misfit[::-1], receiver_term)
     imaging = jnp.sum(stored * adjoint[::-1], axis=(0, 1))
-    group_count = shot_here * lax.axis_size(("shot", "net"))
+    image, cot, low, high = gather_pieces(imaging, velocity, cotangent)
+    tall = jnp.concatenate([low, velocity, high], 0)
+    around = lax.dynamic_slice_in_dim(
+        jnp.pad(tall, ((0, 0), (piece_cols, piece_cols))),
+        lax.axis_index(group_axes) * piece_cols, 3 * piece_cols, 1,
+    )
     return update_model(
-        imaging, velocity, cotangent, num_steps, group_count, conv_in, conv_mid, conv_out
+        around, image, cot, velocity, cotangent, num_steps, group_count, conv_in, conv_mid, conv_out
     )
 
 

time: 226 us -> 123 us (0.54)
  Pallas kernels: 47.4 us -> 110 us
  starting transfers between devices: 55.6 us -> 0 us
  other arithmetic: 49.7 us -> 1.73 us
  local copies, waits for them, and re-layouts: 36.7 us -> 9.99 us
  matrix products: 17.3 us -> 0 us
  waiting for transfers between devices: 15.9 us -> 0 us
    pallas_call x1, Pallas kernels: 14.5 us -> 77.9 us  [waves_and_pieces(): pl.pallas_call(functools.partial(wave_kernel, (shots, nets, bands)), name...]
    ppermute x18 -> x0, starting transfers between devices: 55.6 us -> none  [the longest x9 44 us: extended_2(): lax.ppermute(lax.slice_in_dim(block, block.shape[dim] - width, None, axis...]
    add x25 -> x0, other arithmetic: 22.5 us -> none  [the longest x24 21.6 us: block(): 2.0 * current[:, 4:-4] - earlier[:, 4:-4] + speed_part * laplace(current)]
    dot_general x17 -> x0, matrix products: 17.3 us -> none  [the longest x16 16.8 us: receiver_term(): injected = jnp.einsum('swk,sk->sw', table, residual, precision=highest)]
    ppermute x18 -> x0, waiting for transfers between devices: 15.9 us -> none  [the longest x9 10.6 us: extended_2(): lax.ppermute(lax.slice_in_dim(block, 0, width, axis=dim), axis, backward)]
    reshape x2 -> x0, local copies, waits for them, and re-layouts: 11.2 us -> none  [propagate(): return states.reshape((num_steps,) + start.shape)]
    dynamic_update_slice x8 -> x0, other arithmetic: 8.83 us -> none  [propagate(): ignored, states = lax.scan(block, (start, prior), grouped)]
    reduce_sum x1 -> x0, other arithmetic: 7.07 us -> none  [on_device(): imaging = jnp.sum(stored * adjoint[::-1], axis=(0, 1))]
  transfers between devices with their start and end apart: 18 -> 0, of which waited for: 8 -> 0; matrix products, arithmetic and copies ran while one was open for 11% -> 0% of each run, Pallas kernels for 0% -> 0%
where the time goes in v1:
time: 123 us; the launch traced here: 122 us
  Pallas kernels  110 us (89%)
  local copies, waits for them, and re-layouts  9.99 us (8%)
  other arithmetic  1.73 us (1%)
    pallas_call x1, Pallas kernels, waves_and_pieces(): pl.pallas_call(functools.partial(wave_kernel, (shots, nets, bands)), name...  77.9 us
    pallas_call x1, Pallas kernels, total_grads(): pl.pallas_call(functools.partial(total_kernel, sizes), name='total_grads'...  16 us
    pallas_call x1, Pallas kernels, network(): pl.pallas_call(functools.partial(network_kernel, width), name='network',...  15.6 us
    unnamed x17, local copies, waits for them, and re-layouts  3.38 us

profile of v1, /device:TPU:0, one launch (start us, length us, event | category | flops | bytes accessed | tf_op | source)
XLA Modules:
  0.0 122.2 jit_solution(17046916852757221762)
XLA Ops:
  0.6 0.7 reduce
  1.3 0.1 reshape.102
  1.5 0.0 copy-start.6
  1.5 0.1 copy.27
  1.5 0.6 copy-done.6
  2.2 0.0 copy-start
  2.2 0.1 copy.26
  2.3 0.7 copy-done
  3.0 0.1 copy.28
  3.1 0.1 copy.29
  3.2 0.1 copy.30.middle_back
  3.3 0.1 reshape.106
  3.4 77.9 %waves.1 = (f32[48,384]{1,0:T(8,128)}, f32[48,384]{1,0:T(8,128)}, f32[48,384]{1,0:T(8,128)}) custom-call(f32[32,1024]{1,0:T(8,128)} %velocity.1, f32[2,32,1024]{2,1,0:T(8,128)} %wave_now.1, f32[2,32,1024]{2,1,0:T(8,128)} %wave_before.1, f32[2,32,1024]{2,1,0:T(8,128)} %adjoint_last.1, f32[2,32,1024]{2,1,0:T(8,128)} %adjoint_after.1, f32[2,16]{1,0:T(2,128)} %wavelet.1, ...), custom_call_target="tpu_custom_call" | custom-call | tf_op jit(solution)/shard_map/waves/pallas_call | solution.py:992
  81.3 0.0 copy-start.4
  81.3 1.0 slice.30
  82.3 0.0 copy-start.3
  82.3 0.2 stack.22
  82.5 0.0 copy-done.4
  82.5 0.6 copy-done.3
  83.1 1.0 slice_multiply_fusion.1
  84.1 0.2 stack.23
  84.3 0.2 stack.24
  84.5 0.2 stack.25
  84.6 0.1 and.43
  84.7 0.2 and.44
  84.9 0.2 and.47
  85.2 0.0 copy-start.5
  85.2 0.7 copy-done.5
  85.9 0.2 stack.28
  86.1 15.6 %network.1 = (f32[1,5120]{1,0:T(1,128)S(1)}, f32[32,640]{1,0:T(8,128)S(1)}) custom-call(f32[64,72]{1,0:T(8,128)S(1)} %pad_maximum_fusion.first, f32[32,288]{1,0:T(8,128)S(1)} %copy-done, f32[32,288]{1,0:T(8,128)S(1)} %copy.30.middle_back, f32[16,32]{1,0:T(8,128)S(1)} %pad.18.last, f32[8,5120]{1,0:T(8,128)S(1)} %pad.19.layers), custom_call_target="tpu_custom_call" | custom-call | tf_op jit(solution)/shard_map/network/pallas_call | solution.py:467
  101.7 0.0 copy-start.1
  101.7 0.6 copy-done.1
  102.3 0.1 slice_reduce_fusion
  102.4 0.1 reshape_squeeze.3
  102.5 0.7 slice.40
  103.2 16.0 %total_grads.1 = f32[32,640]{1,0:T(8,128)} custom-call(f32[32,640]{1,0:T(8,128)} %copy-done.1), custom_call_target="tpu_custom_call" | custom-call | tf_op jit(solution)/shard_map/total_grads/pallas_call | solution.py:331
  119.3 0.0 copy-start.2
  119.3 0.8 fusion
  120.1 0.1 copy.31
  120.2 0.6 reshape.108
  120.8 0.0 copy-done.2
  120.8 0.6 slice.37
  121.4 0.1 copy.32
  121.5 0.6 reshape.110
  (18 shorter events, 0.2 us)
Async XLA Ops:
  1.5 0.7 copy-start.6
  2.2 0.8 copy-start
  81.3 1.2 copy-start.4
  82.3 0.8 copy-start.3
  85.2 0.7 copy-start.5
  101.7 0.6 copy-start.1
  119.3 1.5 %copy-start.2 = (f32[32,640]{1,0:T(8,128)S(1)}, f32[32,640]{1,0:T(8,128)}, u32[]{:S(2)}) copy-start(f32[32,640]{1,0:T(8,128)} %total_grads.1) | copy-start | bytes 245764

commit v2 on v1

--- a/solution.py
+++ b/solution.py
@@ -8,6 +8,8 @@
 from jax.experimental.pallas import tpu as pltpu
 from jax.sharding import PartitionSpec as P
 
+weights = (-28700.0, 8064.0, -1008.0, 128.0, -9.0)
+weight_scale = 5040.0
 coefficients = (-205.0 / 72.0, 8.0 / 5.0, -1.0 / 5.0, 8.0 / 315.0, -1.0 / 560.0)
 speed_factor = 0.11
 source_depth = 2
@@ -492,9 +494,9 @@
     rec_last, rec_count, observed, cotangent,
     out_image, out_cot, out_speed,
     arrived, speed_all, speed_sq, small, observed_cols, source_mask, receiver_mask,
-    forward, adjoint, image, flat, parts, part_slots, cross, cross_slots, held, lines, line_slots,
+    down_weights, across_weights, split, forward, adjoint, image, parts, part_slots, cross, cross_slots, held, lines, line_slots,
     strips, cot_all,
-    own_sem, speed_send, speed_recv, plane_send, plane_recv, field_send, field_recv, small_send,
+    own_sem, edge_send, edge_recv, speed_send, speed_recv, plane_send, plane_recv, field_send, field_recv, small_send,
     small_recv, cot_send, cot_recv, part_send, part_recv, cross_send, cross_recv, line_send, line_recv,
 ):
     shots, nets, bands = sizes
@@ -504,25 +506,26 @@
     slots = observed.shape[2]
     piece = cotangent.shape[1]
     sides = bands // mine_shots
-    per_side = shots // sides
-    pieces = per_side * nets
+    pairs = shots // sides
+    pieces = pairs * nets
     groups = shots * nets
     half = breadth // sides
     margin = 8 * steps
     width = half + margin
-    depth = total_rows // 8
+    tiles = width // 128
     f32 = jnp.float32
     shot = lax.axis_index("shot")
     net = lax.axis_index("net")
     band = lax.axis_index("band")
-    side = shot // per_side
-    lane_in_side = lax.rem(shot, per_side)
+    side = lax.rem(shot, sides)
+    pair = shot // sides
     group = shot * nets + net
-    place = lane_in_side * nets + net
+    place = pair * nets + net
     owner_side = lax.rem(band, sides)
     owner_slot = band // sides
     is_mine = owner_side == side
-    own_start = side * margin
+    kept = side * pieces + place
+    swapped = kept != group
 
     cot_all[...] = jnp.zeros(cot_all.shape, f32)
     barrier = pltpu.get_barrier_semaphore()
@@ -536,25 +539,39 @@
         pl.semaphore_signal(
             barrier, inc=1, device_id={"band": lax.rem(band + step, bands)}, device_id_type=MESH
         )
-    for turn in range(1, sides):
-        other = lax.rem(side + turn, sides) * per_side + lane_in_side
+    for step in range(1, bands):
+        pl.semaphore_signal(
+            barrier, inc=1,
+            device_id={"shot": pair * sides + 1 - side, "band": lax.rem(band + step, bands)},
+            device_id_type=MESH,
+        )
+
+    @pl.when(swapped)
+    def _():
         for step in range(1, bands):
             pl.semaphore_signal(
-                barrier, inc=1, device_id={"shot": other, "band": lax.rem(band + step, bands)},
+                barrier, inc=1,
+                device_id={
+                    "shot": kept // nets, "net": lax.rem(kept, nets),
+                    "band": lax.rem(band + step, bands),
+                },
                 device_id_type=MESH,
             )
 
     column = pl.multiple_of(group * piece, 128)
 
     def window(which):
-        return pl.ds(pl.multiple_of(which * (half - margin), 128), width)
+        return pl.ds(which * half if isinstance(which, int) else pl.multiple_of(which * half, 128), half)
+
+    def landing(which):
+        return pl.ds(which * margin if isinstance(which, int) else pl.multiple_of(which * margin, 128), half)
 
     fields = (wave_now, wave_before, adjoint_last, adjoint_after)
 
     def own_field(index):
         return pltpu.make_async_copy(
             fields[index].at[owner_slot, :, window(side)],
-            arrived.at[index, pl.ds(pl.multiple_of(band * rows, 8), rows)],
+            arrived.at[index, pl.ds(pl.multiple_of(band * rows, 8), rows), landing(side)],
             own_sem.at[index],
         )
 
@@ -586,7 +603,7 @@
         small[0:8] = table
         small[8 : 8 + steps] = observed[owner_slot]
 
-    peers = groups - 1 + bands - 1 + (sides - 1) * (bands - 1)
+    peers = groups - 1 + 2 * (bands - 1) + (bands - 1) * lax.min(lax.abs(kept - group), 1)
     pl.semaphore_wait(barrier, peers)
 
     def speed_line(step):
@@ -626,7 +643,7 @@
     def small_out(turn):
         return remote(
             small, small, small_send.at[turn], small_recv.at[0],
-            {"shot": lax.rem(side + turn, sides) * per_side + lane_in_side},
+            {"shot": pair * sides + 1 - side},
         )
 
     def cot_down():
@@ -661,17 +678,24 @@
         target = slot * sides + side
         return target, remote(
             fields[index].at[slot, :, window(which)],
-            arrived.at[index, pl.ds(pl.multiple_of(band * rows, 8), rows)],
+            arrived.at[index, pl.ds(pl.multiple_of(band * rows, 8), rows), landing(which)],
             field_send.at[index, turn * sides + which], field_recv.at[index, band],
-            {"shot": which * per_side + lane_in_side, "band": target},
+            {"shot": pair * sides + which, "band": target},
         )
 
     def field_in(index, source):
         return remote(
-            fields[index].at[0, :, pl.ds(0, width)],
-            arrived.at[index, pl.ds(source * rows, rows)],
+            fields[index].at[0, :, pl.ds(0, half)],
+            arrived.at[index, pl.ds(source * rows, rows), pl.ds(0, half)],
             field_send.at[index, 0], field_recv.at[index, source],
-            {"shot": owner_side * per_side + lane_in_side, "band": source},
+            {"shot": pair * sides + owner_side, "band": source},
+        )
+
+    def edge(index):
+        return remote(
+            arrived.at[index, :, pl.ds(pl.multiple_of((half - margin) * (1 - side) + margin * side, 128), margin)],
+            arrived.at[index, :, pl.ds(pl.multiple_of(half * side, 128), margin)],
+            edge_send.at[index], edge_recv.at[index], {"shot": pair * sides + 1 - side},
         )
 
     def each_field_out(index, act):
@@ -711,17 +735,35 @@
 
     cols = lax.broadcasted_iota(jnp.int32, (8, width), 1)
     level = lax.broadcasted_iota(jnp.int32, (8, width), 0)
+    down_gap = lax.broadcasted_iota(jnp.int32, (total_rows, 2 * total_rows), 1)
+    down_gap = jnp.abs(
+        jnp.where(down_gap < total_rows, down_gap, down_gap - total_rows)
+        - lax.broadcasted_iota(jnp.int32, (total_rows, 2 * total_rows), 0)
+    )
+    across_gap = lax.broadcasted_iota(jnp.int32, (768, 128), 0)
+    across_gap = jnp.abs(
+        jnp.where(across_gap < 384, across_gap, across_gap - 384) - 128
+        - lax.broadcasted_iota(jnp.int32, (768, 128), 1)
+    )
+
+    def banded(gap):
+        matrix = jnp.zeros(gap.shape, f32)
+        for reach in range(1, 5):
+            matrix = jnp.where(gap == reach, weights[reach], matrix)
+        return matrix.astype(jnp.bfloat16)
+
+    down_weights[...] = banded(down_gap)
+    across_weights[...] = banded(across_gap)
     first_cell = jnp.where(side == 0, 0, 4)
     last_cell = jnp.where(side == 0, width - 4, width)
     inside = (cols >= first_cell) & (cols < last_cell)
-    keep = inside.astype(f32)
-    top = inside & (level == 0)
+    keep = inside.astype(f32)[0:1]
     actual = (cols + side * (half - margin)).astype(f32)
 
     def setting(index):
         return jnp.broadcast_to(small[index : index + 1, 0:1], (8, width))
 
-    source_mask[...] = jnp.where(top & (actual == setting(1)), 1.0, 0.0)
+    source_mask[...] = jnp.where(inside & (level == source_depth) & (actual == setting(1)), 1.0, 0.0)
     first = small[2:3, 0:1]
     span = small[3:4, 0:1] - first
     count = small[4:5, 0:1]
@@ -742,110 +784,107 @@
         stacked, chosen, (((1,), (0,)), ((), ())), preferred_element_type=f32
     )
     observed_cols[...] = (spread[:steps] + spread[steps : 2 * steps]) + spread[2 * steps : 3 * steps]
-    receiver_mask[...] = jnp.where(top, spread[3 * steps : 3 * steps + 8], 0.0)
+    receiver_mask[...] = jnp.where(inside & (level == receiver_depth), spread[3 * steps : 3 * steps + 8], 0.0)
 
     for step in range(1, groups):
         speed_plane_in(step).wait_recv()
-    tiles = width // 128
     for tile in range(tiles):
         start = pl.multiple_of(piece + side * (half - margin) + tile * 128, 128)
-        flat[tile] = speed_all[pl.ds(8, total_rows), pl.ds(start, 128)]
-
-    def picked(line):
-        return jnp.concatenate(
-            [flat[tile, pl.ds(line, 8, stride=depth), :] for tile in range(tiles)], 1
-        )
-
-    for line in range(depth):
-        value = picked(line) * speed_factor
-        speed_sq[line] = value * value * keep
-
-    def refill(ref, at):
-        above = pltpu.roll(ref[at, depth : depth + 4], 1, 1)
-        below = pltpu.roll(ref[at, 4:8], 7, 1)
-        edge = lax.broadcasted_iota(jnp.int32, (4, 8, width), 1)
-        ref[at, 0:4] = jnp.where(edge == 0, 0.0, above)
-        ref[at, depth + 4 :] = jnp.where(edge == 7, 0.0, below)
-
-    def unpack(index, ref, at):
+        at = slice(tile * 128, tile * 128 + 128)
+        value = speed_all[pl.ds(8, total_rows), pl.ds(start, 128)] * speed_factor
+        speed_sq[:, at] = value * value * (keep[:, at] * (1.0 / weight_scale))
+
+    def advance(ref, now, before, finish):
         for tile in range(tiles):
-            flat[tile] = arrived[index, :, tile * 128 : tile * 128 + 128]
-        for line in range(depth):
-            ref[at, 4 + line] = picked(line) * keep
-
-    tall = 2
-
-    def advance(ref, now, before, line):
-        center = ref[now, pl.ds(4 + line, tall)]
-        running = (2.0 * coefficients[0]) * center
-        for reach in range(1, 5):
-            vertical = ref[now, pl.ds(4 + line - reach, tall)] + ref[now, pl.ds(4 + line + reach, tall)]
-            lateral = pltpu.roll(center, reach, 2) + pltpu.roll(center, width - reach, 2)
-            running = running + coefficients[reach] * (vertical + lateral)
-        return 2.0 * center - ref[before, pl.ds(4 + line, tall)] + speed_sq[pl.ds(line, tall)] * running
-
-    each_field_in(0)
-    unpack(0, forward, 1)
-    refill(forward, 1)
-    each_field_in(1)
-    unpack(1, forward, 0)
+            at = slice(tile * 128, tile * 128 + 128)
+            value = ref[now, :, at]
+            high = value.astype(jnp.bfloat16)
+            split[0:total_rows, at] = high
+            split[total_rows:, at] = (value - high.astype(f32)).astype(jnp.bfloat16)
+        down = lax.dot_general(
+            down_weights[...], split[...], (((1,), (0,)), ((), ())), preferred_element_type=f32
+        )
+        rows_of = []
+        for tile in range(tiles):
+            near = [(tile + tiles + shift) % tiles for shift in (-1, 0, 1)]
+            rows_of.append(
+                jnp.concatenate(
+                    [
+                        split[part * total_rows : part * total_rows + total_rows, t * 128 : t * 128 + 128]
+                        for part in range(2)
+                        for t in near
+                    ],
+                    1,
+                )
+            )
+        across = lax.dot_general(
+            jnp.concatenate(rows_of, 0), across_weights[...], (((1,), (0,)), ((), ())),
+            preferred_element_type=f32,
+        )
+        for tile in range(tiles):
+            at = slice(tile * 128, tile * 128 + 128)
+            value = ref[now, :, at]
+            total = (
+                weights[0] * value + down[:, at]
+                + across[tile * total_rows : tile * total_rows + total_rows]
+            )
+            finish(at, 2.0 * value - ref[before, :, at] + speed_sq[:, at] * total)
+
+    def settle(index, ref, at):
+        edge(index).wait_recv()
+        ref[at] = arrived[index] * keep
+
+    for index in (0, 1):
+        each_field_in(index)
+        edge(index).start()
     for index in (2, 3):
         each_field_out(index, lambda copy: copy.start())
+    settle(0, forward, 1)
+    settle(1, forward, 0)
 
     pulses = small[0:1]
     pulse_ids = lax.broadcasted_iota(jnp.int32, (1, 128), 1)
 
     def forward_step(index, carry):
-        for line in range(0, depth, tall):
-            forward[index + 2, pl.ds(4 + line, tall)] = advance(forward, index + 1, index, line)
         amount = jnp.sum(jnp.where(pulse_ids == index, pulses, 0.0), axis=1, keepdims=True)
-        forward[index + 2, 4 + source_depth] = (
-            forward[index + 2, 4 + source_depth] + source_mask[...] * amount
-        )
-        refill(forward, index + 2)
+        added = source_mask[...] * amount
+
+        def finish(at, fresh):
+            forward[index + 2, :, at] = jnp.concatenate([fresh[0:8] + added[:, at], fresh[8:]], 0)
+
+        advance(forward, index + 1, index, finish)
         return carry
 
     lax.fori_loop(0, steps, forward_step, 0)
 
     for index in (2, 3):
         each_field_in(index)
-    unpack(2, adjoint, 0)
-    refill(adjoint, 0)
-    unpack(3, adjoint, 1)
+        edge(index).start()
+    settle(2, adjoint, 0)
+    settle(3, adjoint, 1)
     image[...] = jnp.zeros(image.shape, f32)
 
     def adjoint_step(index, carry):
         moment = steps - 1 - index
         now = lax.rem(index, 2)
         later = 1 - now
-        held_now = forward.at[moment + 2]
-        injected = receiver_mask[...] * (
-            held_now[4 + receiver_depth] - observed_cols[pl.ds(moment, 1), :]
-        )
-        for line in range(0, depth, tall):
-            fresh = advance(adjoint, now, later, line)
-            if line <= receiver_depth < line + tall:
-                blank = jnp.zeros((1, 8, width), f32)
-                fresh = fresh + jnp.concatenate(
-                    [injected[None] if line + k == receiver_depth else blank for k in range(tall)], 0
-                )
-            adjoint[later, pl.ds(4 + line, tall)] = fresh
-            image[pl.ds(line, tall)] = (
-                image[pl.ds(line, tall)] + held_now[pl.ds(4 + line, tall)] * fresh
-            )
-        refill(adjoint, later)
+        added = receiver_mask[...] * (
+            forward[moment + 2, 0:8] - observed_cols[pl.ds(moment, 1), :]
+        )
+
+        def finish(at, fresh):
+            fresh = jnp.concatenate([fresh[0:8] + added[:, at], fresh[8:]], 0)
+            adjoint[later, :, at] = fresh
+            image[:, at] = image[:, at] + forward[moment + 2, :, at] * fresh
+
+        advance(adjoint, now, later, finish)
         return carry
 
     lax.fori_loop(0, steps, adjoint_step, 0)
-
-    for line in range(depth):
-        value = image[line]
-        for tile in range(tiles):
-            flat[tile, pl.ds(line, 8, stride=depth), :] = value[:, tile * 128 : tile * 128 + 128]
 
     parts[...] = jnp.zeros(parts.shape, f32)
     for index in range(pieces):
-        block = flat[own_start // 128 + index]
+        block = image[:, pl.ds(pl.multiple_of(side * margin + index * piece, 128), piece)]
         parts[index, 0:total_rows] = block
         turned = block.T
         if index + 1 < pieces:
@@ -857,25 +896,28 @@
         else:
             cross[0] = turned[0:8]
 
+    def holder(which, index):
+        return {"shot": index // nets * sides + which, "net": lax.rem(index, nets)}
+
     def part_out(step):
         peer = lax.rem(place + step, pieces)
         return remote(
             parts.at[peer], part_slots.at[pieces - step], part_send.at[step],
-            part_recv.at[pieces - step], member(side * pieces + peer),
+            part_recv.at[pieces - step], holder(side, peer),
         )
 
     def part_in(step):
         peer = lax.rem(place + step, pieces)
         return remote(
             parts.at[peer], part_slots.at[step], part_send.at[step],
-            part_recv.at[step], member(side * pieces + peer),
+            part_recv.at[step], holder(side, peer),
         )
 
     def cross_out(toward):
-        target = (side + 1) * pieces if toward else side * pieces - 1
+        target = holder(side + 1, 0) if toward else holder(side - 1, jnp.int32(pieces - 1))
         return remote(
             cross.at[toward], cross_slots.at[1 - toward, place], cross_send.at[toward],
-            cross_recv.at[1 - toward, place], member(target),
+            cross_recv.at[1 - toward, place], target,
         )
 
     def cross_in(came, source):
@@ -916,19 +958,26 @@
     def line_out(step):
         peer = lax.rem(band + step, bands)
         return remote(
-            lines.at[peer], line_slots.at[bands - step], line_send.at[step],
-            line_recv.at[bands - step], {"band": peer},
+            lines.at[peer], line_slots.at[(bands - step) % bands], line_send.at[step],
+            line_recv.at[(bands - step) % bands],
+            {"shot": kept // nets, "net": lax.rem(kept, nets), "band": peer},
         )
 
     def line_in(step):
         peer = lax.rem(band + step, bands)
         return remote(
             lines.at[peer], line_slots.at[step], line_send.at[step], line_recv.at[step],
-            {"band": peer},
+            {"shot": kept // nets, "net": lax.rem(kept, nets), "band": peer},
         )
 
     for step in range(1, bands):
         line_out(step).start()
+    pl.when(swapped)(lambda: line_out(0).start())
+
+    @pl.when(jnp.logical_not(swapped))
+    def _():
+        line_slots[0] = lines[band]
+
     out_speed[...] = speed_all[
         pl.ds(pl.multiple_of(band * rows, 8), rows + 16), pl.ds(column, 3 * piece)
     ]
@@ -937,7 +986,8 @@
     out_cot[...] = cot_all[...]
     out_image[...] = jnp.zeros(out_image.shape, f32)
     strips[...] = jnp.zeros(strips.shape, f32)
-    final = lines[band]
+    pl.when(swapped)(lambda: line_in(0).wait_recv())
+    final = line_slots[0]
     for step in range(1, bands):
         line_in(step).wait_recv()
         final = final + line_slots[step]
@@ -956,6 +1006,7 @@
         pl.when(is_mine)(lambda turn=turn: small_out(turn).wait_send())
     for index in range(4):
         each_field_out(index, lambda copy: copy.wait_send())
+        edge(index).wait_send()
     for step in range(1, groups):
         speed_plane(step).wait_send()
     pl.when(group < groups - 1)(lambda: cot_right().wait_send())
@@ -966,6 +1017,7 @@
         part_out(step).wait_send()
     for step in range(1, bands):
         line_out(step).wait_send()
+    pl.when(swapped)(lambda: line_out(0).wait_send())
 
 
 def waves_and_pieces(
@@ -984,7 +1036,6 @@
     groups = shots * nets
     half = breadth // sides
     width = half + 8 * steps
-    depth = total_rows // 8
     f32 = jnp.float32
     dma = pltpu.SemaphoreType.DMA
     anywhere = [pl.BlockSpec(memory_space=pl.ANY)]
@@ -998,15 +1049,17 @@
         scratch_shapes=[
             pltpu.VMEM((4, total_rows, width), f32),
             pltpu.VMEM((total_rows + 16, breadth + 2 * piece), f32),
-            pltpu.VMEM((depth, 8, width), f32),
+            pltpu.VMEM((total_rows, width), f32),
             pltpu.VMEM((8 + steps, 128), f32),
             pltpu.VMEM((steps, width), f32),
             pltpu.VMEM((8, width), f32),
             pltpu.VMEM((8, width), f32),
-            pltpu.VMEM((steps + 2, depth + 8, 8, width), f32),
-            pltpu.VMEM((2, depth + 8, 8, width), f32),
-            pltpu.VMEM((depth, 8, width), f32),
-            pltpu.VMEM((width // 128, total_rows, 128), f32),
+            pltpu.VMEM((total_rows, 2 * total_rows), jnp.bfloat16),
+            pltpu.VMEM((768, 128), jnp.bfloat16),
+            pltpu.VMEM((2 * total_rows, width), jnp.bfloat16),
+            pltpu.VMEM((steps + 2, total_rows, width), f32),
+            pltpu.VMEM((2, total_rows, width), f32),
+            pltpu.VMEM((total_rows, width), f32),
             pltpu.VMEM((pieces, total_rows + 16, piece), f32),
             pltpu.VMEM((pieces, total_rows + 16, piece), f32),
             pltpu.VMEM((2, 8, total_rows), f32),
@@ -1017,6 +1070,8 @@
             pltpu.VMEM((total_rows + 16, 128), f32),
             pltpu.VMEM((rows + 16, 3 * piece), f32),
             dma((5,)),
+            dma((4,)),
+            dma((4,)),
             dma((bands,)),
             dma((bands,)),
             dma((groups,)),

time: 123 us -> 99.8 us (0.81)
  Pallas kernels: 110 us -> 86.6 us
    pallas_call x1, Pallas kernels: 77.9 us -> 55.6 us  [waves_and_pieces(): pl.pallas_call(functools.partial(wave_kernel, (shots, nets, bands)), name...]
where the time goes in v2:
time: 99.8 us; the launch traced here: 99.2 us
  Pallas kernels  86.6 us (87%)
  local copies, waits for them, and re-layouts  9.99 us (10%)
  other arithmetic  1.73 us (2%)
    pallas_call x1, Pallas kernels, waves_and_pieces(): pl.pallas_call(functools.partial(wave_kernel, (shots, nets, bands)), name...  55.6 us
    pallas_call x1, Pallas kernels, network(): pl.pallas_call(functools.partial(network_kernel, width), name='network',...  15.6 us
    pallas_call x1, Pallas kernels, total_grads(): pl.pallas_call(functools.partial(total_kernel, sizes), name='total_grads'...  15.4 us
    unnamed x17, local copies, waits for them, and re-layouts  3.38 us

profile of v2, /device:TPU:0, one launch (start us, length us, event | category | flops | bytes accessed | tf_op | source)
XLA Modules:
  0.0 99.2 jit_solution(3038173984583349528)
XLA Ops:
  0.6 0.7 reduce
  1.3 0.1 reshape.102
  1.5 0.0 copy-start.6
  1.5 0.1 copy.27
  1.5 0.6 copy-done.6
  2.2 0.0 copy-start
  2.2 0.1 copy.26
  2.3 0.7 copy-done
  3.0 0.1 copy.28
  3.1 0.1 copy.29
  3.2 0.1 copy.30.middle_back
  3.3 0.1 reshape.106
  3.4 55.6 %waves.1 = (f32[48,384]{1,0:T(8,128)}, f32[48,384]{1,0:T(8,128)}, f32[48,384]{1,0:T(8,128)}) custom-call(f32[32,1024]{1,0:T(8,128)} %velocity.1, f32[2,32,1024]{2,1,0:T(8,128)} %wave_now.1, f32[2,32,1024]{2,1,0:T(8,128)} %wave_before.1, f32[2,32,1024]{2,1,0:T(8,128)} %adjoint_last.1, f32[2,32,1024]{2,1,0:T(8,128)} %adjoint_after.1, f32[2,16]{1,0:T(2,128)} %wavelet.1, ...), custom_call_target="tpu_custom_call" | custom-call | tf_op jit(solution)/shard_map/waves/pallas_call | solution.py:1043
  59.0 0.0 copy-start.4
  59.0 1.0 %slice.30 = f32[38,134]{1,0:T(8,128)S(1)} slice(f32[48,384]{1,0:T(8,128)} %get-tuple-element.9), slice={[5:43], [125:259]} | slice | bytes 40736 | tf_op jit(solution)/shard_map/slice | solution.py:1129
  60.0 0.0 copy-start.3
  60.0 0.2 stack.22
  60.2 0.0 copy-done.4
  60.2 0.6 copy-done.3
  60.8 1.0 slice_multiply_fusion.1
  61.8 0.2 stack.23
  62.0 0.2 stack.24
  62.1 0.2 stack.25
  62.3 0.1 and.43
  62.4 0.2 and.44
  62.6 0.2 and.47
  62.8 0.0 copy-start.5
  62.9 0.7 copy-done.5
  63.6 0.2 stack.28
  63.8 15.6 %network.1 = (f32[1,5120]{1,0:T(1,128)S(1)}, f32[32,640]{1,0:T(8,128)S(1)}) custom-call(f32[64,72]{1,0:T(8,128)S(1)} %pad_maximum_fusion.first, f32[32,288]{1,0:T(8,128)S(1)} %copy-done, f32[32,288]{1,0:T(8,128)S(1)} %copy.30.middle_back, f32[16,32]{1,0:T(8,128)S(1)} %pad.18.last, f32[8,5120]{1,0:T(8,128)S(1)} %pad.19.layers), custom_call_target="tpu_custom_call" | custom-call | tf_op jit(solution)/shard_map/network/pallas_call | solution.py:469
  79.4 0.0 copy-start.1
  79.4 0.6 copy-done.1
  80.0 0.1 slice_reduce_fusion
  80.1 0.1 reshape_squeeze.3
  80.2 0.7 slice.40
  80.9 15.4 %total_grads.1 = f32[32,640]{1,0:T(8,128)} custom-call(f32[32,640]{1,0:T(8,128)} %copy-done.1), custom_call_target="tpu_custom_call" | custom-call | tf_op jit(solution)/shard_map/total_grads/pallas_call | solution.py:333
  96.3 0.0 copy-start.2
  96.3 0.8 fusion
  97.1 0.1 copy.31
  97.2 0.6 reshape.108
  97.8 0.0 copy-done.2
  97.8 0.6 slice.37
  98.4 0.1 copy.32
  98.6 0.6 reshape.110
  (18 shorter events, 0.2 us)
Async XLA Ops:
  1.5 0.7 copy-start.6
  2.2 0.8 copy-start
  59.0 1.2 %copy-start.4 = (f32[48,384]{1,0:T(8,128)S(1)}, f32[48,384]{1,0:T(8,128)}, u32[]{:S(2)}) copy-start(f32[48,384]{1,0:T(8,128)} %get-tuple-element.10) | copy-start | bytes 221188
  60.0 0.8 copy-start.3
  62.8 0.7 copy-start.5
  79.4 0.6 copy-start.1
  96.3 1.5 %copy-start.2 = (f32[32,640]{1,0:T(8,128)S(1)}, f32[32,640]{1,0:T(8,128)}, u32[]{:S(2)}) copy-start(f32[32,640]{1,0:T(8,128)} %total_grads.1) | copy-start | bytes 245764

commit v3 on v2

--- a/solution.py
+++ b/solution.py
@@ -488,16 +488,215 @@
     )(first, conv_mid, flipped(conv_mid), last, layers)
 
 
-def wave_kernel(
+def exact_spread(values, table):
+    total = None
+    for turn in range(3):
+        part = values.astype(jnp.bfloat16)
+        values = values - part.astype(jnp.float32)
+        dot = lax.dot_general(
+            part, table, (((1,), (0,)), ((), ())), preferred_element_type=jnp.float32
+        )
+        total = dot if total is None else total + dot
+    return total
+
+
+def stacked_halves(values):
+    return jnp.concatenate(list(halves(values)), 0)
+
+
+def dot_split(left, right_high, right_low, dims):
+    height = left.shape[0] // 2
+    both = lax.dot_general(
+        left, right_high, (dims, ((), ())), preferred_element_type=jnp.float32
+    )
+    rest = lax.dot_general(
+        left[:height], right_low, (dims, ((), ())), preferred_element_type=jnp.float32
+    )
+    return both[:height] + both[height:] + rest
+
+
+def network_weights(conv_in, conv_mid, conv_out, first, middle, middle_back, last):
+    channels = conv_mid.shape[0]
+    three = 3 * channels
+    tap_ids = lax.broadcasted_iota(jnp.int32, (18, 72), 0)
+    lane_ids = lax.broadcasted_iota(jnp.int32, (18, 72), 1)
+    table = jnp.where(lane_ids == tap_ids // 2 * 8 + lax.rem(tap_ids, 2), 1.0, 0.0)
+    top = exact_spread(conv_in[...], table.astype(jnp.bfloat16))
+    blank = jnp.zeros((1, channels), jnp.float32)
+    taps = [conv_out[:, t * channels : t * channels + channels] for t in range(9)]
+    flips = jnp.concatenate(taps[::-1] + [blank] * 7, 0)
+    tap_ids = lax.broadcasted_iota(jnp.int32, (16, 72), 0)
+    lane_ids = lax.broadcasted_iota(jnp.int32, (16, 72), 1)
+    table = jnp.where((lane_ids == tap_ids * 8 + 2) & (tap_ids < 9), 1.0, 0.0)
+    bottom = exact_spread(flips.T, table.astype(jnp.bfloat16))
+    first[...] = stacked_halves(jnp.concatenate([top, bottom], 0))
+    mid = conv_mid[...]
+    middle[...] = stacked_halves(
+        jnp.concatenate([mid[:, d * three : d * three + three] for d in range(3)], 0)
+    )
+    turned = mid.T
+    middle_back[...] = stacked_halves(
+        jnp.concatenate(
+            [
+                jnp.concatenate(
+                    [
+                        turned[(d * 3 + a) * channels : (d * 3 + a) * channels + channels]
+                        for a in range(3)
+                    ],
+                    1,
+                )
+                for d in range(3)
+            ],
+            0,
+        )
+    )
+    order = []
+    for a in range(3):
+        order += [taps[d * 3 + a] for d in range(3)] + [blank] * 5
+    last[...] = stacked_halves(jnp.concatenate(order + [blank] * 8, 0))
+
+
+def network_stage(
+    width, layers, first, middle, middle_back, last, new_velocity, sums,
+    patch, near_high, near_low, far_high, far_low, down_high, down_low, taps, slope_one, hidden,
+    slope_two, last_taps, update, back,
+):
+    length = layers.shape[1]
+    channels = hidden.shape[0]
+    three = 3 * channels
+    rows, piece = new_velocity.shape
+    shifts = [down * width + across for down in (-1, 0, 1) for across in (-1, 0, 1)]
+    pieces = length // chunk
+    flat = ((1,), (0,))
+    over = ((1,), (1,))
+
+    def moved(values, shift):
+        return pltpu.roll(values, shift % length, 1)
+
+    for tap, shift in enumerate(shifts):
+        patch[tap * 8 : tap * 8 + 8] = moved(layers[...], -shift)
+
+    def each(body, init=0):
+        def step(index, carry):
+            return body(pl.ds(pl.multiple_of(index * chunk, chunk), chunk), carry)
+
+        return lax.fori_loop(0, pieces, step, init)
+
+    def squash(values):
+        return 1.0 / (1.0 + jnp.exp(-values))
+
+    def bend(values, squashed):
+        return squashed * (1.0 + values * (1.0 - squashed))
+
+    def open_layer(at, carry):
+        high, low = halves(patch[:, at])
+        both = dot_split(first[...], high, low, flat)
+        inside = layers[4:5, at] > 0.5
+        owned = layers[5:6, at] > 0.5
+        before = both[:channels]
+        squashed = squash(before)
+        slope_one[:, at] = jnp.where(owned, bend(before, squashed), 0.0)
+        hidden[:, at] = jnp.where(inside, before * squashed, 0.0)
+        slope_two[:, at] = both[channels:]
+        return carry
+
+    each(open_layer)
+
+    def fan(source, unit, high_ref, low_ref):
+        for group in range(channels // 16):
+            values = source(group)
+            for index, way in enumerate((-1, 0, 1)):
+                high, low = halves(moved(values, way * unit))
+                start = index * channels + group * 16
+                high_ref[start : start + 16] = high
+                low_ref[start : start + 16] = low
+
+    def fold(unit, target):
+        for group in range(channels // 8):
+            at = slice(group * 8, group * 8 + 8)
+            target[at] = (
+                taps[channels + group * 8 : channels + group * 8 + 8]
+                + moved(taps[at], -unit)
+                + moved(taps[2 * channels + group * 8 : 2 * channels + group * 8 + 8], unit)
+            )
+
+    fan(lambda group: hidden[group * 16 : group * 16 + 16], -1, near_high, near_low)
+
+    def middle_layer(at, carry):
+        taps[:, at] = dot_split(middle[...], near_high[:, at], near_low[:, at], flat)
+        return carry
+
+    each(middle_layer)
+    fold(-width, hidden)
+
+    def second_layer(at, carry):
+        before = hidden[:, at]
+        inside = layers[4:5, at] > 0.5
+        squashed = squash(before)
+        after = jnp.where(inside, before * squashed, 0.0)
+        hidden[:, at] = after
+        slope_two[:, at] = jnp.where(inside, slope_two[:, at] * bend(before, squashed), 0.0)
+        high, low = halves(after)
+        last_taps[:, at] = dot_split(last[...], high, low, flat)[0:24]
+        return carry
+
+    each(second_layer)
+    owned = layers[5:6] > 0.5
+    fan(
+        lambda group: jnp.where(owned, slope_two[group * 16 : group * 16 + 16], 0.0),
+        width, down_high, down_low,
+    )
+    fan(lambda group: slope_two[group * 16 : group * 16 + 16], 1, far_high, far_low)
+    mixed = last_taps[8:16] + moved(last_taps[0:8], 1) + moved(last_taps[16:24], -1)
+    update[...] = jnp.broadcast_to(
+        layers[0:1] + mixed[1:2] + moved(mixed, width)[0:1] + moved(mixed, -width)[2:3],
+        update.shape,
+    )
+
+    def back_layer(at, carry):
+        taps[:, at] = dot_split(middle_back[...], far_high[:, at], far_low[:, at], flat)
+        left = jnp.concatenate([down_high[:, at], down_low[:, at]], 0)
+        return carry + dot_split(left, near_high[:, at], near_low[:, at], over)
+
+    sums[0:three, 0:three] = each(back_layer, jnp.zeros((three, three), jnp.float32))
+    for row in range(rows):
+        start = (row + 3) * width + 3
+        tile = start // 128 * 128
+        segment = update[:, tile : tile + 256]
+        new_velocity[row : row + 1, :] = pltpu.roll(segment, 256 - start % 128, 1)[0:1, :piece]
+    fold(width, back)
+
+    def first_grads(at, carry):
+        fall = back[:, at] * slope_one[:, at]
+        high, low = halves(patch[:, at])
+        left = stacked_halves(jnp.concatenate([fall, hidden[:, at]], 0))
+        return carry + dot_split(left, high, low, over)
+
+    outer = each(first_grads, jnp.zeros((2 * channels, 72), jnp.float32))
+    tap_ids = lax.broadcasted_iota(jnp.int32, (72, 128), 0)
+    lane_ids = lax.broadcasted_iota(jnp.int32, (72, 128), 1)
+    which = lax.rem(tap_ids, 8)
+    table_in = jnp.where((which < 2) & (lane_ids == tap_ids // 8 * 2 + which), 1.0, 0.0)
+    table_out = jnp.where((which == 3) & (lane_ids == 26 - tap_ids // 8), 1.0, 0.0)
+    sums[three:] = exact_spread(outer[:channels], table_in.astype(jnp.bfloat16)) + exact_spread(
+        outer[channels:], table_out.astype(jnp.bfloat16)
+    )
+
+
+def whole_kernel(
     sizes,
     velocity, wave_now, wave_before, adjoint_last, adjoint_after, wavelet, source_col, rec_first,
-    rec_last, rec_count, observed, cotangent,
-    out_image, out_cot, out_speed,
+    rec_last, rec_count, observed, cotangent, conv_in, conv_mid, conv_out,
+    new_velocity, grad_in, grad_mid, grad_out,
+    out_image, windows, layers, sums, sum_slots, band_sums, final_sums, first_weights, middle_weights,
+    back_weights, last_weights, patch, near_high, near_low, far_high, far_low, down_high, down_low,
+    taps, slope_one, hidden, slope_two, last_taps, update, back,
     arrived, speed_all, speed_sq, small, observed_cols, source_mask, receiver_mask,
     down_weights, across_weights, split, forward, adjoint, image, parts, part_slots, cross, cross_slots, held, lines, line_slots,
     strips, cot_all,
     own_sem, edge_send, edge_recv, speed_send, speed_recv, plane_send, plane_recv, field_send, field_recv, small_send,
-    small_recv, cot_send, cot_recv, part_send, part_recv, cross_send, cross_recv, line_send, line_recv,
+    small_recv, cot_send, cot_recv, part_send, part_recv, cross_send, cross_recv, line_send, line_recv, sum_send, sum_recv, band_send, band_recv,
+    last_send, last_recv,
 ):
     shots, nets, bands = sizes
     mine_shots, rows, breadth = wave_now.shape
@@ -786,6 +985,9 @@
     observed_cols[...] = (spread[:steps] + spread[steps : 2 * steps]) + spread[2 * steps : 3 * steps]
     receiver_mask[...] = jnp.where(inside & (level == receiver_depth), spread[3 * steps : 3 * steps + 8], 0.0)
 
+    network_weights(
+        conv_in, conv_mid, conv_out, first_weights, middle_weights, back_weights, last_weights
+    )
     for step in range(1, groups):
         speed_plane_in(step).wait_recv()
     for tile in range(tiles):
@@ -978,12 +1180,40 @@
     def _():
         line_slots[0] = lines[band]
 
-    out_speed[...] = speed_all[
+    pl.when(group > 0)(lambda: cot_right().wait_recv())
+    pl.when(group < groups - 1)(lambda: cot_left().wait_recv())
+    reach_rows = rows + 16
+    window_rows = lax.broadcasted_iota(jnp.int32, (reach_rows, 3 * piece), 0)
+    window_cols = lax.broadcasted_iota(jnp.int32, (reach_rows, 3 * piece), 1)
+    near = (window_cols >= piece - 3) & (window_cols < 2 * piece + 3)
+    mine = (
+        (window_cols >= piece) & (window_cols < 2 * piece)
+        & (window_rows >= 8) & (window_rows < rows + 8)
+    )
+    real_row = band * rows - 8 + window_rows
+    real_col = group * piece - piece + window_cols
+    real = (
+        near & (real_row >= 0) & (real_row < total_rows) & (real_col >= 0) & (real_col < breadth)
+    )
+
+    def widen(field, values):
+        for tile in range(3 * piece // 128):
+            for part in range(reach_rows // 8):
+                windows[tile, pl.ds(part * 64 + field, 8, stride=8), :] = values[
+                    part * 8 : part * 8 + 8, tile * 128 : tile * 128 + 128
+                ]
+
+    speeds = speed_all[
         pl.ds(pl.multiple_of(band * rows, 8), rows + 16), pl.ds(column, 3 * piece)
     ]
-    pl.when(group > 0)(lambda: cot_right().wait_recv())
-    pl.when(group < groups - 1)(lambda: cot_left().wait_recv())
-    out_cot[...] = cot_all[...]
+    widen(0, jnp.where(near, speeds, 0.0))
+    widen(2, jnp.where(near, cot_all[...], 0.0))
+    widen(3, jnp.where(mine, cot_all[...], 0.0))
+    widen(4, real.astype(f32))
+    widen(5, mine.astype(f32))
+    widen(6, jnp.zeros((reach_rows, 3 * piece), f32))
+    widen(7, jnp.zeros((reach_rows, 3 * piece), f32))
+    layers[...] = jnp.zeros(layers.shape, f32)
     out_image[...] = jnp.zeros(out_image.shape, f32)
     strips[...] = jnp.zeros(strips.shape, f32)
     pl.when(swapped)(lambda: line_in(0).wait_recv())
@@ -994,9 +1224,100 @@
     out_image[:, piece : 2 * piece] = final[0 : rows + 16]
     strips[8 : 8 + total_rows, 0:16] = final[rows + 16 :].T
     around = pl.ds(pl.multiple_of(band * rows, 8), rows + 16)
-    near = strips[around, :]
-    out_image[:, piece - 8 : piece] = near[:, 0:8]
-    out_image[:, 2 * piece : 2 * piece + 8] = near[:, 8:16]
+    beside = strips[around, :]
+    out_image[:, piece - 8 : piece] = beside[:, 0:8]
+    out_image[:, 2 * piece : 2 * piece + 8] = beside[:, 8:16]
+    widen(1, jnp.where(near, out_image[...] / float(steps * mine_shots * groups) ** 0.5, 0.0))
+    reach_cols = piece + 6
+    for row in range(rows + 6):
+        line = jnp.concatenate(
+            [windows[tile, (row + 5) * 8 : (row + 5) * 8 + 8, :] for tile in range(3 * piece // 128)], 1
+        )
+        start = row * reach_cols
+        inset = start % 128
+        span = -(-(inset + reach_cols) // 128) * 128
+        first_lane = start - inset
+        line = pltpu.roll(line, (inset - (piece - 3)) % (3 * piece), 1)[:, :span]
+        layers[:, first_lane : first_lane + span] = layers[:, first_lane : first_lane + span] + line
+    network_stage(
+        reach_cols, layers, first_weights, middle_weights, back_weights, last_weights, new_velocity,
+        sums, patch, near_high, near_low, far_high, far_low, down_high, down_low, taps, slope_one,
+        hidden, slope_two, last_taps, update, back,
+    )
+    share = sums.shape[0] // groups
+
+    def share_of(index):
+        return pl.ds(pl.multiple_of(index * share, 8), share)
+
+    def sum_out(step):
+        peer = lax.rem(group + step, groups)
+        return remote(
+            sums.at[share_of(peer)], sum_slots.at[groups - step], sum_send.at[step],
+            sum_recv.at[groups - step], member(peer),
+        )
+
+    def sum_in(step):
+        peer = lax.rem(group + step, groups)
+        return remote(
+            sums.at[share_of(peer)], sum_slots.at[step], sum_send.at[step], sum_recv.at[step],
+            member(peer),
+        )
+
+    def band_out(step):
+        return remote(
+            band_sums.at[0], band_sums.at[bands - step], band_send.at[step],
+            band_recv.at[bands - step], {"band": lax.rem(band + step, bands)},
+        )
+
+    def band_in(step):
+        return remote(
+            band_sums.at[0], band_sums.at[step], band_send.at[step], band_recv.at[step],
+            {"band": lax.rem(band + step, bands)},
+        )
+
+    def last_out(step):
+        return remote(
+            final_sums.at[share_of(group)], final_sums.at[share_of(group)], last_send.at[step],
+            last_recv.at[groups - step], member(lax.rem(group + step, groups)),
+        )
+
+    def last_in(step):
+        peer = lax.rem(group + step, groups)
+        return remote(
+            final_sums.at[share_of(peer)], final_sums.at[share_of(peer)], last_send.at[step],
+            last_recv.at[step], member(peer),
+        )
+
+    for step in range(1, groups):
+        sum_out(step).start()
+    sum_slots[0] = sums[share_of(group)]
+    for step in range(1, groups):
+        sum_in(step).wait_recv()
+    running = sum_slots[lax.rem(groups - group, groups)]
+    for index in range(1, groups):
+        running = running + sum_slots[lax.rem(index + groups - group, groups)]
+    band_sums[0] = running
+    for step in range(1, bands):
+        band_out(step).start()
+    for step in range(1, bands):
+        band_in(step).wait_recv()
+    running = band_sums[lax.rem(bands - band, bands)]
+    for index in range(1, bands):
+        running = running + band_sums[lax.rem(index + bands - band, bands)]
+    final_sums[share_of(group)] = running
+    for step in range(1, groups):
+        last_out(step).start()
+    for step in range(1, groups):
+        last_in(step).wait_recv()
+    channels = conv_mid.shape[0]
+    three = 3 * channels
+    grad_mid[...] = jnp.concatenate(
+        [final_sums[d * channels : d * channels + channels, 0:three] for d in range(3)], 1
+    )
+    small_sums = final_sums[three : three + channels, :]
+    grad_in[...] = small_sums[:, 0:18]
+    turned_sums = small_sums.T
+    grad_out[...] = jnp.concatenate([turned_sums[18 + t : 19 + t] for t in range(9)], 1)
 
     for step in range(1, bands):
         speed_line(step).wait_send()
@@ -1018,11 +1339,16 @@
     for step in range(1, bands):
         line_out(step).wait_send()
     pl.when(swapped)(lambda: line_out(0).wait_send())
-
-
-def waves_and_pieces(
+    for step in range(1, groups):
+        sum_out(step).wait_send()
+        last_out(step).wait_send()
+    for step in range(1, bands):
+        band_out(step).wait_send()
+
+
+def whole_iteration(
     velocity, wave_now, wave_before, adjoint_last, adjoint_after, wavelet, source_col, rec_first,
-    rec_last, rec_count, observed, cotangent,
+    rec_last, rec_count, observed, cotangent, conv_in, conv_mid, conv_out,
 ):
     shots = lax.axis_size("shot")
     nets = lax.axis_size("net")
@@ -1036,17 +1362,43 @@
     groups = shots * nets
     half = breadth // sides
     width = half + 8 * steps
+    channels = conv_mid.shape[0]
+    length = -(-(rows + 6) * (piece + 6) // chunk) * chunk
+    half_type = jnp.bfloat16
     f32 = jnp.float32
     dma = pltpu.SemaphoreType.DMA
     anywhere = [pl.BlockSpec(memory_space=pl.ANY)]
     scalars = [pl.BlockSpec(memory_space=pltpu.SMEM)]
     return pl.pallas_call(
-        functools.partial(wave_kernel, (shots, nets, bands)),
-        name="waves",
-        out_shape=[jax.ShapeDtypeStruct((rows + 16, 3 * piece), f32)] * 3,
-        in_specs=anywhere * 5 + scalars * 5 + vmem(2),
-        out_specs=vmem(3),
+        functools.partial(whole_kernel, (shots, nets, bands)),
+        name="whole",
+        out_shape=[
+            jax.ShapeDtypeStruct(shape, f32)
+            for shape in (cotangent.shape, conv_in.shape, conv_mid.shape, conv_out.shape)
+        ],
+        in_specs=anywhere * 5 + scalars * 5 + vmem(5),
+        out_specs=vmem(4),
         scratch_shapes=[
+            pltpu.VMEM((rows + 16, 3 * piece), f32),
+            pltpu.VMEM((3 * piece // 128, (rows + 16) * 8, 128), f32),
+            pltpu.VMEM((8, length), f32),
+            pltpu.VMEM((4 * channels, 128), f32),
+            pltpu.VMEM((groups, 4 * channels // groups, 128), f32),
+            pltpu.VMEM((bands, 4 * channels // groups, 128), f32),
+            pltpu.VMEM((4 * channels, 128), f32),
+            pltpu.VMEM((4 * channels, 72), half_type),
+            pltpu.VMEM((6 * channels, 3 * channels), half_type),
+            pltpu.VMEM((6 * channels, 3 * channels), half_type),
+            pltpu.VMEM((64, channels), half_type),
+            pltpu.VMEM((72, length), f32),
+            *[pltpu.VMEM((3 * channels, length), half_type)] * 6,
+            pltpu.VMEM((3 * channels, length), f32),
+            pltpu.VMEM((channels, length), f32),
+            pltpu.VMEM((channels, length), f32),
+            pltpu.VMEM((channels, length), f32),
+            pltpu.VMEM((24, length), f32),
+            pltpu.VMEM((8, length), f32),
+            pltpu.VMEM((channels, length), f32),
             pltpu.VMEM((4, total_rows, width), f32),
             pltpu.VMEM((total_rows + 16, breadth + 2 * piece), f32),
             pltpu.VMEM((total_rows, width), f32),
@@ -1088,17 +1440,23 @@
             dma((2, pieces)),
             dma((bands,)),
             dma((bands,)),
+            dma((groups,)),
+            dma((groups,)),
+            dma((bands,)),
+            dma((bands,)),
+            dma((groups,)),
+            dma((groups,)),
         ],
         compiler_params=pltpu.CompilerParams(
             collective_id=3, has_side_effects=True, vmem_limit_bytes=56 * 1024 * 1024
         ),
     )(
         velocity, wave_now, wave_before, adjoint_last, adjoint_after, wavelet, source_col,
-        rec_first, rec_last, rec_count, observed, cotangent,
-    )
-
-
-def fits_whole_columns(wave_now, observed, cotangent):
+        rec_first, rec_last, rec_count, observed, cotangent, conv_in, conv_mid, conv_out,
+    )
+
+
+def fits_whole_columns(wave_now, observed, cotangent, conv_mid):
     mine_shots, rows, breadth = wave_now.shape
     shots = lax.axis_size("shot")
     nets = lax.axis_size("net")
@@ -1113,6 +1471,8 @@
         and cotangent.shape[1] == 128
         and 8 * steps == 128
         and slots == 128
+        and conv_mid.shape[0] == 32
+        and 4 * conv_mid.shape[0] % (8 * shots * nets) == 0
         and breadth * slots < 2**24
     )
 
@@ -1174,13 +1534,12 @@
     slots = observed.shape[2]
     piece_cols = cotangent.shape[1]
     group_count = shot_here * lax.axis_size(("shot", "net"))
-    if fits_whole_columns(wave_now, observed, cotangent):
-        image, cot, around = waves_and_pieces(
-            velocity, wave_now, wave_before, adjoint_last, adjoint_after, wavelet, source_col,
-            rec_first, rec_last, rec_count, observed, cotangent,
-        )
-        return update_model(
-            around, image, cot, velocity, cotangent, num_steps, group_count, conv_in, conv_mid, conv_out
+    if fits_whole_columns(wave_now, observed, cotangent, conv_mid):
+        return tuple(
+            whole_iteration(
+                velocity, wave_now, wave_before, adjoint_last, adjoint_after, wavelet, source_col,
+                rec_first, rec_last, rec_count, observed, cotangent, conv_in, conv_mid, conv_out,
+            )
         )
     first_row = lax.axis_index("band") * rows_here
     speed_sq = (velocity * speed_factor) ** 2

time: 99.8 us -> 87 us (0.87)
  Pallas kernels: 86.6 us -> 80.5 us
  local copies, waits for them, and re-layouts: 9.99 us -> 5.36 us
  other arithmetic: 1.73 us -> 0 us
    pallas_call x3 -> x1, Pallas kernels: 86.6 us -> 80.5 us  [whole_iteration(): pl.pallas_call(functools.partial(whole_kernel, (shots, nets, bands)), nam...]
    slice x9 -> x0, local copies, waits for them, and re-layouts: 3.32 us -> none  [the longest x1 0.99 us: update_model(): around = around[5:-5, piece - 3:2 * piece + 3]]
    reshape x10 -> x0, local copies, waits for them, and re-layouts: 1.67 us -> none  [the longest x1 0.64 us: update_model(): spare.T.reshape(1, 9 * channels)]
    pallas_call x0 -> x1, local copies, waits for them, and re-layouts: none -> 1.41 us  [whole_iteration(): pl.pallas_call(functools.partial(whole_kernel, (shots, nets, bands)), nam...]
    another operation x7 -> x0, local copies, waits for them, and re-layouts: 1.04 us -> none  [the longest x6 0.9 us: update_model(): jnp.stack([around, scaled, cot, cot * owned, inside.astype(jnp.float32),...]
    unnamed x17 -> x8, local copies, waits for them, and re-layouts: 3.38 us -> 3.95 us
where the time goes in v3:
time: 87 us; the launch traced here: 86.6 us
  Pallas kernels  80.5 us (93%)
  local copies, waits for them, and re-layouts  5.36 us (6%)
    pallas_call x1, Pallas kernels, whole_iteration(): pl.pallas_call(functools.partial(whole_kernel, (shots, nets, bands)), nam...  80.5 us
    unnamed x8, local copies, waits for them, and re-layouts  3.95 us

profile of v3, /device:TPU:0, one launch (start us, length us, event | category | flops | bytes accessed | tf_op | source)
XLA Modules:
  0.0 86.6 jit_solution(14009783847689486557)
XLA Ops:
  0.6 1.4 %copy.19.conv_in = f32[32,18]{1,0:T(8,128)} copy(f32[32,18]{0,1:T(8,128)} %param.26) | data formatting | bytes 4608 | tf_op args[11]
  2.0 80.5 %whole.1 = (f32[32,128]{1,0:T(8,128)}, f32[32,18]{1,0:T(8,128)}, f32[32,288]{1,0:T(8,128)}, f32[1,288]{1,0:T(1,128)}) custom-call(f32[32,1024]{1,0:T(8,128)} %velocity.1, f32[2,32,1024]{2,1,0:T(8,128)} %wave_now.1, f32[2,32,1024]{2,1,0:T(8,128)} %wave_before.1, f32[2,32,1024]{2,1,0:T(8,128)} %adjoint_last.1, f32[2,32,1024]{2,1,0:T(8,128)} %adjoint_after.1, ...), custom_call_target="tpu_custom_call" | custom-call | tf_op jit(solution)/shard_map/whole/pallas_call | solution.py:1372
  82.6 0.0 copy-start
  82.6 1.4 %copy.20 = f32[32,18]{0,1:T(8,128)} copy(f32[32,18]{1,0:T(8,128)} %get-tuple-element.5) | data formatting | bytes 4608 | tf_op jit(solution)/shard_map/whole/pallas_call | solution.py:1372
  84.0 1.3 %copy.24 = f32[32,128]{1,0:T(8,128)} copy(f32[32,128]{1,0:T(8,128)} %get-tuple-element.12) | data formatting | bytes 32768
  85.3 0.0 copy-done
  85.3 0.0 copy-start.1
  85.3 0.6 copy.25
  85.9 0.0 copy-done.1
  86.0 0.6 copy.26
Async XLA Ops:
  82.6 2.7 %copy-start = (f32[32,288]{1,0:T(8,128)S(1)}, f32[32,288]{1,0:T(8,128)}, u32[]{:S(2)}) copy-start(f32[32,288]{1,0:T(8,128)} %get-tuple-element.14) | copy-start | bytes 110596
  85.3 0.7 copy-start.1

commit v4 on v3

--- a/solution.py
+++ b/solution.py
@@ -521,7 +521,7 @@
     tap_ids = lax.broadcasted_iota(jnp.int32, (18, 72), 0)
     lane_ids = lax.broadcasted_iota(jnp.int32, (18, 72), 1)
     table = jnp.where(lane_ids == tap_ids // 2 * 8 + lax.rem(tap_ids, 2), 1.0, 0.0)
-    top = exact_spread(conv_in[...], table.astype(jnp.bfloat16))
+    top = exact_spread(conv_in[...].T, table.astype(jnp.bfloat16))
     blank = jnp.zeros((1, channels), jnp.float32)
     taps = [conv_out[:, t * channels : t * channels + channels] for t in range(9)]
     flips = jnp.concatenate(taps[::-1] + [blank] * 7, 0)
@@ -562,6 +562,7 @@
     slope_two, last_taps, update, back,
 ):
     length = layers.shape[1]
+    chunk = length
     channels = hidden.shape[0]
     three = 3 * channels
     rows, piece = new_velocity.shape
@@ -576,11 +577,10 @@
     for tap, shift in enumerate(shifts):
         patch[tap * 8 : tap * 8 + 8] = moved(layers[...], -shift)
 
-    def each(body, init=0):
-        def step(index, carry):
-            return body(pl.ds(pl.multiple_of(index * chunk, chunk), chunk), carry)
-
-        return lax.fori_loop(0, pieces, step, init)
+    def each(body, carry=0):
+        for index in range(pieces):
+            carry = body(slice(index * chunk, index * chunk + chunk), carry)
+        return carry
 
     def squash(values):
         return 1.0 / (1.0 + jnp.exp(-values))
@@ -687,12 +687,12 @@
     sizes,
     velocity, wave_now, wave_before, adjoint_last, adjoint_after, wavelet, source_col, rec_first,
     rec_last, rec_count, observed, cotangent, conv_in, conv_mid, conv_out,
-    new_velocity, grad_in, grad_mid, grad_out,
+    new_velocity, totals,
     out_image, windows, layers, sums, sum_slots, band_sums, final_sums, first_weights, middle_weights,
     back_weights, last_weights, patch, near_high, near_low, far_high, far_low, down_high, down_low,
     taps, slope_one, hidden, slope_two, last_taps, update, back,
-    arrived, speed_all, speed_sq, small, observed_cols, source_mask, receiver_mask,
-    down_weights, across_weights, split, forward, adjoint, image, parts, part_slots, cross, cross_slots, held, lines, line_slots,
+    arrived, speed_all, speed_sq, small, observed_cols, pulse_cols, source_mask, receiver_mask,
+    down_weights, across_weights, rims, split, forward, adjoint, image, parts, part_slots, cross, cross_slots, held, lines, line_slots,
     strips, cot_all,
     own_sem, edge_send, edge_recv, speed_send, speed_recv, plane_send, plane_recv, field_send, field_recv, small_send,
     small_recv, cot_send, cot_recv, part_send, part_recv, cross_send, cross_recv, line_send, line_recv, sum_send, sum_recv, band_send, band_recv,
@@ -939,11 +939,15 @@
         jnp.where(down_gap < total_rows, down_gap, down_gap - total_rows)
         - lax.broadcasted_iota(jnp.int32, (total_rows, 2 * total_rows), 0)
     )
-    across_gap = lax.broadcasted_iota(jnp.int32, (768, 128), 0)
+    far = lax.broadcasted_iota(jnp.int32, (512, 128), 0)
+    lane = lax.rem(far, 128)
     across_gap = jnp.abs(
-        jnp.where(across_gap < 384, across_gap, across_gap - 384) - 128
-        - lax.broadcasted_iota(jnp.int32, (768, 128), 1)
-    )
+        jnp.where(far < 256, lane, jnp.where(lane < 64, lane + 128, lane - 128))
+        - lax.broadcasted_iota(jnp.int32, (512, 128), 1)
+    )
+    rim_lanes = lax.broadcasted_iota(jnp.int32, (16, 128), 1)
+    rims[0] = jnp.where(rim_lanes >= 64, 1.0, 0.0).astype(jnp.bfloat16)
+    rims[1] = jnp.where(rim_lanes < 64, 1.0, 0.0).astype(jnp.bfloat16)
 
     def banded(gap):
         matrix = jnp.zeros(gap.shape, f32)
@@ -982,8 +986,12 @@
     spread = lax.dot_general(
         stacked, chosen, (((1,), (0,)), ((), ())), preferred_element_type=f32
     )
-    observed_cols[...] = (spread[:steps] + spread[steps : 2 * steps]) + spread[2 * steps : 3 * steps]
+    recorded = (spread[:steps] + spread[steps : 2 * steps]) + spread[2 * steps : 3 * steps]
     receiver_mask[...] = jnp.where(inside & (level == receiver_depth), spread[3 * steps : 3 * steps + 8], 0.0)
+    for step in range(steps):
+        observed_cols[step] = receiver_mask[...] * jnp.broadcast_to(recorded[step : step + 1], (8, width))
+        amount = jnp.broadcast_to(small[0:1, step : step + 1], (8, width))
+        pulse_cols[step] = source_mask[...] * amount
 
     network_weights(
         conv_in, conv_mid, conv_out, first_weights, middle_weights, back_weights, last_weights
@@ -1003,19 +1011,21 @@
             high = value.astype(jnp.bfloat16)
             split[0:total_rows, at] = high
             split[total_rows:, at] = (value - high.astype(f32)).astype(jnp.bfloat16)
-        down = lax.dot_general(
-            down_weights[...], split[...], (((1,), (0,)), ((), ())), preferred_element_type=f32
-        )
+        left_rim = jnp.broadcast_to(rims[0, 0:1], (total_rows, 128))
+        right_rim = jnp.broadcast_to(rims[1, 0:1], (total_rows, 128))
         rows_of = []
         for tile in range(tiles):
-            near = [(tile + tiles + shift) % tiles for shift in (-1, 0, 1)]
+            parts_of = [
+                [
+                    split[part * total_rows : part * total_rows + total_rows, t * 128 : t * 128 + 128]
+                    for t in ((tile + tiles - 1) % tiles, tile, (tile + 1) % tiles)
+                ]
+                for part in range(2)
+            ]
             rows_of.append(
                 jnp.concatenate(
-                    [
-                        split[part * total_rows : part * total_rows + total_rows, t * 128 : t * 128 + 128]
-                        for part in range(2)
-                        for t in near
-                    ],
+                    [middle for _, middle, _ in parts_of]
+                    + [before * left_rim + after * right_rim for before, _, after in parts_of],
                     1,
                 )
             )
@@ -1023,14 +1033,21 @@
             jnp.concatenate(rows_of, 0), across_weights[...], (((1,), (0,)), ((), ())),
             preferred_element_type=f32,
         )
-        for tile in range(tiles):
-            at = slice(tile * 128, tile * 128 + 128)
-            value = ref[now, :, at]
-            total = (
-                weights[0] * value + down[:, at]
-                + across[tile * total_rows : tile * total_rows + total_rows]
+        for pair_start in range(0, tiles, 2):
+            pair_tiles = range(pair_start, min(pair_start + 2, tiles))
+            down = lax.dot_general(
+                down_weights[...], split[:, pair_start * 128 : pair_tiles[-1] * 128 + 128],
+                (((1,), (0,)), ((), ())), preferred_element_type=f32,
             )
-            finish(at, 2.0 * value - ref[before, :, at] + speed_sq[:, at] * total)
+            for tile in pair_tiles:
+                at = slice(tile * 128, tile * 128 + 128)
+                value = ref[now, :, at]
+                total = (
+                    weights[0] * value
+                    + down[:, (tile - pair_start) * 128 : (tile - pair_start) * 128 + 128]
+                    + across[tile * total_rows : tile * total_rows + total_rows]
+                )
+                finish(at, 2.0 * value - ref[before, :, at] + speed_sq[:, at] * total)
 
     def settle(index, ref, at):
         edge(index).wait_recv()
@@ -1044,12 +1061,8 @@
     settle(0, forward, 1)
     settle(1, forward, 0)
 
-    pulses = small[0:1]
-    pulse_ids = lax.broadcasted_iota(jnp.int32, (1, 128), 1)
-
     def forward_step(index, carry):
-        amount = jnp.sum(jnp.where(pulse_ids == index, pulses, 0.0), axis=1, keepdims=True)
-        added = source_mask[...] * amount
+        added = pulse_cols[index]
 
         def finish(at, fresh):
             forward[index + 2, :, at] = jnp.concatenate([fresh[0:8] + added[:, at], fresh[8:]], 0)
@@ -1058,6 +1071,19 @@
         return carry
 
     lax.fori_loop(0, steps, forward_step, 0)
+    for step in range(1, bands):
+        speed_line(step).wait_send()
+    pl.when(band < bands - 1)(lambda: cot_down().wait_send())
+    pl.when(band > 0)(lambda: cot_up().wait_send())
+    for turn in range(1, sides):
+        pl.when(is_mine)(lambda turn=turn: small_out(turn).wait_send())
+    for index in (0, 1):
+        each_field_out(index, lambda copy: copy.wait_send())
+        edge(index).wait_send()
+    for step in range(1, groups):
+        speed_plane(step).wait_send()
+    pl.when(group < groups - 1)(lambda: cot_right().wait_send())
+    pl.when(group > 0)(lambda: cot_left().wait_send())
 
     for index in (2, 3):
         each_field_in(index)
@@ -1070,9 +1096,7 @@
         moment = steps - 1 - index
         now = lax.rem(index, 2)
         later = 1 - now
-        added = receiver_mask[...] * (
-            forward[moment + 2, 0:8] - observed_cols[pl.ds(moment, 1), :]
-        )
+        added = receiver_mask[...] * forward[moment + 2, 0:8] - observed_cols[moment]
 
         def finish(at, fresh):
             fresh = jnp.concatenate([fresh[0:8] + added[:, at], fresh[8:]], 0)
@@ -1175,6 +1199,13 @@
     for step in range(1, bands):
         line_out(step).start()
     pl.when(swapped)(lambda: line_out(0).start())
+    for index in (2, 3):
+        each_field_out(index, lambda copy: copy.wait_send())
+        edge(index).wait_send()
+    pl.when(has_right)(lambda: cross_out(1).wait_send())
+    pl.when(has_left)(lambda: cross_out(0).wait_send())
+    for step in range(1, pieces):
+        part_out(step).wait_send()
 
     @pl.when(jnp.logical_not(swapped))
     def _():
@@ -1300,6 +1331,11 @@
     for step in range(1, bands):
         band_out(step).start()
     for step in range(1, bands):
+        line_out(step).wait_send()
+    pl.when(swapped)(lambda: line_out(0).wait_send())
+    for step in range(1, groups):
+        sum_out(step).wait_send()
+    for step in range(1, bands):
         band_in(step).wait_recv()
     running = band_sums[lax.rem(bands - band, bands)]
     for index in range(1, bands):
@@ -1307,43 +1343,13 @@
     final_sums[share_of(group)] = running
     for step in range(1, groups):
         last_out(step).start()
+    for step in range(1, bands):
+        band_out(step).wait_send()
     for step in range(1, groups):
         last_in(step).wait_recv()
-    channels = conv_mid.shape[0]
-    three = 3 * channels
-    grad_mid[...] = jnp.concatenate(
-        [final_sums[d * channels : d * channels + channels, 0:three] for d in range(3)], 1
-    )
-    small_sums = final_sums[three : three + channels, :]
-    grad_in[...] = small_sums[:, 0:18]
-    turned_sums = small_sums.T
-    grad_out[...] = jnp.concatenate([turned_sums[18 + t : 19 + t] for t in range(9)], 1)
-
-    for step in range(1, bands):
-        speed_line(step).wait_send()
-    pl.when(band < bands - 1)(lambda: cot_down().wait_send())
-    pl.when(band > 0)(lambda: cot_up().wait_send())
-    for turn in range(1, sides):
-        pl.when(is_mine)(lambda turn=turn: small_out(turn).wait_send())
-    for index in range(4):
-        each_field_out(index, lambda copy: copy.wait_send())
-        edge(index).wait_send()
+    totals[...] = final_sums[...]
     for step in range(1, groups):
-        speed_plane(step).wait_send()
-    pl.when(group < groups - 1)(lambda: cot_right().wait_send())
-    pl.when(group > 0)(lambda: cot_left().wait_send())
-    pl.when(has_right)(lambda: cross_out(1).wait_send())
-    pl.when(has_left)(lambda: cross_out(0).wait_send())
-    for step in range(1, pieces):
-        part_out(step).wait_send()
-    for step in range(1, bands):
-        line_out(step).wait_send()
-    pl.when(swapped)(lambda: line_out(0).wait_send())
-    for step in range(1, groups):
-        sum_out(step).wait_send()
         last_out(step).wait_send()
-    for step in range(1, bands):
-        band_out(step).wait_send()
 
 
 def whole_iteration(
@@ -1374,10 +1380,10 @@
         name="whole",
         out_shape=[
             jax.ShapeDtypeStruct(shape, f32)
-            for shape in (cotangent.shape, conv_in.shape, conv_mid.shape, conv_out.shape)
+            for shape in (cotangent.shape, (4 * channels, 128))
         ],
         in_specs=anywhere * 5 + scalars * 5 + vmem(5),
-        out_specs=vmem(4),
+        out_specs=vmem(2),
         scratch_shapes=[
             pltpu.VMEM((rows + 16, 3 * piece), f32),
             pltpu.VMEM((3 * piece // 128, (rows + 16) * 8, 128), f32),
@@ -1403,11 +1409,13 @@
             pltpu.VMEM((total_rows + 16, breadth + 2 * piece), f32),
             pltpu.VMEM((total_rows, width), f32),
             pltpu.VMEM((8 + steps, 128), f32),
-            pltpu.VMEM((steps, width), f32),
+            pltpu.VMEM((steps, 8, width), f32),
+            pltpu.VMEM((steps, 8, width), f32),
             pltpu.VMEM((8, width), f32),
             pltpu.VMEM((8, width), f32),
             pltpu.VMEM((total_rows, 2 * total_rows), jnp.bfloat16),
-            pltpu.VMEM((768, 128), jnp.bfloat16),
+            pltpu.VMEM((512, 128), jnp.bfloat16),
+            pltpu.VMEM((2, 16, 128), jnp.bfloat16),
             pltpu.VMEM((2 * total_rows, width), jnp.bfloat16),
             pltpu.VMEM((steps + 2, total_rows, width), f32),
             pltpu.VMEM((2, total_rows, width), f32),
@@ -1452,8 +1460,32 @@
         ),
     )(
         velocity, wave_now, wave_before, adjoint_last, adjoint_after, wavelet, source_col,
-        rec_first, rec_last, rec_count, observed, cotangent, conv_in, conv_mid, conv_out,
-    )
+        rec_first, rec_last, rec_count, observed, cotangent, conv_in.T, conv_mid, conv_out,
+    )
+
+
+def deliver_kernel(fresh, totals, new_velocity, grad_in, grad_mid, grad_out):
+    channels = grad_mid.shape[0]
+    three = 3 * channels
+    new_velocity[...] = fresh[...]
+    grad_mid[...] = jnp.concatenate(
+        [totals[d * channels : d * channels + channels, 0:three] for d in range(3)], 1
+    )
+    turned = totals[three:, :].T
+    grad_in[...] = turned[0:18]
+    grad_out[...] = jnp.concatenate([turned[18 + t : 19 + t] for t in range(9)], 1)
+
+
+def deliver(fresh, totals, conv_in, conv_mid, conv_out):
+    shapes = (fresh.shape, conv_in.shape[::-1], conv_mid.shape, conv_out.shape)
+    fresh, grad_in, grad_mid, grad_out = pl.pallas_call(
+        deliver_kernel,
+        name="deliver",
+        out_shape=[jax.ShapeDtypeStruct(shape, jnp.float32) for shape in shapes],
+        in_specs=vmem(2),
+        out_specs=vmem(4),
+    )(fresh, totals)
+    return fresh, grad_in.T, grad_mid, grad_out
 
 
 def fits_whole_columns(wave_now, observed, cotangent, conv_mid):
@@ -1535,12 +1567,11 @@
     piece_cols = cotangent.shape[1]
     group_count = shot_here * lax.axis_size(("shot", "net"))
     if fits_whole_columns(wave_now, observed, cotangent, conv_mid):
-        return tuple(
-            whole_iteration(
-                velocity, wave_now, wave_before, adjoint_last, adjoint_after, wavelet, source_col,
-                rec_first, rec_last, rec_count, observed, cotangent, conv_in, conv_mid, conv_out,
-            )
-        )
+        fresh, totals = whole_iteration(
+            velocity, wave_now, wave_before, adjoint_last, adjoint_after, wavelet, source_col,
+            rec_first, rec_last, rec_count, observed, cotangent, conv_in, conv_mid, conv_out,
+        )
+        return deliver(fresh, totals, conv_in, conv_mid, conv_out)
     first_row = lax.axis_index("band") * rows_here
     speed_sq = (velocity * speed_factor) ** 2
     columns = jnp.arange(breadth, dtype=jnp.int32)

time: 87 us -> 71.3 us (0.82)
  Pallas kernels: 80.5 us -> 70.4 us
  local copies, waits for them, and re-layouts: 5.36 us -> 0 us
    pallas_call x1, Pallas kernels: 80.5 us -> 68.8 us  [whole_iteration(): pl.pallas_call(functools.partial(whole_kernel, (shots, nets, bands)), nam...]
    unnamed x8 -> x0, local copies, waits for them, and re-layouts: 3.95 us -> none
    pallas_call x0 -> x1, Pallas kernels: none -> 1.65 us  [deliver(): pl.pallas_call(deliver_kernel, name='deliver', out_shape=[jax.ShapeDtypeS...]
    pallas_call x1 -> x0, local copies, waits for them, and re-layouts: 1.41 us -> none  [whole_iteration(): pl.pallas_call(functools.partial(whole_kernel, (shots, nets, bands)), nam...]
where the time goes in v4:
time: 71.3 us; the launch traced here: 71.1 us
  Pallas kernels  70.4 us (99%)
    pallas_call x1, Pallas kernels, whole_iteration(): pl.pallas_call(functools.partial(whole_kernel, (shots, nets, bands)), nam...  68.8 us
    pallas_call x1, Pallas kernels, deliver(): pl.pallas_call(deliver_kernel, name='deliver', out_shape=[jax.ShapeDtypeS...  1.65 us

profile of v4, /device:TPU:0, one launch (start us, length us, event | category | flops | bytes accessed | tf_op | source)
XLA Modules:
  0.0 71.1 jit_solution(10061692354209488307)
XLA Ops:
  0.6 68.8 %whole.1 = (f32[32,128]{1,0:T(8,128)}, f32[128,128]{1,0:T(8,128)}) custom-call(f32[32,1024]{1,0:T(8,128)} %velocity.1, f32[2,32,1024]{2,1,0:T(8,128)} %wave_now.1, f32[2,32,1024]{2,1,0:T(8,128)} %wave_before.1, f32[2,32,1024]{2,1,0:T(8,128)} %adjoint_last.1, f32[2,32,1024]{2,1,0:T(8,128)} %adjoint_after.1, f32[2,16]{1,0:T(2,128)} %wavelet.1, s32[2]{0:T(128)} %source_col.1, ...), custom_call_target="tpu_custom_call" | custom-call | tf_op jit(solution)/shard_map/whole/pallas_call | solution.py:1378
  69.4 1.7 %deliver.1 = (f32[32,128]{1,0:T(8,128)}, f32[18,32]{1,0:T(8,128)}, f32[32,288]{1,0:T(8,128)}, f32[1,288]{1,0:T(1,128)}) custom-call(f32[32,128]{1,0:T(8,128)} %get-tuple-element.10.fresh, f32[128,128]{1,0:T(8,128)} %get-tuple-element.11.totals), custom_call_target="tpu_custom_call" | custom-call | tf_op jit(solution)/shard_map/deliver/pallas_call | solution.py:1481

commit v5 on v4

--- a/solution.py
+++ b/solution.py
@@ -504,38 +504,49 @@
     return jnp.concatenate(list(halves(values)), 0)
 
 
-def dot_split(left, right_high, right_low, dims):
-    height = left.shape[0] // 2
+def doubled(values):
+    return stacked_halves(jnp.concatenate([values, values], 1))
+
+
+def dot_split(left, right):
     both = lax.dot_general(
-        left, right_high, (dims, ((), ())), preferred_element_type=jnp.float32
-    )
-    rest = lax.dot_general(
-        left[:height], right_low, (dims, ((), ())), preferred_element_type=jnp.float32
-    )
-    return both[:height] + both[height:] + rest
+        left, right, (((1,), (0,)), ((), ())), preferred_element_type=jnp.float32
+    )
+    height = both.shape[0] // 2
+    return both[:height] + both[height:]
+
+
+def dot_over(left, right):
+    both = lax.dot_general(
+        left, right, (((1,), (1,)), ((), ())), preferred_element_type=jnp.float32
+    )
+    height = both.shape[0] // 2
+    both = both[:height] + both[height:]
+    breadth = both.shape[1] // 2
+    return both[:, :breadth] + both[:, breadth:]
 
 
 def network_weights(conv_in, conv_mid, conv_out, first, middle, middle_back, last):
     channels = conv_mid.shape[0]
     three = 3 * channels
-    tap_ids = lax.broadcasted_iota(jnp.int32, (18, 72), 0)
-    lane_ids = lax.broadcasted_iota(jnp.int32, (18, 72), 1)
+    tap_ids = lax.broadcasted_iota(jnp.int32, (18, 80), 0)
+    lane_ids = lax.broadcasted_iota(jnp.int32, (18, 80), 1)
     table = jnp.where(lane_ids == tap_ids // 2 * 8 + lax.rem(tap_ids, 2), 1.0, 0.0)
     top = exact_spread(conv_in[...].T, table.astype(jnp.bfloat16))
     blank = jnp.zeros((1, channels), jnp.float32)
     taps = [conv_out[:, t * channels : t * channels + channels] for t in range(9)]
     flips = jnp.concatenate(taps[::-1] + [blank] * 7, 0)
-    tap_ids = lax.broadcasted_iota(jnp.int32, (16, 72), 0)
-    lane_ids = lax.broadcasted_iota(jnp.int32, (16, 72), 1)
+    tap_ids = lax.broadcasted_iota(jnp.int32, (16, 80), 0)
+    lane_ids = lax.broadcasted_iota(jnp.int32, (16, 80), 1)
     table = jnp.where((lane_ids == tap_ids * 8 + 2) & (tap_ids < 9), 1.0, 0.0)
     bottom = exact_spread(flips.T, table.astype(jnp.bfloat16))
-    first[...] = stacked_halves(jnp.concatenate([top, bottom], 0))
+    first[...] = doubled(jnp.concatenate([top, bottom], 0))
     mid = conv_mid[...]
-    middle[...] = stacked_halves(
+    middle[...] = doubled(
         jnp.concatenate([mid[:, d * three : d * three + three] for d in range(3)], 0)
     )
     turned = mid.T
-    middle_back[...] = stacked_halves(
+    middle_back[...] = doubled(
         jnp.concatenate(
             [
                 jnp.concatenate(
@@ -553,12 +564,12 @@
     order = []
     for a in range(3):
         order += [taps[d * 3 + a] for d in range(3)] + [blank] * 5
-    last[...] = stacked_halves(jnp.concatenate(order + [blank] * 8, 0))
+    last[...] = doubled(jnp.concatenate(order + [blank] * 8, 0))
 
 
 def network_stage(
     width, layers, first, middle, middle_back, last, new_velocity, sums,
-    patch, near_high, near_low, far_high, far_low, down_high, down_low, taps, slope_one, hidden,
+    patch, near, far, shifted, taps, slope_one, hidden,
     slope_two, last_taps, update, back,
 ):
     length = layers.shape[1]
@@ -568,14 +579,21 @@
     rows, piece = new_velocity.shape
     shifts = [down * width + across for down in (-1, 0, 1) for across in (-1, 0, 1)]
     pieces = length // chunk
-    flat = ((1,), (0,))
-    over = ((1,), (1,))
-
     def moved(values, shift):
         return pltpu.roll(values, shift % length, 1)
 
-    for tap, shift in enumerate(shifts):
-        patch[tap * 8 : tap * 8 + 8] = moved(layers[...], -shift)
+    for tap in range(0, 10, 2):
+        high, low = halves(
+            jnp.concatenate(
+                [
+                    moved(layers[...], -shifts[t]) if t < 9 else jnp.zeros((8, length), jnp.float32)
+                    for t in (tap, tap + 1)
+                ],
+                0,
+            )
+        )
+        patch[tap * 8 : tap * 8 + 16] = high
+        patch[80 + tap * 8 : 96 + tap * 8] = low
 
     def each(body, carry=0):
         for index in range(pieces):
@@ -589,8 +607,7 @@
         return squashed * (1.0 + values * (1.0 - squashed))
 
     def open_layer(at, carry):
-        high, low = halves(patch[:, at])
-        both = dot_split(first[...], high, low, flat)
+        both = dot_split(first[...], patch[:, at])
         inside = layers[4:5, at] > 0.5
         owned = layers[5:6, at] > 0.5
         before = both[:channels]
@@ -602,14 +619,14 @@
 
     each(open_layer)
 
-    def fan(source, unit, high_ref, low_ref):
+    def fan(source, unit, target):
         for group in range(channels // 16):
             values = source(group)
             for index, way in enumerate((-1, 0, 1)):
                 high, low = halves(moved(values, way * unit))
                 start = index * channels + group * 16
-                high_ref[start : start + 16] = high
-                low_ref[start : start + 16] = low
+                target[start : start + 16] = high
+                target[three + start : three + start + 16] = low
 
     def fold(unit, target):
         for group in range(channels // 8):
@@ -620,10 +637,10 @@
                 + moved(taps[2 * channels + group * 8 : 2 * channels + group * 8 + 8], unit)
             )
 
-    fan(lambda group: hidden[group * 16 : group * 16 + 16], -1, near_high, near_low)
+    fan(lambda group: hidden[group * 16 : group * 16 + 16], -1, near)
 
     def middle_layer(at, carry):
-        taps[:, at] = dot_split(middle[...], near_high[:, at], near_low[:, at], flat)
+        taps[:, at] = dot_split(middle[...], near[:, at])
         return carry
 
     each(middle_layer)
@@ -636,51 +653,51 @@
         after = jnp.where(inside, before * squashed, 0.0)
         hidden[:, at] = after
         slope_two[:, at] = jnp.where(inside, slope_two[:, at] * bend(before, squashed), 0.0)
-        high, low = halves(after)
-        last_taps[:, at] = dot_split(last[...], high, low, flat)[0:24]
+        last_taps[:, at] = dot_split(last[...], stacked_halves(after))[0:24]
         return carry
 
     each(second_layer)
     owned = layers[5:6] > 0.5
     fan(
         lambda group: jnp.where(owned, slope_two[group * 16 : group * 16 + 16], 0.0),
-        width, down_high, down_low,
-    )
-    fan(lambda group: slope_two[group * 16 : group * 16 + 16], 1, far_high, far_low)
-    mixed = last_taps[8:16] + moved(last_taps[0:8], 1) + moved(last_taps[16:24], -1)
-    update[...] = jnp.broadcast_to(
-        layers[0:1] + mixed[1:2] + moved(mixed, width)[0:1] + moved(mixed, -width)[2:3],
-        update.shape,
-    )
-
+        width, shifted,
+    )
+    fan(lambda group: slope_two[group * 16 : group * 16 + 16], 1, far)
     def back_layer(at, carry):
-        taps[:, at] = dot_split(middle_back[...], far_high[:, at], far_low[:, at], flat)
-        left = jnp.concatenate([down_high[:, at], down_low[:, at]], 0)
-        return carry + dot_split(left, near_high[:, at], near_low[:, at], over)
+        taps[:, at] = dot_split(middle_back[...], far[:, at])
+        return carry + dot_over(shifted[:, at], near[:, at])
 
     sums[0:three, 0:three] = each(back_layer, jnp.zeros((three, three), jnp.float32))
-    for row in range(rows):
-        start = (row + 3) * width + 3
-        tile = start // 128 * 128
-        segment = update[:, tile : tile + 256]
-        new_velocity[row : row + 1, :] = pltpu.roll(segment, 256 - start % 128, 1)[0:1, :piece]
     fold(width, back)
 
     def first_grads(at, carry):
         fall = back[:, at] * slope_one[:, at]
-        high, low = halves(patch[:, at])
         left = stacked_halves(jnp.concatenate([fall, hidden[:, at]], 0))
-        return carry + dot_split(left, high, low, over)
-
-    outer = each(first_grads, jnp.zeros((2 * channels, 72), jnp.float32))
-    tap_ids = lax.broadcasted_iota(jnp.int32, (72, 128), 0)
-    lane_ids = lax.broadcasted_iota(jnp.int32, (72, 128), 1)
+        return carry + dot_over(left, patch[:, at])
+
+    outer = each(first_grads, jnp.zeros((2 * channels, 80), jnp.float32))
+    tap_ids = lax.broadcasted_iota(jnp.int32, (80, 128), 0)
+    lane_ids = lax.broadcasted_iota(jnp.int32, (80, 128), 1)
     which = lax.rem(tap_ids, 8)
     table_in = jnp.where((which < 2) & (lane_ids == tap_ids // 8 * 2 + which), 1.0, 0.0)
     table_out = jnp.where((which == 3) & (lane_ids == 26 - tap_ids // 8), 1.0, 0.0)
     sums[three:] = exact_spread(outer[:channels], table_in.astype(jnp.bfloat16)) + exact_spread(
         outer[channels:], table_out.astype(jnp.bfloat16)
     )
+
+    def paint():
+        mixed = last_taps[8:16] + moved(last_taps[0:8], 1) + moved(last_taps[16:24], -1)
+        update[...] = jnp.broadcast_to(
+            layers[0:1] + mixed[1:2] + moved(mixed, width)[0:1] + moved(mixed, -width)[2:3],
+            update.shape,
+        )
+        for row in range(rows):
+            start = (row + 3) * width + 3
+            tile = start // 128 * 128
+            segment = update[:, tile : tile + 256]
+            new_velocity[row : row + 1, :] = pltpu.roll(segment, 256 - start % 128, 1)[0:1, :piece]
+
+    return paint
 
 
 def whole_kernel(
@@ -689,9 +706,8 @@
     rec_last, rec_count, observed, cotangent, conv_in, conv_mid, conv_out,
     new_velocity, totals,
     out_image, windows, layers, sums, sum_slots, band_sums, final_sums, first_weights, middle_weights,
-    back_weights, last_weights, patch, near_high, near_low, far_high, far_low, down_high, down_low,
-    taps, slope_one, hidden, slope_two, last_taps, update, back,
-    arrived, speed_all, speed_sq, small, observed_cols, pulse_cols, source_mask, receiver_mask,
+    back_weights, last_weights, patch, near_taps, far_taps, shifted_taps, taps, slope_one, hidden, slope_two, last_taps, update, back,
+    arrived, speed_all, speed_sq, drift, small, observed_cols, pulse_cols, source_mask, receiver_mask,
     down_weights, across_weights, rims, split, forward, adjoint, image, parts, part_slots, cross, cross_slots, held, lines, line_slots,
     strips, cot_all,
     own_sem, edge_send, edge_recv, speed_send, speed_recv, plane_send, plane_recv, field_send, field_recv, small_send,
@@ -1002,7 +1018,9 @@
         start = pl.multiple_of(piece + side * (half - margin) + tile * 128, 128)
         at = slice(tile * 128, tile * 128 + 128)
         value = speed_all[pl.ds(8, total_rows), pl.ds(start, 128)] * speed_factor
-        speed_sq[:, at] = value * value * (keep[:, at] * (1.0 / weight_scale))
+        value = value * value * (keep[:, at] * (1.0 / weight_scale))
+        speed_sq[:, at] = value
+        drift[:, at] = 2.0 + weights[0] * value
 
     def advance(ref, now, before, finish):
         for tile in range(tiles):
@@ -1011,8 +1029,7 @@
             high = value.astype(jnp.bfloat16)
             split[0:total_rows, at] = high
             split[total_rows:, at] = (value - high.astype(f32)).astype(jnp.bfloat16)
-        left_rim = jnp.broadcast_to(rims[0, 0:1], (total_rows, 128))
-        right_rim = jnp.broadcast_to(rims[1, 0:1], (total_rows, 128))
+        left_rim = jnp.broadcast_to(rims[0, 0:1] > 0.5, (total_rows, 128))
         rows_of = []
         for tile in range(tiles):
             parts_of = [
@@ -1025,7 +1042,7 @@
             rows_of.append(
                 jnp.concatenate(
                     [middle for _, middle, _ in parts_of]
-                    + [before * left_rim + after * right_rim for before, _, after in parts_of],
+                    + [jnp.where(left_rim, before, after) for before, _, after in parts_of],
                     1,
                 )
             )
@@ -1043,11 +1060,10 @@
                 at = slice(tile * 128, tile * 128 + 128)
                 value = ref[now, :, at]
                 total = (
-                    weights[0] * value
-                    + down[:, (tile - pair_start) * 128 : (tile - pair_start) * 128 + 128]
+                    down[:, (tile - pair_start) * 128 : (tile - pair_start) * 128 + 128]
                     + across[tile * total_rows : tile * total_rows + total_rows]
                 )
-                finish(at, 2.0 * value - ref[before, :, at] + speed_sq[:, at] * total)
+                finish(at, drift[:, at] * value - ref[before, :, at] + speed_sq[:, at] * total)
 
     def settle(index, ref, at):
         edge(index).wait_recv()
@@ -1270,9 +1286,9 @@
         first_lane = start - inset
         line = pltpu.roll(line, (inset - (piece - 3)) % (3 * piece), 1)[:, :span]
         layers[:, first_lane : first_lane + span] = layers[:, first_lane : first_lane + span] + line
-    network_stage(
+    paint = network_stage(
         reach_cols, layers, first_weights, middle_weights, back_weights, last_weights, new_velocity,
-        sums, patch, near_high, near_low, far_high, far_low, down_high, down_low, taps, slope_one,
+        sums, patch, near_taps, far_taps, shifted_taps, taps, slope_one,
         hidden, slope_two, last_taps, update, back,
     )
     share = sums.shape[0] // groups
@@ -1322,6 +1338,7 @@
     for step in range(1, groups):
         sum_out(step).start()
     sum_slots[0] = sums[share_of(group)]
+    paint()
     for step in range(1, groups):
         sum_in(step).wait_recv()
     running = sum_slots[lax.rem(groups - group, groups)]
@@ -1392,12 +1409,12 @@
             pltpu.VMEM((groups, 4 * channels // groups, 128), f32),
             pltpu.VMEM((bands, 4 * channels // groups, 128), f32),
             pltpu.VMEM((4 * channels, 128), f32),
-            pltpu.VMEM((4 * channels, 72), half_type),
-            pltpu.VMEM((6 * channels, 3 * channels), half_type),
-            pltpu.VMEM((6 * channels, 3 * channels), half_type),
-            pltpu.VMEM((64, channels), half_type),
-            pltpu.VMEM((72, length), f32),
-            *[pltpu.VMEM((3 * channels, length), half_type)] * 6,
+            pltpu.VMEM((4 * channels, 160), half_type),
+            pltpu.VMEM((6 * channels, 6 * channels), half_type),
+            pltpu.VMEM((6 * channels, 6 * channels), half_type),
+            pltpu.VMEM((64, 2 * channels), half_type),
+            pltpu.VMEM((160, length), half_type),
+            *[pltpu.VMEM((6 * channels, length), half_type)] * 3,
             pltpu.VMEM((3 * channels, length), f32),
             pltpu.VMEM((channels, length), f32),
             pltpu.VMEM((channels, length), f32),
@@ -1407,6 +1424,7 @@
             pltpu.VMEM((channels, length), f32),
             pltpu.VMEM((4, total_rows, width), f32),
             pltpu.VMEM((total_rows + 16, breadth + 2 * piece), f32),
+            pltpu.VMEM((total_rows, width), f32),
             pltpu.VMEM((total_rows, width), f32),
             pltpu.VMEM((8 + steps, 128), f32),
             pltpu.VMEM((steps, 8, width), f32),

time: 71.3 us -> 70.5 us (0.989)
  Pallas kernels: 70.4 us -> 69.6 us
    pallas_call x1, Pallas kernels: 68.8 us -> 67.9 us  [whole_iteration(): pl.pallas_call(functools.partial(whole_kernel, (shots, nets, bands)), nam...]
where the time goes in v5:
time: 70.5 us; the launch traced here: 70.2 us
  Pallas kernels  69.6 us (99%)
    pallas_call x1, Pallas kernels, whole_iteration(): pl.pallas_call(functools.partial(whole_kernel, (shots, nets, bands)), nam...  67.9 us
    pallas_call x1, Pallas kernels, deliver(): pl.pallas_call(deliver_kernel, name='deliver', out_shape=[jax.ShapeDtypeS...  1.65 us

profile of v5, /device:TPU:0, one launch (start us, length us, event | category | flops | bytes accessed | tf_op | source)
XLA Modules:
  0.0 70.2 jit_solution(10593905665820068645)
XLA Ops:
  0.6 67.9 %whole.1 = (f32[32,128]{1,0:T(8,128)}, f32[128,128]{1,0:T(8,128)}) custom-call(f32[32,1024]{1,0:T(8,128)} %velocity.1, f32[2,32,1024]{2,1,0:T(8,128)} %wave_now.1, f32[2,32,1024]{2,1,0:T(8,128)} %wave_before.1, f32[2,32,1024]{2,1,0:T(8,128)} %adjoint_last.1, f32[2,32,1024]{2,1,0:T(8,128)} %adjoint_after.1, f32[2,16]{1,0:T(2,128)} %wavelet.1, s32[2]{0:T(128)} %source_col.1, ...), custom_call_target="tpu_custom_call" | custom-call | tf_op jit(solution)/shard_map/whole/pallas_call | solution.py:1395
  68.6 1.7 %deliver.1 = (f32[32,128]{1,0:T(8,128)}, f32[18,32]{1,0:T(8,128)}, f32[32,288]{1,0:T(8,128)}, f32[1,288]{1,0:T(1,128)}) custom-call(f32[32,128]{1,0:T(8,128)} %get-tuple-element.10.fresh, f32[128,128]{1,0:T(8,128)} %get-tuple-element.11.totals), custom_call_target="tpu_custom_call" | custom-call | tf_op jit(solution)/shard_map/deliver/pallas_call | solution.py:1499

commit v6 on v5

--- a/solution.py
+++ b/solution.py
@@ -704,7 +704,8 @@
     sizes,
     velocity, wave_now, wave_before, adjoint_last, adjoint_after, wavelet, source_col, rec_first,
     rec_last, rec_count, observed, cotangent, conv_in, conv_mid, conv_out,
-    new_velocity, totals,
+    velocity_far, totals,
+    new_velocity, output_sem,
     out_image, windows, layers, sums, sum_slots, band_sums, final_sums, first_weights, middle_weights,
     back_weights, last_weights, patch, near_taps, far_taps, shifted_taps, taps, slope_one, hidden, slope_two, last_taps, update, back,
     arrived, speed_all, speed_sq, drift, small, observed_cols, pulse_cols, source_mask, receiver_mask,
@@ -1072,8 +1073,7 @@
     for index in (0, 1):
         each_field_in(index)
         edge(index).start()
-    for index in (2, 3):
-        each_field_out(index, lambda copy: copy.start())
+        each_field_out(index + 2, lambda copy: copy.start())
     settle(0, forward, 1)
     settle(1, forward, 0)
 
@@ -1324,14 +1324,14 @@
 
     def last_out(step):
         return remote(
-            final_sums.at[share_of(group)], final_sums.at[share_of(group)], last_send.at[step],
+            final_sums, totals.at[share_of(group)], last_send.at[step],
             last_recv.at[groups - step], member(lax.rem(group + step, groups)),
         )
 
     def last_in(step):
         peer = lax.rem(group + step, groups)
         return remote(
-            final_sums.at[share_of(peer)], final_sums.at[share_of(peer)], last_send.at[step],
+            final_sums, totals.at[share_of(peer)], last_send.at[step],
             last_recv.at[step], member(peer),
         )
 
@@ -1339,6 +1339,8 @@
         sum_out(step).start()
     sum_slots[0] = sums[share_of(group)]
     paint()
+    deliver_velocity = pltpu.make_async_copy(new_velocity, velocity_far, output_sem.at[0])
+    deliver_velocity.start()
     for step in range(1, groups):
         sum_in(step).wait_recv()
     running = sum_slots[lax.rem(groups - group, groups)]
@@ -1357,14 +1359,17 @@
     running = band_sums[lax.rem(bands - band, bands)]
     for index in range(1, bands):
         running = running + band_sums[lax.rem(index + bands - band, bands)]
-    final_sums[share_of(group)] = running
+    final_sums[...] = running
+    own_totals = pltpu.make_async_copy(final_sums, totals.at[share_of(group)], output_sem.at[1])
+    own_totals.start()
     for step in range(1, groups):
         last_out(step).start()
     for step in range(1, bands):
         band_out(step).wait_send()
     for step in range(1, groups):
         last_in(step).wait_recv()
-    totals[...] = final_sums[...]
+    own_totals.wait()
+    deliver_velocity.wait()
     for step in range(1, groups):
         last_out(step).wait_send()
 
@@ -1400,15 +1405,17 @@
             for shape in (cotangent.shape, (4 * channels, 128))
         ],
         in_specs=anywhere * 5 + scalars * 5 + vmem(5),
-        out_specs=vmem(2),
+        out_specs=anywhere * 2,
         scratch_shapes=[
+            pltpu.VMEM((rows, piece), f32),
+            dma((2,)),
             pltpu.VMEM((rows + 16, 3 * piece), f32),
             pltpu.VMEM((3 * piece // 128, (rows + 16) * 8, 128), f32),
             pltpu.VMEM((8, length), f32),
             pltpu.VMEM((4 * channels, 128), f32),
             pltpu.VMEM((groups, 4 * channels // groups, 128), f32),
             pltpu.VMEM((bands, 4 * channels // groups, 128), f32),
-            pltpu.VMEM((4 * channels, 128), f32),
+            pltpu.VMEM((4 * channels // groups, 128), f32),
             pltpu.VMEM((4 * channels, 160), half_type),
             pltpu.VMEM((6 * channels, 6 * channels), half_type),
             pltpu.VMEM((6 * channels, 6 * channels), half_type),

time: 70.5 us -> 69.8 us (0.990)
  no operation moved by 1% of the time
where the time goes in v6:
time: 69.8 us; the launch traced here: 69.6 us
  Pallas kernels  68.9 us (99%)
    pallas_call x1, Pallas kernels, whole_iteration(): pl.pallas_call(functools.partial(whole_kernel, (shots, nets, bands)), nam...  67.3 us
    pallas_call x1, Pallas kernels, deliver(): pl.pallas_call(deliver_kernel, name='deliver', out_shape=[jax.ShapeDtypeS...  1.65 us

profile of v6, /device:TPU:0, one launch (start us, length us, event | category | flops | bytes accessed | tf_op | source)
XLA Modules:
  0.0 69.6 jit_solution(1460285536209052451)
XLA Ops:
  0.6 67.3 %whole.1 = (f32[32,128]{1,0:T(8,128)}, f32[128,128]{1,0:T(8,128)}) custom-call(f32[32,1024]{1,0:T(8,128)} %velocity.1, f32[2,32,1024]{2,1,0:T(8,128)} %wave_now.1, f32[2,32,1024]{2,1,0:T(8,128)} %wave_before.1, f32[2,32,1024]{2,1,0:T(8,128)} %adjoint_last.1, f32[2,32,1024]{2,1,0:T(8,128)} %adjoint_after.1, f32[2,16]{1,0:T(2,128)} %wavelet.1, s32[2]{0:T(128)} %source_col.1, ...), custom_call_target="tpu_custom_call" | custom-call | tf_op jit(solution)/shard_map/whole/pallas_call | solution.py:1400
  67.9 1.7 %deliver.1 = (f32[32,128]{1,0:T(8,128)}, f32[18,32]{1,0:T(8,128)}, f32[32,288]{1,0:T(8,128)}, f32[1,288]{1,0:T(1,128)}) custom-call(f32[32,128]{1,0:T(8,128)} %get-tuple-element.10.fresh, f32[128,128]{1,0:T(8,128)} %get-tuple-element.11.totals), custom_call_target="tpu_custom_call" | custom-call | tf_op jit(solution)/shard_map/deliver/pallas_call | solution.py:1506

commit v7 on v6

--- a/solution.py
+++ b/solution.py
@@ -709,7 +709,7 @@
     out_image, windows, layers, sums, sum_slots, band_sums, final_sums, first_weights, middle_weights,
     back_weights, last_weights, patch, near_taps, far_taps, shifted_taps, taps, slope_one, hidden, slope_two, last_taps, update, back,
     arrived, speed_all, speed_sq, drift, small, observed_cols, pulse_cols, source_mask, receiver_mask,
-    down_weights, across_weights, rims, split, forward, adjoint, image, parts, part_slots, cross, cross_slots, held, lines, line_slots,
+    down_weights, across_weights, rims, split, forward, adjoint, image, parts, part_slots, lead_slots, tail_slots, cross, cross_slots, held, lines, line_slots,
     strips, cot_all,
     own_sem, edge_send, edge_recv, speed_send, speed_recv, plane_send, plane_recv, field_send, field_recv, small_send,
     small_recv, cot_send, cot_recv, part_send, part_recv, cross_send, cross_recv, line_send, line_recv, sum_send, sum_recv, band_send, band_recv,
@@ -1141,19 +1141,36 @@
     def holder(which, index):
         return {"shot": index // nets * sides + which, "net": lax.rem(index, nets)}
 
-    def part_out(step):
+    top_first = band // (bands // 2)
+    lead_rows = total_rows // 2 + 8
+    lead = pl.multiple_of((1 - top_first) * (total_rows - lead_rows), 8)
+    tail = pl.multiple_of(top_first * lead_rows, 8)
+    landed = (part_slots, lead_slots, tail_slots)
+    segments = ((total_rows, 16), (lead, lead_rows), (tail, total_rows - lead_rows))
+
+    def part_out(step, which):
         peer = lax.rem(place + step, pieces)
-        return remote(
-            parts.at[peer], part_slots.at[pieces - step], part_send.at[step],
-            part_recv.at[pieces - step], holder(side, peer),
-        )
-
-    def part_in(step):
+        at = pl.ds(*segments[which])
+        return remote(
+            parts.at[peer, at], landed[which].at[pieces - step], part_send.at[step, which],
+            part_recv.at[pieces - step, which], holder(side, peer),
+        )
+
+    def part_in(step, which):
         peer = lax.rem(place + step, pieces)
-        return remote(
-            parts.at[peer], part_slots.at[step], part_send.at[step],
-            part_recv.at[step], holder(side, peer),
-        )
+        at = pl.ds(*segments[which])
+        return remote(
+            parts.at[peer, at], landed[which].at[step], part_send.at[step, which],
+            part_recv.at[step, which], holder(side, peer),
+        )
+
+    def gathered(which):
+        at = pl.ds(*segments[which])
+        summed = parts[place, at]
+        for step in range(1, pieces):
+            part_in(step, which).wait_recv()
+            summed = summed + landed[which][step]
+        return summed
 
     def cross_out(toward):
         target = holder(side + 1, 0) if toward else holder(side - 1, jnp.int32(pieces - 1))
@@ -1172,16 +1189,12 @@
     has_left = side > 0
     pl.when(has_right)(lambda: cross_out(1).start())
     pl.when(has_left)(lambda: cross_out(0).start())
-    for step in range(1, pieces):
-        part_out(step).start()
-    summed = parts[place]
-    for step in range(1, pieces):
-        part_in(step).wait_recv()
-        summed = summed + part_slots[step]
+    for which in range(3):
+        for step in range(1, pieces):
+            part_out(step, which).start()
     held[0:8] = jnp.zeros((8, piece), f32)
-    held[8 : 8 + total_rows] = summed[0:total_rows]
     held[8 + total_rows : 16 + total_rows] = jnp.zeros((8, piece), f32)
-    held[16 + total_rows :] = summed[total_rows:]
+    held[16 + total_rows :] = gathered(0)
     for came, present, at in (
         (0, has_left & (place == 0), 0), (1, has_right & (place == pieces - 1), 8)
     ):
@@ -1193,39 +1206,46 @@
                 running = running + cross_slots[came, source]
             held[16 + total_rows + at : 24 + total_rows + at] = running
 
-    for target in range(bands):
-        lines[target, 0 : rows + 16] = held[target * rows : target * rows + rows + 16]
+    def line_target(turn):
+        return (1 - top_first) * (bands - 1 - turn) + top_first * turn
+
+    def line_out(turn):
+        target = line_target(turn)
+        return remote(
+            lines.at[target], line_slots.at[band], line_send.at[turn], line_recv.at[band],
+            {"shot": kept // nets, "net": lax.rem(kept, nets), "band": target},
+        )
+
+    def line_in(source):
+        return remote(
+            lines.at[source], line_slots.at[source], line_send.at[0], line_recv.at[source],
+            {"shot": kept // nets, "net": lax.rem(kept, nets), "band": source},
+        )
+
+    def line_away(turn):
+        return swapped | (line_target(turn) != band)
+
+    held[pl.ds(8 + lead, lead_rows)] = gathered(1)
+    for turn in range(bands):
+        if turn == bands // 2:
+            held[pl.ds(8 + tail, total_rows - lead_rows)] = gathered(2)
+        target = line_target(turn)
+        lines[target, 0 : rows + 16] = held[pl.ds(pl.multiple_of(target * rows, 8), rows + 16)]
         lines[target, rows + 16 :] = held[16 + total_rows :]
-
-    def line_out(step):
-        peer = lax.rem(band + step, bands)
-        return remote(
-            lines.at[peer], line_slots.at[(bands - step) % bands], line_send.at[step],
-            line_recv.at[(bands - step) % bands],
-            {"shot": kept // nets, "net": lax.rem(kept, nets), "band": peer},
-        )
-
-    def line_in(step):
-        peer = lax.rem(band + step, bands)
-        return remote(
-            lines.at[peer], line_slots.at[step], line_send.at[step], line_recv.at[step],
-            {"shot": kept // nets, "net": lax.rem(kept, nets), "band": peer},
-        )
-
-    for step in range(1, bands):
-        line_out(step).start()
-    pl.when(swapped)(lambda: line_out(0).start())
+        pl.when(line_away(turn))(lambda turn=turn: line_out(turn).start())
+
+    @pl.when(jnp.logical_not(swapped))
+    def _():
+        line_slots[band] = lines[band]
+
     for index in (2, 3):
         each_field_out(index, lambda copy: copy.wait_send())
         edge(index).wait_send()
     pl.when(has_right)(lambda: cross_out(1).wait_send())
     pl.when(has_left)(lambda: cross_out(0).wait_send())
-    for step in range(1, pieces):
-        part_out(step).wait_send()
-
-    @pl.when(jnp.logical_not(swapped))
-    def _():
-        line_slots[0] = lines[band]
+    for which in range(3):
+        for step in range(1, pieces):
+            part_out(step, which).wait_send()
 
     pl.when(group > 0)(lambda: cot_right().wait_recv())
     pl.when(group < groups - 1)(lambda: cot_left().wait_recv())
@@ -1263,11 +1283,10 @@
     layers[...] = jnp.zeros(layers.shape, f32)
     out_image[...] = jnp.zeros(out_image.shape, f32)
     strips[...] = jnp.zeros(strips.shape, f32)
-    pl.when(swapped)(lambda: line_in(0).wait_recv())
-    final = line_slots[0]
-    for step in range(1, bands):
-        line_in(step).wait_recv()
-        final = final + line_slots[step]
+    final = None
+    for source in range(bands):
+        pl.when(swapped | (band != source))(lambda source=source: line_in(source).wait_recv())
+        final = line_slots[source] if final is None else final + line_slots[source]
     out_image[:, piece : 2 * piece] = final[0 : rows + 16]
     strips[8 : 8 + total_rows, 0:16] = final[rows + 16 :].T
     around = pl.ds(pl.multiple_of(band * rows, 8), rows + 16)
@@ -1349,9 +1368,8 @@
     band_sums[0] = running
     for step in range(1, bands):
         band_out(step).start()
-    for step in range(1, bands):
-        line_out(step).wait_send()
-    pl.when(swapped)(lambda: line_out(0).wait_send())
+    for turn in range(bands):
+        pl.when(line_away(turn))(lambda turn=turn: line_out(turn).wait_send())
     for step in range(1, groups):
         sum_out(step).wait_send()
     for step in range(1, bands):
@@ -1446,7 +1464,9 @@
             pltpu.VMEM((2, total_rows, width), f32),
             pltpu.VMEM((total_rows, width), f32),
             pltpu.VMEM((pieces, total_rows + 16, piece), f32),
-            pltpu.VMEM((pieces, total_rows + 16, piece), f32),
+            pltpu.VMEM((pieces, 16, piece), f32),
+            pltpu.VMEM((pieces, total_rows // 2 + 8, piece), f32),
+            pltpu.VMEM((pieces, total_rows // 2 - 8, piece), f32),
             pltpu.VMEM((2, 8, total_rows), f32),
             pltpu.VMEM((2, pieces, 8, total_rows), f32),
             pltpu.VMEM((total_rows + 32, piece), f32),
@@ -1467,8 +1487,8 @@
             dma((1,)),
             dma((4,)),
             dma((4,)),
-            dma((pieces,)),
-            dma((pieces,)),
+            dma((pieces, 3)),
+            dma((pieces, 3)),
             dma((2,)),
             dma((2, pieces)),
             dma((bands,)),

time: 69.8 us -> 68.9 us (0.987)
  Pallas kernels: 68.9 us -> 68 us
    pallas_call x1, Pallas kernels: 67.3 us -> 66.3 us  [whole_iteration(): pl.pallas_call(functools.partial(whole_kernel, (shots, nets, bands)), nam...]
where the time goes in v7:
time: 68.9 us; the launch traced here: 68.6 us
  Pallas kernels  68 us (99%)
    pallas_call x1, Pallas kernels, whole_iteration(): pl.pallas_call(functools.partial(whole_kernel, (shots, nets, bands)), nam...  66.3 us
    pallas_call x1, Pallas kernels, deliver(): pl.pallas_call(deliver_kernel, name='deliver', out_shape=[jax.ShapeDtypeS...  1.65 us

profile of v7, /device:TPU:0, one launch (start us, length us, event | category | flops | bytes accessed | tf_op | source)
XLA Modules:
  0.0 68.6 jit_solution(5499362744226686461)
XLA Ops:
  0.6 66.3 %whole.1 = (f32[32,128]{1,0:T(8,128)}, f32[128,128]{1,0:T(8,128)}) custom-call(f32[32,1024]{1,0:T(8,128)} %velocity.1, f32[2,32,1024]{2,1,0:T(8,128)} %wave_now.1, f32[2,32,1024]{2,1,0:T(8,128)} %wave_before.1, f32[2,32,1024]{2,1,0:T(8,128)} %adjoint_last.1, f32[2,32,1024]{2,1,0:T(8,128)} %adjoint_after.1, f32[2,16]{1,0:T(2,128)} %wavelet.1, s32[2]{0:T(128)} %source_col.1, ...), custom_call_target="tpu_custom_call" | custom-call | tf_op jit(solution)/shard_map/whole/pallas_call | solution.py:1418
  67.0 1.7 %deliver.1 = (f32[32,128]{1,0:T(8,128)}, f32[18,32]{1,0:T(8,128)}, f32[32,288]{1,0:T(8,128)}, f32[1,288]{1,0:T(1,128)}) custom-call(f32[32,128]{1,0:T(8,128)} %get-tuple-element.10.fresh, f32[128,128]{1,0:T(8,128)} %get-tuple-element.11.totals), custom_call_target="tpu_custom_call" | custom-call | tf_op jit(solution)/shard_map/deliver/pallas_call | solution.py:1526

commit v8 on v7

--- a/solution.py
+++ b/solution.py
@@ -709,7 +709,7 @@
     out_image, windows, layers, sums, sum_slots, band_sums, final_sums, first_weights, middle_weights,
     back_weights, last_weights, patch, near_taps, far_taps, shifted_taps, taps, slope_one, hidden, slope_two, last_taps, update, back,
     arrived, speed_all, speed_sq, drift, small, observed_cols, pulse_cols, source_mask, receiver_mask,
-    down_weights, across_weights, rims, split, forward, adjoint, image, parts, part_slots, lead_slots, tail_slots, cross, cross_slots, held, lines, line_slots,
+    down_weights, across_weights, rims, splits, forward, walk, adjoint, image, parts, part_slots, lead_slots, tail_slots, cross, cross_slots, held, lines, line_slots,
     strips, cot_all,
     own_sem, edge_send, edge_recv, speed_send, speed_recv, plane_send, plane_recv, field_send, field_recv, small_send,
     small_recv, cot_send, cot_recv, part_send, part_recv, cross_send, cross_recv, line_send, line_recv, sum_send, sum_recv, band_send, band_recv,
@@ -1023,7 +1023,7 @@
         speed_sq[:, at] = value
         drift[:, at] = 2.0 + weights[0] * value
 
-    def advance(ref, now, before, finish):
+    def advance(ref, now, before, finish, split):
         for tile in range(tiles):
             at = slice(tile * 128, tile * 128 + 128)
             value = ref[now, :, at]
@@ -1047,23 +1047,16 @@
                     1,
                 )
             )
-        across = lax.dot_general(
-            jnp.concatenate(rows_of, 0), across_weights[...], (((1,), (0,)), ((), ())),
-            preferred_element_type=f32,
-        )
-        for pair_start in range(0, tiles, 2):
-            pair_tiles = range(pair_start, min(pair_start + 2, tiles))
+        for first_tile, last_tile in ((0, 2), (2, 4), (4, 5)):
             down = lax.dot_general(
-                down_weights[...], split[:, pair_start * 128 : pair_tiles[-1] * 128 + 128],
-                (((1,), (0,)), ((), ())), preferred_element_type=f32,
-            )
-            for tile in pair_tiles:
+                down_weights[...], split[:, first_tile * 128 : last_tile * 128], (((1,), (0,)), ((), ())), preferred_element_type=f32)
+            across = lax.dot_general(
+                jnp.concatenate(rows_of[first_tile:last_tile], 0), across_weights[...], (((1,), (0,)), ((), ())), preferred_element_type=f32)
+            for tile in range(first_tile, last_tile):
                 at = slice(tile * 128, tile * 128 + 128)
                 value = ref[now, :, at]
-                total = (
-                    down[:, (tile - pair_start) * 128 : (tile - pair_start) * 128 + 128]
-                    + across[tile * total_rows : tile * total_rows + total_rows]
-                )
+                turn = tile - first_tile
+                total = down[:, turn * 128 : turn * 128 + 128] + across[turn * total_rows : turn * total_rows + total_rows]
                 finish(at, drift[:, at] * value - ref[before, :, at] + speed_sq[:, at] * total)
 
     def settle(index, ref, at):
@@ -1074,19 +1067,23 @@
         each_field_in(index)
         edge(index).start()
         each_field_out(index + 2, lambda copy: copy.start())
-    settle(0, forward, 1)
-    settle(1, forward, 0)
-
-    def forward_step(index, carry):
-        added = pulse_cols[index]
-
-        def finish(at, fresh):
-            forward[index + 2, :, at] = jnp.concatenate([fresh[0:8] + added[:, at], fresh[8:]], 0)
-
-        advance(forward, index + 1, index, finish)
+    settle(0, walk, 0)
+    settle(1, walk, 1)
+
+    def forward_step(pair, carry):
+        for turn in range(4):
+            index = 4 * pair + turn
+            added = pulse_cols[index]
+
+            def finish(at, fresh, turn=turn, index=index, added=added):
+                fresh = jnp.concatenate([fresh[0:8] + added[:, at], fresh[8:]], 0)
+                forward[index, :, at] = fresh
+                walk[1 - turn % 2, :, at] = fresh
+
+            advance(walk, turn % 2, 1 - turn % 2, finish, splits.at[turn % 2])
         return carry
 
-    lax.fori_loop(0, steps, forward_step, 0)
+    lax.fori_loop(0, steps // 4, forward_step, 0)
     for step in range(1, bands):
         speed_line(step).wait_send()
     pl.when(band < bands - 1)(lambda: cot_down().wait_send())
@@ -1108,21 +1105,20 @@
     settle(3, adjoint, 1)
     image[...] = jnp.zeros(image.shape, f32)
 
-    def adjoint_step(index, carry):
-        moment = steps - 1 - index
-        now = lax.rem(index, 2)
-        later = 1 - now
-        added = receiver_mask[...] * forward[moment + 2, 0:8] - observed_cols[moment]
-
-        def finish(at, fresh):
-            fresh = jnp.concatenate([fresh[0:8] + added[:, at], fresh[8:]], 0)
-            adjoint[later, :, at] = fresh
-            image[:, at] = image[:, at] + forward[moment + 2, :, at] * fresh
-
-        advance(adjoint, now, later, finish)
+    def adjoint_step(pair, carry):
+        for turn in range(4):
+            moment = steps - 1 - (4 * pair + turn)
+            added = receiver_mask[...] * forward[moment, 0:8] - observed_cols[moment]
+
+            def finish(at, fresh, turn=turn, moment=moment, added=added):
+                fresh = jnp.concatenate([fresh[0:8] + added[:, at], fresh[8:]], 0)
+                adjoint[1 - turn % 2, :, at] = fresh
+                image[:, at] = image[:, at] + forward[moment, :, at] * fresh
+
+            advance(adjoint, turn % 2, 1 - turn % 2, finish, splits.at[turn % 2])
         return carry
 
-    lax.fori_loop(0, steps, adjoint_step, 0)
+    lax.fori_loop(0, steps // 4, adjoint_step, 0)
 
     parts[...] = jnp.zeros(parts.shape, f32)
     for index in range(pieces):
@@ -1459,8 +1455,9 @@
             pltpu.VMEM((total_rows, 2 * total_rows), jnp.bfloat16),
             pltpu.VMEM((512, 128), jnp.bfloat16),
             pltpu.VMEM((2, 16, 128), jnp.bfloat16),
-            pltpu.VMEM((2 * total_rows, width), jnp.bfloat16),
-            pltpu.VMEM((steps + 2, total_rows, width), f32),
+            pltpu.VMEM((2, 2 * total_rows, width), jnp.bfloat16),
+            pltpu.VMEM((steps, total_rows, width), f32),
+            pltpu.VMEM((2, total_rows, width), f32),
             pltpu.VMEM((2, total_rows, width), f32),
             pltpu.VMEM((total_rows, width), f32),
             pltpu.VMEM((pieces, total_rows + 16, piece), f32),

time: 68.9 us -> 67 us (0.972)
  Pallas kernels: 68 us -> 66.1 us
    pallas_call x1, Pallas kernels: 66.3 us -> 64.4 us  [whole_iteration(): pl.pallas_call(functools.partial(whole_kernel, (shots, nets, bands)), nam...]
where the time goes in v8:
time: 67 us; the launch traced here: 66.7 us
  Pallas kernels  66.1 us (99%)
    pallas_call x1, Pallas kernels, whole_iteration(): pl.pallas_call(functools.partial(whole_kernel, (shots, nets, bands)), nam...  64.4 us
    pallas_call x1, Pallas kernels, deliver(): pl.pallas_call(deliver_kernel, name='deliver', out_shape=[jax.ShapeDtypeS...  1.65 us

profile of v8, /device:TPU:0, one launch (start us, length us, event | category | flops | bytes accessed | tf_op | source)
XLA Modules:
  0.0 66.7 jit_solution(9580817787718803838)
XLA Ops:
  0.6 64.4 %whole.1 = (f32[32,128]{1,0:T(8,128)}, f32[128,128]{1,0:T(8,128)}) custom-call(f32[32,1024]{1,0:T(8,128)} %velocity.1, f32[2,32,1024]{2,1,0:T(8,128)} %wave_now.1, f32[2,32,1024]{2,1,0:T(8,128)} %wave_before.1, f32[2,32,1024]{2,1,0:T(8,128)} %adjoint_last.1, f32[2,32,1024]{2,1,0:T(8,128)} %adjoint_after.1, f32[2,16]{1,0:T(2,128)} %wavelet.1, s32[2]{0:T(128)} %source_col.1, ...), custom_call_target="tpu_custom_call" | custom-call | tf_op jit(solution)/shard_map/whole/pallas_call | solution.py:1414
  65.1 1.7 %deliver.1 = (f32[32,128]{1,0:T(8,128)}, f32[18,32]{1,0:T(8,128)}, f32[32,288]{1,0:T(8,128)}, f32[1,288]{1,0:T(1,128)}) custom-call(f32[32,128]{1,0:T(8,128)} %get-tuple-element.10.fresh, f32[128,128]{1,0:T(8,128)} %get-tuple-element.11.totals), custom_call_target="tpu_custom_call" | custom-call | tf_op jit(solution)/shard_map/deliver/pallas_call | solution.py:1523

commit v9 on v8

--- a/solution.py
+++ b/solution.py
@@ -570,7 +570,7 @@
 def network_stage(
     width, layers, first, middle, middle_back, last, new_velocity, sums,
     patch, near, far, shifted, taps, slope_one, hidden,
-    slope_two, last_taps, update, back,
+    slope_two, last_taps, update, back, early,
 ):
     length = layers.shape[1]
     chunk = length
@@ -668,6 +668,7 @@
         return carry + dot_over(shifted[:, at], near[:, at])
 
     sums[0:three, 0:three] = each(back_layer, jnp.zeros((three, three), jnp.float32))
+    early()
     fold(width, back)
 
     def first_grads(at, carry):
@@ -740,8 +741,9 @@
     owner_side = lax.rem(band, sides)
     owner_slot = band // sides
     is_mine = owner_side == side
-    kept = side * pieces + place
-    swapped = kept != group
+    piece_side = group // pieces
+    piece_index = lax.rem(group, pieces)
+    own_part = piece_side == side
 
     cot_all[...] = jnp.zeros(cot_all.shape, f32)
     barrier = pltpu.get_barrier_semaphore()
@@ -762,18 +764,6 @@
             device_id_type=MESH,
         )
 
-    @pl.when(swapped)
-    def _():
-        for step in range(1, bands):
-            pl.semaphore_signal(
-                barrier, inc=1,
-                device_id={
-                    "shot": kept // nets, "net": lax.rem(kept, nets),
-                    "band": lax.rem(band + step, bands),
-                },
-                device_id_type=MESH,
-            )
-
     column = pl.multiple_of(group * piece, 128)
 
     def window(which):
@@ -819,7 +809,7 @@
         small[0:8] = table
         small[8 : 8 + steps] = observed[owner_slot]
 
-    peers = groups - 1 + 2 * (bands - 1) + (bands - 1) * lax.min(lax.abs(kept - group), 1)
+    peers = groups - 1 + 2 * (bands - 1)
     pl.semaphore_wait(barrier, peers)
 
     def speed_line(step):
@@ -1071,8 +1061,8 @@
     settle(1, walk, 1)
 
     def forward_step(pair, carry):
-        for turn in range(4):
-            index = 4 * pair + turn
+        for turn in range(8):
+            index = 8 * pair + turn
             added = pulse_cols[index]
 
             def finish(at, fresh, turn=turn, index=index, added=added):
@@ -1083,7 +1073,7 @@
             advance(walk, turn % 2, 1 - turn % 2, finish, splits.at[turn % 2])
         return carry
 
-    lax.fori_loop(0, steps // 4, forward_step, 0)
+    lax.fori_loop(0, steps // 8, forward_step, 0)
     for step in range(1, bands):
         speed_line(step).wait_send()
     pl.when(band < bands - 1)(lambda: cot_down().wait_send())
@@ -1106,8 +1096,8 @@
     image[...] = jnp.zeros(image.shape, f32)
 
     def adjoint_step(pair, carry):
-        for turn in range(4):
-            moment = steps - 1 - (4 * pair + turn)
+        for turn in range(8):
+            moment = steps - 1 - (8 * pair + turn)
             added = receiver_mask[...] * forward[moment, 0:8] - observed_cols[moment]
 
             def finish(at, fresh, turn=turn, moment=moment, added=added):
@@ -1118,7 +1108,7 @@
             advance(adjoint, turn % 2, 1 - turn % 2, finish, splits.at[turn % 2])
         return carry
 
-    lax.fori_loop(0, steps // 4, adjoint_step, 0)
+    lax.fori_loop(0, steps // 8, adjoint_step, 0)
 
     parts[...] = jnp.zeros(parts.shape, f32)
     for index in range(pieces):
@@ -1134,9 +1124,6 @@
         else:
             cross[0] = turned[0:8]
 
-    def holder(which, index):
-        return {"shot": index // nets * sides + which, "net": lax.rem(index, nets)}
-
     top_first = band // (bands // 2)
     lead_rows = total_rows // 2 + 8
     lead = pl.multiple_of((1 - top_first) * (total_rows - lead_rows), 8)
@@ -1144,32 +1131,39 @@
     landed = (part_slots, lead_slots, tail_slots)
     segments = ((total_rows, 16), (lead, lead_rows), (tail, total_rows - lead_rows))
 
-    def part_out(step, which):
-        peer = lax.rem(place + step, pieces)
-        at = pl.ds(*segments[which])
-        return remote(
-            parts.at[peer, at], landed[which].at[pieces - step], part_send.at[step, which],
-            part_recv.at[pieces - step, which], holder(side, peer),
-        )
-
-    def part_in(step, which):
-        peer = lax.rem(place + step, pieces)
-        at = pl.ds(*segments[which])
-        return remote(
-            parts.at[peer, at], landed[which].at[step], part_send.at[step, which],
-            part_recv.at[step, which], holder(side, peer),
-        )
+    def part_out(turn, which):
+        target = lax.rem(piece_index + 1 + turn, pieces)
+        return remote(
+            parts.at[target, pl.ds(*segments[which])], landed[which].at[place],
+            part_send.at[turn, which], part_recv.at[place, which], member(side * pieces + target),
+        )
+
+    def part_in(source, which):
+        return remote(
+            landed[which].at[source], landed[which].at[source], part_send.at[0, which],
+            part_recv.at[source, which],
+            {"shot": source // nets * sides + piece_side, "net": source % nets},
+        )
+
+    def part_away(turn):
+        if turn < pieces - 1:
+            return piece_index >= 0
+        return jnp.logical_not(own_part)
 
     def gathered(which):
-        at = pl.ds(*segments[which])
-        summed = parts[place, at]
-        for step in range(1, pieces):
-            part_in(step, which).wait_recv()
-            summed = summed + landed[which][step]
+        summed = None
+        for source in range(pieces):
+            pl.when(jnp.logical_not(own_part & (place == source)))(
+                lambda source=source: part_in(source, which).wait_recv()
+            )
+            summed = landed[which][source] if summed is None else summed + landed[which][source]
         return summed
 
+    def cross_target(toward):
+        return (side + 1) * pieces if toward else side * pieces - 1
+
     def cross_out(toward):
-        target = holder(side + 1, 0) if toward else holder(side - 1, jnp.int32(pieces - 1))
+        target = member(cross_target(toward))
         return remote(
             cross.at[toward], cross_slots.at[1 - toward, place], cross_send.at[toward],
             cross_recv.at[1 - toward, place], target,
@@ -1178,27 +1172,49 @@
     def cross_in(came, source):
         return remote(
             cross.at[came], cross_slots.at[came, source], cross_send.at[came],
-            cross_recv.at[came, source], member(lax.rem(group + 1, groups)),
+            cross_recv.at[came, source],
+            {"shot": source // nets * sides + piece_side + (1 if came else -1), "net": source % nets},
         )
 
     has_right = side < sides - 1
     has_left = side > 0
-    pl.when(has_right)(lambda: cross_out(1).start())
-    pl.when(has_left)(lambda: cross_out(0).start())
+    far_right = has_right & (cross_target(1) != group)
+    far_left = has_left & (cross_target(0) != group)
+    pl.when(far_right)(lambda: cross_out(1).start())
+    pl.when(far_left)(lambda: cross_out(0).start())
+
+    @pl.when(has_right & (cross_target(1) == group))
+    def _():
+        cross_slots[0, place] = cross[1]
+
+    @pl.when(has_left & (cross_target(0) == group))
+    def _():
+        cross_slots[1, place] = cross[0]
+
     for which in range(3):
-        for step in range(1, pieces):
-            part_out(step, which).start()
+        for turn in range(pieces):
+            pl.when(part_away(turn))(lambda turn=turn: part_out(turn, which).start())
+
+    @pl.when(own_part)
+    def _():
+        for which in range(3):
+            landed[which][place] = parts[piece_index, pl.ds(*segments[which])]
+
     held[0:8] = jnp.zeros((8, piece), f32)
     held[8 + total_rows : 16 + total_rows] = jnp.zeros((8, piece), f32)
     held[16 + total_rows :] = gathered(0)
     for came, present, at in (
-        (0, has_left & (place == 0), 0), (1, has_right & (place == pieces - 1), 8)
+        (0, (piece_side > 0) & (piece_index == 0), 0),
+        (1, (piece_side < sides - 1) & (piece_index == pieces - 1), 8),
     ):
         @pl.when(present)
         def _(came=came, at=at):
             running = held[16 + total_rows + at : 24 + total_rows + at]
             for source in range(pieces):
-                cross_in(came, source).wait_recv()
+                here = (place == source) & (side == piece_side + (1 if came else -1))
+                pl.when(jnp.logical_not(here))(
+                    lambda source=source: cross_in(came, source).wait_recv()
+                )
                 running = running + cross_slots[came, source]
             held[16 + total_rows + at : 24 + total_rows + at] = running
 
@@ -1209,17 +1225,17 @@
         target = line_target(turn)
         return remote(
             lines.at[target], line_slots.at[band], line_send.at[turn], line_recv.at[band],
-            {"shot": kept // nets, "net": lax.rem(kept, nets), "band": target},
+            {"band": target},
         )
 
     def line_in(source):
         return remote(
             lines.at[source], line_slots.at[source], line_send.at[0], line_recv.at[source],
-            {"shot": kept // nets, "net": lax.rem(kept, nets), "band": source},
+            {"band": source},
         )
 
     def line_away(turn):
-        return swapped | (line_target(turn) != band)
+        return line_target(turn) != band
 
     held[pl.ds(8 + lead, lead_rows)] = gathered(1)
     for turn in range(bands):
@@ -1230,18 +1246,16 @@
         lines[target, rows + 16 :] = held[16 + total_rows :]
         pl.when(line_away(turn))(lambda turn=turn: line_out(turn).start())
 
-    @pl.when(jnp.logical_not(swapped))
-    def _():
-        line_slots[band] = lines[band]
+    line_slots[band] = lines[band]
 
     for index in (2, 3):
         each_field_out(index, lambda copy: copy.wait_send())
         edge(index).wait_send()
-    pl.when(has_right)(lambda: cross_out(1).wait_send())
-    pl.when(has_left)(lambda: cross_out(0).wait_send())
+    pl.when(far_right)(lambda: cross_out(1).wait_send())
+    pl.when(far_left)(lambda: cross_out(0).wait_send())
     for which in range(3):
-        for step in range(1, pieces):
-            part_out(step, which).wait_send()
+        for turn in range(pieces):
+            pl.when(part_away(turn))(lambda turn=turn: part_out(turn, which).wait_send())
 
     pl.when(group > 0)(lambda: cot_right().wait_recv())
     pl.when(group < groups - 1)(lambda: cot_left().wait_recv())
@@ -1281,7 +1295,7 @@
     strips[...] = jnp.zeros(strips.shape, f32)
     final = None
     for source in range(bands):
-        pl.when(swapped | (band != source))(lambda source=source: line_in(source).wait_recv())
+        pl.when(band != source)(lambda source=source: line_in(source).wait_recv())
         final = line_slots[source] if final is None else final + line_slots[source]
     out_image[:, piece : 2 * piece] = final[0 : rows + 16]
     strips[8 : 8 + total_rows, 0:16] = final[rows + 16 :].T
@@ -1301,23 +1315,31 @@
         first_lane = start - inset
         line = pltpu.roll(line, (inset - (piece - 3)) % (3 * piece), 1)[:, :span]
         layers[:, first_lane : first_lane + span] = layers[:, first_lane : first_lane + span] + line
+    share = sums.shape[0] // groups
+
+    def share_of(index):
+        return pl.ds(pl.multiple_of(index * share, 8), share)
+
+    def sum_out(step):
+        peer = lax.rem(group + step, groups)
+        return remote(
+            sums.at[share_of(peer)], sum_slots.at[groups - step], sum_send.at[step],
+            sum_recv.at[groups - step], member(peer),
+        )
+
+    early_count = 3 * conv_mid.shape[0] // share
+
+    def early():
+        for step in range(1, groups):
+            pl.when(lax.rem(group + step, groups) < early_count)(
+                lambda step=step: sum_out(step).start()
+            )
+
     paint = network_stage(
         reach_cols, layers, first_weights, middle_weights, back_weights, last_weights, new_velocity,
         sums, patch, near_taps, far_taps, shifted_taps, taps, slope_one,
-        hidden, slope_two, last_taps, update, back,
-    )
-    share = sums.shape[0] // groups
-
-    def share_of(index):
-        return pl.ds(pl.multiple_of(index * share, 8), share)
-
-    def sum_out(step):
-        peer = lax.rem(group + step, groups)
-        return remote(
-            sums.at[share_of(peer)], sum_slots.at[groups - step], sum_send.at[step],
-            sum_recv.at[groups - step], member(peer),
-        )
-
+        hidden, slope_two, last_taps, update, back, early,
+    )
     def sum_in(step):
         peer = lax.rem(group + step, groups)
         return remote(
@@ -1351,7 +1373,9 @@
         )
 
     for step in range(1, groups):
-        sum_out(step).start()
+        pl.when(lax.rem(group + step, groups) >= early_count)(
+            lambda step=step: sum_out(step).start()
+        )
     sum_slots[0] = sums[share_of(group)]
     paint()
     deliver_velocity = pltpu.make_async_copy(new_velocity, velocity_far, output_sem.at[0])

time: 67 us -> 66.4 us (level)
  no operation moved by 1% of the time
where the time goes in v9:
time: 66.4 us; the launch traced here: 66.1 us
  Pallas kernels  65.5 us (99%)
    pallas_call x1, Pallas kernels, whole_iteration(): pl.pallas_call(functools.partial(whole_kernel, (shots, nets, bands)), nam...  63.8 us
    pallas_call x1, Pallas kernels, deliver(): pl.pallas_call(deliver_kernel, name='deliver', out_shape=[jax.ShapeDtypeS...  1.65 us

profile of v9, /device:TPU:0, one launch (start us, length us, event | category | flops | bytes accessed | tf_op | source)
XLA Modules:
  0.0 66.1 jit_solution(2262594202230087589)
XLA Ops:
  0.6 63.8 %whole.1 = (f32[32,128]{1,0:T(8,128)}, f32[128,128]{1,0:T(8,128)}) custom-call(f32[32,1024]{1,0:T(8,128)} %velocity.1, f32[2,32,1024]{2,1,0:T(8,128)} %wave_now.1, f32[2,32,1024]{2,1,0:T(8,128)} %wave_before.1, f32[2,32,1024]{2,1,0:T(8,128)} %adjoint_last.1, f32[2,32,1024]{2,1,0:T(8,128)} %adjoint_after.1, f32[2,16]{1,0:T(2,128)} %wavelet.1, s32[2]{0:T(128)} %source_col.1, ...), custom_call_target="tpu_custom_call" | custom-call | tf_op jit(solution)/shard_map/whole/pallas_call | solution.py:1438
  64.5 1.7 %deliver.1 = (f32[32,128]{1,0:T(8,128)}, f32[18,32]{1,0:T(8,128)}, f32[32,288]{1,0:T(8,128)}, f32[1,288]{1,0:T(1,128)}) custom-call(f32[32,128]{1,0:T(8,128)} %get-tuple-element.10.fresh, f32[128,128]{1,0:T(8,128)} %get-tuple-element.11.totals), custom_call_target="tpu_custom_call" | custom-call | tf_op jit(solution)/shard_map/deliver/pallas_call | solution.py:1547
